TPU v7x, 256 devices: a whole 4x4x8 slice. The times are simulated.
256 devices in a mesh: head: 8 (over y, x_hi), blk: 32 (over x_lo, z, core).
Axes of the slice: x: 4 (x_hi: 2, x_lo: 2; x = x_hi * 2 + x_lo), y: 4, z: 8, core: 2. Of those that a mesh axis runs over, the one named last changes fastest.
Arguments:
- queries: bfloat16 [32768, 2048], P(('blk', 'head')), may hold values from -10.5 to 10.5
- keys: bfloat16 [32768, 2048], P(('blk', 'head')), may hold values from -10.5 to 10.5
- values: bfloat16 [32768, 2048], P(('blk', 'head')), may hold values from -6 to 6
- d_out: bfloat16 [32768, 2048], P(('blk', 'head')), may hold values from -6 to 6
- saved_out: bfloat16 [32768, 2048], P(('blk', 'head')), may hold values from -3 to 3
- mask: int32 [256, 256], P('blk'), may hold values from 0 to 1, as said below
Outputs:
- d_queries: bfloat16 [32768, 2048], P(('blk', 'head'))
- d_keys: bfloat16 [32768, 2048], P(('blk', 'head'))
- d_values: bfloat16 [32768, 2048], P(('blk', 'head'))
Inputs may be any that keep to these rules, and one draw needn't show every extreme that they name: mask[i, i] = 1. Tile i has grid position (i // 128, (i // 8) % 16, i % 8) in a grid of 2 x 16 x 8 tiles; mask[i, j] = 1 only where the positions of i and j differ by at most one along each of the three grid axes.
All inputs are finite; a program needn't handle non-finite values.
Results may differ from a plain program's by a relative error of at most 0.01.
Values may be sent and summed in bfloat16 or wider, within the bound.
No kernel may reach another device: no remote copies, remote signals or barrier semaphores. Data moves between devices by JAX's collectives and lax.ppermute only.
A program may use at most 192 MiB of HBM per device.

v0:
```python
import functools

import jax
import jax.numpy as jnp
from jax import lax
from jax.experimental import pallas as pl
from jax.experimental.pallas import tpu as pltpu
from jax.sharding import Mesh, PartitionSpec as P

HEADS = 16
DIM = 128
TILE = 128
COLS = 8
ROWS = 16
FRAMES = 2
GROUP = FRAMES * COLS
PAIRS = GROUP // 2
EXTRA = 16
BIG = 1e30
SCALE = DIM**-0.5
LOG2E = 1.4426950408889634
C = SCALE * LOG2E

F32 = jnp.float32
BF16 = jnp.bfloat16
VMEM_LIMIT = 58 * 1024 * 1024


def params(**kw):
    return pltpu.CompilerParams(vmem_limit_bytes=VMEM_LIMIT, **kw)


def pack_two_kernel(a_ref, b_ref, out_ref):
    for h in range(out_ref.shape[0]):
        out_ref[h, :TILE, :] = a_ref[:, h * DIM : (h + 1) * DIM]
        out_ref[h, TILE : 2 * TILE, :] = b_ref[:, h * DIM : (h + 1) * DIM]


def pack_two(a, b):
    step = 4
    block = pl.BlockSpec((TILE, step * DIM), lambda i: (0, i))
    return pl.pallas_call(
        pack_two_kernel,
        grid=(HEADS // step,),
        in_specs=[block, block],
        out_specs=pl.BlockSpec((step, 2 * TILE, DIM), lambda i: (i, 0, 0)),
        out_shape=jax.ShapeDtypeStruct((HEADS, 2 * TILE, DIM), BF16),
        compiler_params=params(),
        cost_estimate=pl.CostEstimate(flops=0, bytes_accessed=2**21, transcendentals=0),
        name="pack_keys_values",
    )(a, b)


def pack_queries_kernel(w_ref, q_ref, g_ref, o_ref, m_ref, out_ref):
    mine = m_ref[pl.ds(w_ref[0], 1), :].astype(F32)
    rows = lax.broadcasted_iota(jnp.int32, (EXTRA, TILE), 0)
    for h in range(out_ref.shape[0]):
        cols = slice(h * DIM, (h + 1) * DIM)
        q = q_ref[:, cols]
        g = g_ref[:, cols]
        out_ref[h, :TILE, :] = q
        out_ref[h, TILE : 2 * TILE, :] = g
        prod = g.astype(F32) * o_ref[:, cols].astype(F32)
        delta = jnp.sum(prod.T, axis=0, keepdims=True)
        high = delta.astype(BF16).astype(F32)
        low = delta - high
        extra = jnp.where(rows == 0, high, 0.0)
        extra = jnp.where(rows == 1, low, extra)
        extra = jnp.where(rows == 2, mine[:, :TILE], extra)
        extra = jnp.where(rows == 3, mine[:, TILE:], extra)
        out_ref[h, 2 * TILE :, :] = extra.astype(BF16)


def pack_queries(w, q, g, o, mask):
    step = 4
    block = pl.BlockSpec((TILE, step * DIM), lambda i: (0, i))
    return pl.pallas_call(
        pack_queries_kernel,
        grid=(HEADS // step,),
        in_specs=[
            pl.BlockSpec(memory_space=pltpu.SMEM),
            block,
            block,
            block,
            pl.BlockSpec((COLS, 2 * TILE), lambda i: (0, 0)),
        ],
        out_specs=pl.BlockSpec((step, 2 * TILE + EXTRA, DIM), lambda i: (i, 0, 0)),
        out_shape=jax.ShapeDtypeStruct((HEADS, 2 * TILE + EXTRA, DIM), BF16),
        compiler_params=params(),
        cost_estimate=pl.CostEstimate(flops=2**20, bytes_accessed=5 * 2**19, transcendentals=0),
        name="pack_queries",
    )(w, q, g, o, mask)


def unpack_kernel(in_ref, a_ref, b_ref):
    for h in range(in_ref.shape[0]):
        a_ref[:, h * DIM : (h + 1) * DIM] = in_ref[h, :TILE, :]
        b_ref[:, h * DIM : (h + 1) * DIM] = in_ref[h, TILE:, :]


def unpack_two(x):
    step = 4
    block = pl.BlockSpec((TILE, step * DIM), lambda i: (0, i))
    out = jax.ShapeDtypeStruct((TILE, HEADS * DIM), BF16)
    return pl.pallas_call(
        unpack_kernel,
        grid=(HEADS // step,),
        in_specs=[pl.BlockSpec((step, 2 * TILE, DIM), lambda i: (i, 0, 0))],
        out_specs=[block, block],
        out_shape=[out, out],
        compiler_params=params(),
        cost_estimate=pl.CostEstimate(flops=0, bytes_accessed=2**21, transcendentals=0),
        name="unpack_grads",
    )(x)


def dot_nt(a, b):
    return lax.dot_general(a, b, (((1,), (1,)), ((), ())), preferred_element_type=F32)


def dot_nn(a, b):
    return lax.dot_general(a, b, (((1,), (0,)), ((), ())), preferred_element_type=F32)


def key_tiles(wp, frame):
    found = []
    for step in (-1, 0, 1, 2):
        col = 2 * wp + step
        inside = (col >= 0) & (col < COLS)
        clamped = jnp.clip(col, 0, COLS - 1)
        found.append((frame * COLS + clamped, clamped, inside))
    return found


def penalty(rows_ref, m_ref, unit, tile, frame, col, inside):
    row = rows_ref[unit]
    live = (m_ref[tile, frame * TILE + row * COLS + col] != 0) & inside & (rows_ref[unit + 3] != 0)
    return jnp.where(live, 0.0, BIG).astype(F32)


def fold(x, op):
    return op(x.reshape(TILE // 8, 8, TILE), axis=0)


def query_side(qd_ref, t0):
    q = qd_ref[pl.ds(t0, 2), :TILE, :].reshape(2 * TILE, DIM)
    g = qd_ref[pl.ds(t0, 2), TILE : 2 * TILE, :].reshape(2 * TILE, DIM)
    delta = []
    for i in range(2):
        extra = qd_ref[t0 + i, 2 * TILE :, :].astype(F32)
        delta.append(extra[0:1, :] + extra[1:2, :])
    return q, g, jnp.concatenate(delta, axis=1)


SPANS = ((0, 1), (0, 2), (0, 2), (1, 2))


def unit_grads(rows_ref, m_ref, unit, kv_ref, kt_ref, dk_ref, dv_ref, scores, q, g, delta, lse, t0, wp, dqt):
    for frame in range(FRAMES):
        for j, (tile, col, inside) in enumerate(key_tiles(wp, frame)):
            lo, hi = SPANS[j]
            cut = slice(lo * TILE, hi * TILE)
            pens = [
                jnp.broadcast_to(penalty(rows_ref, m_ref, unit, t0 + i, frame, col, inside), (1, TILE))
                for i in range(lo, hi)
            ]
            level = lse[:, cut] + (jnp.concatenate(pens, axis=1) if len(pens) > 1 else pens[0])
            key = kv_ref[tile, :TILE, :]
            value = kv_ref[tile, TILE:, :]
            s = scores(frame, j) if scores is not None else dot_nt(key, q[cut])
            prob = jnp.exp2(s * C - level)
            dprob = dot_nt(value, g[cut])
            dscore = (prob * (dprob - delta[:, cut])).astype(BF16)
            prob = prob.astype(BF16)
            dv_ref[tile] += dot_nn(prob, g[cut])
            dk_ref[tile] += dot_nn(dscore, q[cut])
            part = dot_nn(kt_ref[tile], dscore)
            dqt[lo:hi] = [
                d + part[:, i * TILE : (i + 1) * TILE] for i, d in enumerate(dqt[lo:hi])
            ]
    return dqt


def stats_kernel(rows_ref, m_ref, qd_ref, own_ref, z_ref, c_ref, part_ref, lse_ref, dqt_ref, s_ref, kt_ref, dk_ref, dv_ref):
    dk_ref[...] = jnp.zeros_like(dk_ref)
    dv_ref[...] = jnp.zeros_like(dv_ref)

    def turn(t, carry):
        kt_ref[t] = z_ref[t, :TILE, :].T
        return carry

    lax.fori_loop(0, GROUP, turn, 0)

    def pair(p, carry):
        t0 = 2 * p
        wp = lax.rem(p, COLS // 2)
        q, g, delta = query_side(qd_ref, t0)
        top = [jnp.full((8, TILE), -BIG, F32) for _ in range(2)]
        pens = {}
        for unit, kv_ref in enumerate((z_ref, c_ref, own_ref)):
            for frame in range(FRAMES):
                for j, (tile, col, inside) in enumerate(key_tiles(wp, frame)):
                    lo, hi = SPANS[j]
                    s = dot_nt(kv_ref[tile, :TILE, :], q[lo * TILE : hi * TILE])
                    s_ref[unit, frame, j, :, lo * TILE : hi * TILE] = s
                    for i in range(lo, hi):
                        pen = penalty(rows_ref, m_ref, unit, t0 + i, frame, col, inside)
                        pens[unit, frame, j, i] = pen
                        piece = s[:, (i - lo) * TILE : (i - lo + 1) * TILE]
                        top[i] = jnp.maximum(top[i], fold(piece, jnp.max) - pen)
        lses = []
        for i in range(2):
            peak = jnp.max(top[i], axis=0, keepdims=True) * C
            total = jnp.zeros((8, TILE), F32)
            for unit in range(3):
                for frame in range(FRAMES):
                    for j in range(4):
                        if SPANS[j][0] <= i < SPANS[j][1]:
                            piece = s_ref[unit, frame, j, :, i * TILE : (i + 1) * TILE]
                            total += fold(jnp.exp2(piece * C - (peak + pens[unit, frame, j, i])), jnp.sum)
            lse = peak + jnp.log(jnp.sum(total, axis=0, keepdims=True)) * LOG2E
            lse_ref[t0 + i] = jnp.broadcast_to(lse, (8, TILE))
            lses.append(lse)
        lse = jnp.concatenate(lses, axis=1)

        def scores(frame, j):
            lo, hi = SPANS[j]
            return s_ref[0, frame, j, :, lo * TILE : hi * TILE]

        dqt = [jnp.zeros((DIM, TILE), F32) for _ in range(2)]
        dqt = unit_grads(rows_ref, m_ref, 0, z_ref, kt_ref, dk_ref, dv_ref, scores, q, g, delta, lse, t0, wp, dqt)
        dqt_ref[t0] = dqt[0]
        dqt_ref[t0 + 1] = dqt[1]
        return carry

    lax.fori_loop(0, PAIRS, pair, 0)
    part_ref[:, :TILE, :] = (dk_ref[...] * SCALE).astype(BF16)
    part_ref[:, TILE:, :] = dv_ref[...].astype(BF16)


def rest_kernel(
    rows_ref, m_ref, qd_ref, own_ref, c_ref, lse_ref, dqt_ref, part_ref, mine_ref, dq_ref,
    ktc_ref, kto_ref, dkc_ref, dvc_ref, dko_ref, dvo_ref,
):
    for ref in (dkc_ref, dvc_ref, dko_ref, dvo_ref):
        ref[...] = jnp.zeros_like(ref)

    def turn(t, carry):
        ktc_ref[t] = c_ref[t, :TILE, :].T
        kto_ref[t] = own_ref[t, :TILE, :].T
        return carry

    lax.fori_loop(0, GROUP, turn, 0)

    def pair(p, carry):
        t0 = 2 * p
        wp = lax.rem(p, COLS // 2)
        q, g, delta = query_side(qd_ref, t0)
        lse = jnp.concatenate([lse_ref[t0, 0:1, :], lse_ref[t0 + 1, 0:1, :]], axis=1)
        dqt = [dqt_ref[t0], dqt_ref[t0 + 1]]
        common = (None, q, g, delta, lse, t0, wp)
        dqt = unit_grads(rows_ref, m_ref, 1, c_ref, ktc_ref, dkc_ref, dvc_ref, *common, dqt)
        dqt = unit_grads(rows_ref, m_ref, 2, own_ref, kto_ref, dko_ref, dvo_ref, *common, dqt)
        for i in range(2):
            dq_ref[t0 + i] = (dqt[i].T * SCALE).astype(BF16)
        return carry

    lax.fori_loop(0, PAIRS, pair, 0)
    part_ref[:, :TILE, :] = (dkc_ref[...] * SCALE).astype(BF16)
    part_ref[:, TILE:, :] = dvc_ref[...].astype(BF16)
    mine_ref[:, :TILE, :] = dko_ref[...] * SCALE
    mine_ref[:, TILE:, :] = dvo_ref[...]


SMEM = pl.BlockSpec(memory_space=pltpu.SMEM)
VM = pl.BlockSpec(memory_space=pltpu.VMEM)


def acc():
    return pltpu.VMEM((GROUP, TILE, DIM), F32)


def turned():
    return pltpu.VMEM((GROUP, DIM, TILE), BF16)


def stats_and_far(rows, live, qd, own, far, near):
    return pl.pallas_call(
        stats_kernel,
        in_specs=[SMEM, SMEM, VM, VM, VM, VM],
        out_specs=[VM, VM, VM],
        out_shape=[
            jax.ShapeDtypeStruct((GROUP, 2 * TILE, DIM), BF16),
            jax.ShapeDtypeStruct((GROUP, 8, TILE), F32),
            jax.ShapeDtypeStruct((GROUP, DIM, TILE), F32),
        ],
        scratch_shapes=[
            pltpu.VMEM((3, FRAMES, 4, TILE, 2 * TILE), F32),
            turned(),
            acc(),
            acc(),
        ],
        compiler_params=params(),
        cost_estimate=pl.CostEstimate(flops=3 * 10**9, bytes_accessed=2**23, transcendentals=6 * 10**6),
        name="stats_and_far_row",
    )(rows, live, qd, own, far, near)


def rest(rows, live, qd, own, near, lse, dqt):
    return pl.pallas_call(
        rest_kernel,
        in_specs=[SMEM, SMEM, VM, VM, VM, VM, VM],
        out_specs=[VM, VM, VM],
        out_shape=[
            jax.ShapeDtypeStruct((GROUP, 2 * TILE, DIM), BF16),
            jax.ShapeDtypeStruct((GROUP, 2 * TILE, DIM), F32),
            jax.ShapeDtypeStruct((GROUP, TILE, DIM), BF16),
        ],
        scratch_shapes=[turned(), turned(), acc(), acc(), acc(), acc()],
        compiler_params=params(),
        cost_estimate=pl.CostEstimate(flops=4 * 10**9, bytes_accessed=2**23, transcendentals=3 * 10**6),
        name="near_and_own_rows",
    )(rows, live, qd, own, near, lse, dqt)


def per_device(queries, keys, values, d_out, saved_out, mask):
    group = ("frame", "head")
    row = lax.axis_index("row")
    even = lax.rem(row, 2) == 0
    chip_swap = [(i, i ^ 1) for i in range(ROWS)]
    link_swap = [(i, i + 1) for i in range(1, ROWS - 1, 2)] + [(i + 1, i) for i in range(1, ROWS - 1, 2)]

    def exchange(x):
        return lax.all_to_all(x, group, split_axis=0, concat_axis=0, tiled=True)

    own = exchange(pack_two(keys, values))
    w = lax.axis_index("head").astype(jnp.int32).reshape(1)
    qd = exchange(pack_queries(w, queries, d_out, saved_out, mask))
    far = lax.ppermute(own, "row", link_swap)
    near = lax.ppermute(own, "row", chip_swap)

    far_row = jnp.where(even, row - 1, row + 1)
    near_row = jnp.where(even, row + 1, row - 1)
    rows = jnp.stack([far_row, near_row, row]).astype(jnp.int32)
    inside = ((rows >= 0) & (rows < ROWS)).astype(jnp.int32)
    rows = jnp.concatenate([jnp.clip(rows, 0, ROWS - 1), inside])
    live = qd[:, 2 * TILE + 2 : 2 * TILE + 4, :].astype(jnp.int32).reshape(GROUP, 2 * TILE)

    far_part, lse, dqt = stats_and_far(rows, live, qd, own, far, near)
    far_back = lax.ppermute(far_part, "row", link_swap)
    near_part, mine, dq = rest(rows, live, qd, own, near, lse, dqt)
    near_back = lax.ppermute(near_part, "row", chip_swap)
    dq = exchange(dq)
    total = mine + near_back.astype(F32) + far_back.astype(F32)
    both = exchange(total.astype(BF16))
    d_keys, d_values = unpack_two(both)
    d_queries = dq.transpose(1, 0, 2).reshape(TILE, HEADS * DIM)
    return d_queries, d_keys, d_values


def solution(mesh):
    devices = mesh.devices
    if mesh.axis_names != ("head", "blk"):
        raise ValueError("mesh axes")
    heads = devices.shape[0]
    grid = Mesh(devices.reshape(heads, FRAMES, devices.shape[1] // FRAMES), ("head", "frame", "row"))
    tokens = P(("frame", "row", "head"), None)
    return jax.shard_map(
        per_device,
        mesh=grid,
        in_specs=(tokens,) * 5 + (P(("frame", "row"), None),),
        out_specs=(tokens,) * 3,
        check_vma=False,
    )
```

profile of v0, /device:TPU:97, one launch (start us, length us, event | category | flops | bytes accessed | tf_op | source)
XLA Modules:
  0.0 155.2 jit_solution(13284646364332694367)
XLA Ops:
  0.6 3.5 %pack_keys_values.1 = bf16[16,256,128]{2,1,0:T(8,128)(2,1)} custom-call(bf16[128,2048]{1,0:T(8,128)(2,1)} %a_ref.1, bf16[128,2048]{1,0:T(8,128)(2,1)} %b_ref.1), custom_call_target="tpu_custom_call" | custom-call | bytes 2097152 | tf_op jit(solution)/shard_map/pack_keys_values/pallas_call | solution.py:42
  4.1 6.8 %all-to-all-start.1 = ((bf16[16,256,128]{2,1,0:T(8,128)(2,1)}), bf16[16,256,128]{2,1,0:T(8,128)(2,1)S(1)}, u32[]{:S(2)}, u32[]{:S(2)}) async-start(bf16[16,256,128]{2,1,0:T(8,128)(2,1)} %pack_keys_values.1), calls=%async_computation.1 | async-start | bytes 2097152 | tf_op jit(solution)/shard_map/all_to_all | solution.py:334
  10.9 3.8 %pack_queries.1 = bf16[16,272,128]{2,1,0:T(8,128)(2,1)} custom-call(s32[1]{0:T(128)} %bitcast.3.w_ref, bf16[128,2048]{1,0:T(8,128)(2,1)} %q_ref.1, bf16[128,2048]{1,0:T(8,128)(2,1)} %g_ref.1, bf16[128,2048]{1,0:T(8,128)(2,1)} %o_ref.1, s32[8,256]{1,0:T(8,128)} %m_ref.1), custom_call_target="tpu_custom_call" | custom-call | flops 1048576 | bytes 2621440 | tf_op jit(solution)/shard_map/pack_queries/pallas_call | solution.py:77
  14.7 10.9 %all-to-all-done.1.own_ref = bf16[16,256,128]{2,1,0:T(8,128)(2,1)S(1)} async-done(((bf16[16,256,128]{2,1,0:T(8,128)(2,1)}), bf16[16,256,128]{2,1,0:T(8,128)(2,1)S(1)}, u32[]{:S(2)}, u32[]{:S(2)}) %all-to-all-start.1) | async-done | bytes 1048608 | tf_op jit(solution)/shard_map/all_to_all | solution.py:334
  25.5 0.0 copy-start.2
  25.5 5.6 %all-to-all-start = ((bf16[16,272,128]{2,1,0:T(8,128)(2,1)}), bf16[16,272,128]{2,1,0:T(8,128)(2,1)S(1)}, u32[]{:S(2)}, u32[]{:S(2)}) async-start(bf16[16,272,128]{2,1,0:T(8,128)(2,1)} %pack_queries.1), calls=%async_computation | async-start | bytes 2228224 | tf_op jit(solution)/shard_map/all_to_all | solution.py:334
  31.2 6.5 %collective-permute-start.1 = (bf16[16,256,128]{2,1,0:T(8,128)(2,1)S(1)}, bf16[16,256,128]{2,1,0:T(8,128)(2,1)}, u32[]{:S(2)}, u32[]{:S(2)}) collective-permute-start(bf16[16,256,128]{2,1,0:T(8,128)(2,1)S(1)} %all-to-all-done.1.own_ref), channel_id=1, source_target_pairs={{1,2},{3,4},{5,6},{7,8},{9,10},{11,12},{13,14},{2,1},{4,3},{6,5},{... | collective-permute-start | bytes 3145736 | tf_op jit(solution)/shard_map/ppermute | solution.py:339
  37.7 0.1 collective-permute-start
  37.8 0.1 broadcast_clamp_fusion
  37.9 0.6 pad_add_fusion.1.rows_ref
  38.5 7.3 %all-to-all-done.qd_ref = bf16[16,272,128]{2,1,0:T(8,128)(2,1)S(1)} async-done(((bf16[16,272,128]{2,1,0:T(8,128)(2,1)}), bf16[16,272,128]{2,1,0:T(8,128)(2,1)S(1)}, u32[]{:S(2)}, u32[]{:S(2)}) %all-to-all-start) | async-done | bytes 1114144 | tf_op jit(solution)/shard_map/all_to_all | solution.py:334
  45.7 0.0 copy-start.1
  45.8 0.7 copy.13
  46.4 3.8 %collective-permute-done.1.z_ref = bf16[16,256,128]{2,1,0:T(8,128)(2,1)} collective-permute-done((bf16[16,256,128]{2,1,0:T(8,128)(2,1)S(1)}, bf16[16,256,128]{2,1,0:T(8,128)(2,1)}, u32[]{:S(2)}, u32[]{:S(2)}) %collective-permute-start.1) | collective-permute-done | bytes 1048608 | tf_op jit(solution)/shard_map/ppermute | solution.py:339
  50.2 0.0 collective-permute-done.c_ref
  50.3 0.0 copy-start.3
  50.3 0.0 copy-done.2
  50.3 0.0 copy-done.1
  50.3 1.0 copy-done.3
  51.2 22.1 %stats_and_far_row.1 = (bf16[16,256,128]{2,1,0:T(8,128)(2,1)}, f32[16,8,128]{2,1,0:T(8,128)}, f32[16,128,128]{2,1,0:T(8,128)}) custom-call(s32[6]{0:T(128)} %pad_add_fusion.1.rows_ref, s32[16,256]{1,0:T(8,128)} %bitcast.13, bf16[16,272,128]{2,1,0:T(8,128)(2,1)} %copy-done.1, bf16[16,256,128]{2,1,0:T(8,128)(2,1)} %copy-done.2, ...), custom_call_target="tpu_custom_call" | custom-call | flops 3000000000 | bytes 8388608 | tf_op jit(solution)/shard_map/stats_and_far_row/pallas_call | solution.py:288
  73.4 31.3 %near_and_own_rows.1 = (bf16[16,256,128]{2,1,0:T(8,128)(2,1)}, f32[16,256,128]{2,1,0:T(8,128)}, bf16[16,128,128]{2,1,0:T(8,128)(2,1)}) custom-call(s32[6]{0:T(128)} %pad_add_fusion.1.rows_ref, s32[16,256]{1,0:T(8,128)} %bitcast.14, bf16[16,272,128]{2,1,0:T(8,128)(2,1)} %copy-done.1, bf16[16,256,128]{2,1,0:T(8,128)(2,1)} %copy-done.2, ...), custom_call_target="tpu_custom_call" | custom-call | flops 4000000000 | bytes 8388608 | tf_op jit(solution)/shard_map/near_and_own_rows/pallas_call | solution.py:310
  104.7 0.0 collective-permute-start.2
  104.7 4.8 %collective-permute-start.3 = (bf16[16,256,128]{2,1,0:T(8,128)(2,1)}, bf16[16,256,128]{2,1,0:T(8,128)(2,1)S(1)}, u32[]{:S(2)}, u32[]{:S(2)}) collective-permute-start(bf16[16,256,128]{2,1,0:T(8,128)(2,1)} %get-tuple-element.16), channel_id=1, source_target_pairs={{1,2},{3,4},{5,6},{7,8},{9,10},{11,12},{13,14},{2,1},{4,3},{6,5},{... | collective-permute-start | bytes 3145736 | tf_op jit(solution)/shard_map/ppermute | solution.py:350
  109.5 7.0 %all-to-all-start.2 = ((bf16[16,128,128]{2,1,0:T(8,128)(2,1)}), bf16[16,128,128]{2,1,0:T(8,128)(2,1)S(1)}, u32[]{:S(2)}, u32[]{:S(2)}) async-start(bf16[16,128,128]{2,1,0:T(8,128)(2,1)} %get-tuple-element.13), calls=%async_computation.2 | async-start | bytes 1048576 | tf_op jit(solution)/shard_map/all_to_all | solution.py:334
  116.5 0.0 collective-permute-done.2
  116.5 6.0 %collective-permute-done.3 = bf16[16,256,128]{2,1,0:T(8,128)(2,1)S(1)} collective-permute-done((bf16[16,256,128]{2,1,0:T(8,128)(2,1)}, bf16[16,256,128]{2,1,0:T(8,128)(2,1)S(1)}, u32[]{:S(2)}, u32[]{:S(2)}) %collective-permute-start.3) | collective-permute-done | bytes 1048608 | tf_op jit(solution)/shard_map/ppermute | solution.py:350
  122.5 2.9 %add_convert_fusion = bf16[16,256,128]{2,1,0:T(8,128)(2,1)} fusion(bf16[16,256,128]{2,1,0:T(8,128)(2,1)S(1)} %collective-permute-done.3, f32[16,256,128]{2,1,0:T(8,128)} %get-tuple-element.14, bf16[16,256,128]{2,1,0:T(8,128)(2,1)S(1)} %collective-permute-done.2), kind=kLoop, calls=%fused_computation | loop fusion | flops 2621440 | bytes 5242880 | tf_op jit(solution)/shard_map/convert_element_type | solution.py:355
  125.4 0.7 all-to-all-done.2
  126.1 6.0 %all-to-all-start.3 = ((bf16[16,256,128]{2,1,0:T(8,128)(2,1)}), bf16[16,256,128]{2,1,0:T(8,128)(2,1)S(1)}, u32[]{:S(2)}, u32[]{:S(2)}) async-start(bf16[16,256,128]{2,1,0:T(8,128)(2,1)} %add_convert_fusion), calls=%async_computation.3 | async-start | bytes 2097152 | tf_op jit(solution)/shard_map/all_to_all | solution.py:334
  132.1 0.3 copy.9
  132.4 1.0 copy.10
  133.4 17.4 %all-to-all-done.3.in_ref = bf16[16,256,128]{2,1,0:T(8,128)(2,1)S(1)} async-done(((bf16[16,256,128]{2,1,0:T(8,128)(2,1)}), bf16[16,256,128]{2,1,0:T(8,128)(2,1)S(1)}, u32[]{:S(2)}, u32[]{:S(2)}) %all-to-all-start.3) | async-done | bytes 1048608 | tf_op jit(solution)/shard_map/all_to_all | solution.py:334
  150.8 0.0 copy-start
  150.8 1.0 copy-done
  151.8 3.4 %unpack_grads.1 = (bf16[128,2048]{1,0:T(8,128)(2,1)}, bf16[128,2048]{1,0:T(8,128)(2,1)}) custom-call(bf16[16,256,128]{2,1,0:T(8,128)(2,1)} %copy-done), custom_call_target="tpu_custom_call" | custom-call | bytes 2097152 | tf_op jit(solution)/shard_map/unpack_grads/pallas_call | solution.py:105
  (2 shorter events, 0.0 us)
Async XLA Ops:
  4.1 21.5 %all-to-all-start.1 = ((bf16[16,256,128]{2,1,0:T(8,128)(2,1)}), bf16[16,256,128]{2,1,0:T(8,128)(2,1)S(1)}, u32[]{:S(2)}, u32[]{:S(2)}) async-start(bf16[16,256,128]{2,1,0:T(8,128)(2,1)} %pack_keys_values.1), calls=%async_computation.1 | async-start | bytes 2097152 | tf_op jit(solution)/shard_map/all_to_all | solution.py:334
  25.5 24.7 %copy-start.2 = (bf16[16,256,128]{2,1,0:T(8,128)(2,1)}, bf16[16,256,128]{2,1,0:T(8,128)(2,1)S(1)}, u32[]{:S(2)}) copy-start(bf16[16,256,128]{2,1,0:T(8,128)(2,1)S(1)} %all-to-all-done.1.own_ref) | copy-start | bytes 3145732
  25.5 20.2 %all-to-all-start = ((bf16[16,272,128]{2,1,0:T(8,128)(2,1)}), bf16[16,272,128]{2,1,0:T(8,128)(2,1)S(1)}, u32[]{:S(2)}, u32[]{:S(2)}) async-start(bf16[16,272,128]{2,1,0:T(8,128)(2,1)} %pack_queries.1), calls=%async_computation | async-start | bytes 2228224 | tf_op jit(solution)/shard_map/all_to_all | solution.py:334
  31.2 19.1 %collective-permute-start.1 = (bf16[16,256,128]{2,1,0:T(8,128)(2,1)S(1)}, bf16[16,256,128]{2,1,0:T(8,128)(2,1)}, u32[]{:S(2)}, u32[]{:S(2)}) collective-permute-start(bf16[16,256,128]{2,1,0:T(8,128)(2,1)S(1)} %all-to-all-done.1.own_ref), channel_id=1, source_target_pairs={{1,2},{3,4},{5,6},{7,8},{9,10},{11,12},{13,14},{2,1},{4,3},{6,5},{... | collective-permute-start | bytes 3145736 | tf_op jit(solution)/shard_map/ppermute | solution.py:339
  37.7 12.6 %collective-permute-start = (bf16[16,256,128]{2,1,0:T(8,128)(2,1)S(1)}, bf16[16,256,128]{2,1,0:T(8,128)(2,1)S(1)}, u32[]{:S(2)}, u32[]{:S(2)}) collective-permute-start(bf16[16,256,128]{2,1,0:T(8,128)(2,1)S(1)} %all-to-all-done.1.own_ref), channel_id=1, source_target_pairs={{0,1},{1,0},{2,3},{3,2},{4,5},{5,4},{6,7},{7,6},{8,9},{9,8},{10,11... | collective-permute-start | bytes 3145736 | tf_op jit(solution)/shard_map/ppermute | solution.py:340
  45.7 4.5 %copy-start.1 = (bf16[16,272,128]{2,1,0:T(8,128)(2,1)}, bf16[16,272,128]{2,1,0:T(8,128)(2,1)S(1)}, u32[]{:S(2)}) copy-start(bf16[16,272,128]{2,1,0:T(8,128)(2,1)S(1)} %all-to-all-done.qd_ref) | copy-start | bytes 3342340
  50.3 1.0 copy-start.3
  104.7 11.8 %collective-permute-start.2 = (bf16[16,256,128]{2,1,0:T(8,128)(2,1)}, bf16[16,256,128]{2,1,0:T(8,128)(2,1)S(1)}, u32[]{:S(2)}, u32[]{:S(2)}) collective-permute-start(bf16[16,256,128]{2,1,0:T(8,128)(2,1)} %get-tuple-element.15), channel_id=1, source_target_pairs={{0,1},{1,0},{2,3},{3,2},{4,5},{5,4},{6,7},{7,6},{8,9},{9,8},{10,11... | collective-permute-start | bytes 3145736 | tf_op jit(solution)/shard_map/ppermute | solution.py:352
  104.7 17.8 %collective-permute-start.3 = (bf16[16,256,128]{2,1,0:T(8,128)(2,1)}, bf16[16,256,128]{2,1,0:T(8,128)(2,1)S(1)}, u32[]{:S(2)}, u32[]{:S(2)}) collective-permute-start(bf16[16,256,128]{2,1,0:T(8,128)(2,1)} %get-tuple-element.16), channel_id=1, source_target_pairs={{1,2},{3,4},{5,6},{7,8},{9,10},{11,12},{13,14},{2,1},{4,3},{6,5},{... | collective-permute-start | bytes 3145736 | tf_op jit(solution)/shard_map/ppermute | solution.py:350
  109.5 16.6 %all-to-all-start.2 = ((bf16[16,128,128]{2,1,0:T(8,128)(2,1)}), bf16[16,128,128]{2,1,0:T(8,128)(2,1)S(1)}, u32[]{:S(2)}, u32[]{:S(2)}) async-start(bf16[16,128,128]{2,1,0:T(8,128)(2,1)} %get-tuple-element.13), calls=%async_computation.2 | async-start | bytes 1048576 | tf_op jit(solution)/shard_map/all_to_all | solution.py:334
  126.1 24.7 %all-to-all-start.3 = ((bf16[16,256,128]{2,1,0:T(8,128)(2,1)}), bf16[16,256,128]{2,1,0:T(8,128)(2,1)S(1)}, u32[]{:S(2)}, u32[]{:S(2)}) async-start(bf16[16,256,128]{2,1,0:T(8,128)(2,1)} %add_convert_fusion), calls=%async_computation.3 | async-start | bytes 2097152 | tf_op jit(solution)/shard_map/all_to_all | solution.py:334
  150.8 1.0 copy-start
where the time goes:
time: 156 us; the launch traced here: 155 us
  Pallas kernels  64.1 us (41%)
  waiting for transfers between devices  46.1 us (30%)
  starting transfers between devices  36.7 us (24%)
  local copies, waits for them, and re-layouts  3.92 us (3%)
  other arithmetic  3.64 us (2%)
    all_to_all x4, waiting for transfers between devices, exchange(): return lax.all_to_all(x, group, split_axis=0, concat_axis=0, tiled=True)  36.3 us
    pallas_call x1, Pallas kernels, rest(): pl.pallas_call(rest_kernel, in_specs=[SMEM, SMEM, VM, VM, VM, VM, VM], ou...  31.3 us
    all_to_all x4, starting transfers between devices, exchange(): return lax.all_to_all(x, group, split_axis=0, concat_axis=0, tiled=True)  25.3 us
    pallas_call x1, Pallas kernels, stats_and_far(): pl.pallas_call(stats_kernel, in_specs=[SMEM, SMEM, VM, VM, VM, VM], out_s...  22.1 us
    ppermute x1, starting transfers between devices, per_device(): far = lax.ppermute(own, 'row', link_swap)  6.52 us
    ppermute x1, waiting for transfers between devices, per_device(): far_back = lax.ppermute(far_part, 'row', link_swap)  6 us
    ppermute x1, starting transfers between devices, per_device(): far_back = lax.ppermute(far_part, 'row', link_swap)  4.84 us
    pallas_call x1, Pallas kernels, pack_queries(): pl.pallas_call(pack_queries_kernel, grid=(HEADS // step,), in_specs=[pl.B...  3.83 us
  transfers between devices with their start and end apart: 8, of which 6 were waited for; matrix products, arithmetic and copies ran while one was open for 4% of the time, Pallas kernels for 2%

commit v1 on v0

v1 whole, which is shorter than its diff:
```python
import functools

import jax
import jax.numpy as jnp
from jax import lax
from jax.experimental import pallas as pl
from jax.experimental.pallas import tpu as pltpu
from jax.sharding import Mesh, PartitionSpec as P

HEADS = 16
DIM = 128
TILE = 128
COLS = 8
ROWS = 16
FRAMES = 2
GROUP = FRAMES * COLS
EXTRA = 16
FIRST = 3 * TILE + EXTRA
SECOND = TILE + EXTRA
BIG = 1e30
SCALE = DIM**-0.5
C = SCALE * 1.4426950408889634

F32 = jnp.float32
BF16 = jnp.bfloat16
VMEM_LIMIT = 20 * 1024 * 1024


def params(**kw):
    return pltpu.CompilerParams(vmem_limit_bytes=VMEM_LIMIT, **kw)


def small():
    return pltpu.CompilerParams(vmem_limit_bytes=8 * 1024 * 1024)


SMEM = pl.BlockSpec(memory_space=pltpu.SMEM)
VM = pl.BlockSpec(memory_space=pltpu.VMEM)
ANY = pl.BlockSpec(memory_space=pl.ANY)


CHUNKS = 4


def pack_first_kernel(w_ref, k_ref, v_ref, q_ref, m_ref, out_ref, buf_ref, mine_ref, in_sem, out_sem, mine_sem):
    wide = HEADS // CHUNKS * DIM
    refs = (k_ref, v_ref, q_ref)

    def fetch(part, i):
        cols = pl.ds(i * wide, wide)
        return pltpu.make_async_copy(refs[part].at[:, cols], buf_ref.at[part, :, cols], in_sem.at[part, i])

    def send(part, h):
        return pltpu.make_async_copy(
            buf_ref.at[part, :, pl.ds(h * DIM, DIM)], out_ref.at[h, pl.ds(part * TILE, TILE), :], out_sem.at[part, h]
        )

    def send_mask(h):
        return pltpu.make_async_copy(mine_ref, out_ref.at[h, pl.ds(3 * TILE, EXTRA), :], mine_sem.at[h])

    for i in range(CHUNKS):
        for part in range(3):
            fetch(part, i).start()
    mine = m_ref[pl.ds(w_ref[0], 1), :].astype(F32)
    rows = lax.broadcasted_iota(jnp.int32, (EXTRA, TILE), 0)
    extra = jnp.where(rows == 0, mine[:, :TILE], 0.0)
    mine_ref[...] = jnp.where(rows == 1, mine[:, TILE:], extra).astype(BF16)
    for i in range(CHUNKS):
        for part in range(3):
            fetch(part, i).wait()
            for h in range(i * HEADS // CHUNKS, (i + 1) * HEADS // CHUNKS):
                send(part, h).start()
    for h in range(HEADS):
        send_mask(h).start()
    for h in range(HEADS):
        for part in range(3):
            send(part, h).wait()
        send_mask(h).wait()


def pack_first(w, keys, values, queries, mask):
    return pl.pallas_call(
        pack_first_kernel,
        in_specs=[SMEM, ANY, ANY, ANY, VM],
        out_specs=ANY,
        out_shape=jax.ShapeDtypeStruct((HEADS, FIRST, DIM), BF16),
        scratch_shapes=[
            pltpu.VMEM((3, TILE, HEADS * DIM), BF16),
            pltpu.VMEM((EXTRA, TILE), BF16),
            pltpu.SemaphoreType.DMA((3, CHUNKS)),
            pltpu.SemaphoreType.DMA((3, HEADS)),
            pltpu.SemaphoreType.DMA((HEADS,)),
        ],
        compiler_params=pltpu.CompilerParams(vmem_limit_bytes=58 * 1024 * 1024),
        cost_estimate=pl.CostEstimate(flops=0, bytes_accessed=3 * 2**20, transcendentals=0),
        name="pack_first",
    )(w, keys, values, queries, mask)


def pack_second_kernel(g_ref, o_ref, out_ref):
    rows = lax.broadcasted_iota(jnp.int32, (EXTRA, TILE), 0)
    for h in range(out_ref.shape[0]):
        cols = slice(h * DIM, (h + 1) * DIM)
        g = g_ref[:, cols]
        out_ref[h, :TILE, :] = g
        prod = g.astype(F32) * o_ref[:, cols].astype(F32)
        delta = jnp.sum(prod.T, axis=0, keepdims=True)
        high = delta.astype(BF16).astype(F32)
        extra = jnp.where(rows == 0, high, 0.0)
        out_ref[h, TILE:, :] = jnp.where(rows == 1, delta - high, extra).astype(BF16)


def pack_second(g, o):
    step = 4
    block = pl.BlockSpec((TILE, step * DIM), lambda i: (0, i))
    return pl.pallas_call(
        pack_second_kernel,
        grid=(HEADS // step,),
        in_specs=[block, block],
        out_specs=pl.BlockSpec((step, SECOND, DIM), lambda i: (i, 0, 0)),
        out_shape=jax.ShapeDtypeStruct((HEADS, SECOND, DIM), BF16),
        compiler_params=small(),
        cost_estimate=pl.CostEstimate(flops=2**20, bytes_accessed=3 * 2**19, transcendentals=0),
        name="pack_second",
    )(g, o)


def unpack_kernel(in_ref, q_ref, k_ref, v_ref, sem):
    refs = (q_ref, k_ref, v_ref)

    def move(part, h):
        return pltpu.make_async_copy(
            in_ref.at[h, pl.ds(part * TILE, TILE), :], refs[part].at[:, pl.ds(h * DIM, DIM)], sem.at[part, h]
        )

    for h in range(HEADS):
        for part in range(3):
            move(part, h).start()
    for h in range(HEADS):
        for part in range(3):
            move(part, h).wait()


def unpack(x):
    out = jax.ShapeDtypeStruct((TILE, HEADS * DIM), BF16)
    return pl.pallas_call(
        unpack_kernel,
        in_specs=[VM],
        out_specs=[ANY] * 3,
        out_shape=[out] * 3,
        scratch_shapes=[pltpu.SemaphoreType.DMA((3, HEADS))],
        compiler_params=small(),
        cost_estimate=pl.CostEstimate(flops=0, bytes_accessed=3 * 2**20, transcendentals=0),
        name="unpack_grads",
    )(x)


def add_kernel(mine_ref, near_ref, far_ref, out_ref):
    out_ref[:, :TILE, :] = mine_ref[:, :TILE, :]
    total = mine_ref[:, TILE:, :].astype(F32) + near_ref[...].astype(F32) + far_ref[...].astype(F32)
    out_ref[:, TILE:, :] = total.astype(BF16)


def add_parts(mine, near, far):
    step = 4
    block = pl.BlockSpec((step, 2 * TILE, DIM), lambda i: (i, 0, 0))
    wide = pl.BlockSpec((step, 3 * TILE, DIM), lambda i: (i, 0, 0))
    return pl.pallas_call(
        add_kernel,
        grid=(GROUP // step,),
        in_specs=[wide, block, block],
        out_specs=wide,
        out_shape=jax.ShapeDtypeStruct((GROUP, 3 * TILE, DIM), BF16),
        compiler_params=small(),
        cost_estimate=pl.CostEstimate(flops=2**20, bytes_accessed=5 * 2**20, transcendentals=0),
        name="add_parts",
    )(mine, near, far)


def dot_nt(a, b):
    return lax.dot_general(a, b, (((1,), (1,)), ((), ())), preferred_element_type=F32)


def dot_nn(a, b):
    return lax.dot_general(a, b, (((1,), (0,)), ((), ())), preferred_element_type=F32)


def sweep(body):
    edge = COLS - 1
    body(0, ((1, 0, True, False), (2, 1, True, False)))

    def inner(w, carry):
        body(w, ((0, w - 1, False, True), (1, w, False, False), (2, w + 1, True, False)))
        return carry

    lax.fori_loop(1, edge, inner, 0)
    body(edge, ((0, edge - 1, False, True), (1, edge, False, True)))


def both(ref, col, part):
    rows = slice(part * TILE, (part + 1) * TILE)
    return jnp.concatenate([ref[col, rows, :], ref[COLS + col, rows, :]], axis=0)


def penalties(rows_ref, m_ref, unit, w, col):
    found = []
    inside = rows_ref[unit + 3] != 0
    for key_frame in range(FRAMES):
        at = key_frame * TILE + rows_ref[unit] * COLS + col
        cells = []
        for frame in range(FRAMES):
            live = (m_ref[frame * COLS + w, at] != 0) & inside
            cells.append(jnp.broadcast_to(jnp.where(live, 0.0, BIG).astype(F32), (1, TILE)))
        found.append(jnp.concatenate(cells, axis=1))
    return found


def fold(x, op):
    return op(x.reshape(TILE // 8, 8, 2 * TILE), axis=0)


def grad_side(gd_ref, w):
    g = both(gd_ref, w, 0)
    delta = []
    for frame in range(FRAMES):
        extra = gd_ref[frame * COLS + w, TILE:, :].astype(F32)
        delta.append(extra[0:1, :] + extra[1:2, :])
    return g, jnp.concatenate(delta, axis=1)


def step_grads(kv_ref, kt_ref, dk_ref, dv_ref, out_ref, at, prob, q, g, delta, col, first, last):
    dprob = dot_nt(both(kv_ref, col, 1), g)
    dscore = (prob * (dprob - delta)).astype(BF16)
    prob = prob.astype(BF16)
    dv = dot_nn(prob, g)
    dk = dot_nn(dscore, q)
    if first:
        turned_keys = jnp.concatenate([kv_ref[col, :TILE, :].T, kv_ref[COLS + col, :TILE, :].T], axis=1)
        kt_ref[col] = turned_keys
    else:
        turned_keys = kt_ref[col]
    for frame in range(FRAMES):
        rows = slice(frame * TILE, (frame + 1) * TILE)
        tile = frame * COLS + col
        dv_here, dk_here = dv[rows], dk[rows]
        if not first:
            dv_here += dv_ref[tile]
            dk_here += dk_ref[tile]
        if last:
            out_ref[tile, at * TILE : (at + 1) * TILE, :] = (dk_here * SCALE).astype(BF16)
            out_ref[tile, (at + 1) * TILE : (at + 2) * TILE, :] = dv_here.astype(BF16)
        else:
            dv_ref[tile] = dv_here
            dk_ref[tile] = dk_here
    return dot_nn(turned_keys, dscore)


def halves(x):
    return [x[:TILE], x[TILE:]]


def early_kernel(rows_ref, m_ref, first_ref, near_ref, e_ref, peak_ref, total_ref, s_ref):
    units = ((0, near_ref), (1, first_ref))

    def body(w, steps):
        q = both(first_ref, w, 2)
        top = jnp.full((8, 2 * TILE), -BIG, F32)
        pens = {}
        for unit, kv_ref in units:
            for place, col, _, _ in steps:
                s = dot_nt(both(kv_ref, col, 0), q)
                s_ref[unit, place] = s
                pens[unit, place] = penalties(rows_ref, m_ref, unit, w, col)
                for piece, pen in zip(halves(s), pens[unit, place]):
                    top = jnp.maximum(top, fold(piece, jnp.max) - pen)
        peak = jnp.max(top, axis=0, keepdims=True)
        total = jnp.zeros((8, 2 * TILE), F32)
        for unit, _ in units:
            for place, _, _, _ in steps:
                for frame in range(FRAMES):
                    rows = slice(frame * TILE, (frame + 1) * TILE)
                    e = jnp.exp2(s_ref[unit, place, rows, :] * C - (peak * C + pens[unit, place][frame]))
                    e_ref[w, unit, place, rows, :] = e.astype(BF16)
                    total += fold(e, jnp.sum)
        peak_ref[w] = jnp.broadcast_to(peak, (8, 2 * TILE))
        total_ref[w] = jnp.broadcast_to(jnp.sum(total, axis=0, keepdims=True), (8, 2 * TILE))

    sweep(body)


def far_kernel(
    rows_ref, m_ref, first_ref, gd_ref, far_ref, peak_ref, total_ref, part_ref, share_ref, dqt_ref,
    s_ref, kt_ref, dk_ref, dv_ref,
):
    def body(w, steps):
        q = both(first_ref, w, 2)
        g, delta = grad_side(gd_ref, w)
        early = peak_ref[w]
        top = early
        pens = {}
        for place, col, _, _ in steps:
            s = dot_nt(both(far_ref, col, 0), q)
            s_ref[place] = s
            pens[place] = penalties(rows_ref, m_ref, 2, w, col)
            for piece, pen in zip(halves(s), pens[place]):
                top = jnp.maximum(top, fold(piece, jnp.max) - pen)
        peak = jnp.max(top, axis=0, keepdims=True)
        total = jnp.zeros((8, 2 * TILE), F32)
        for place, _, _, _ in steps:
            for frame in range(FRAMES):
                rows = slice(frame * TILE, (frame + 1) * TILE)
                e = jnp.exp2(s_ref[place, rows, :] * C - (peak * C + pens[place][frame]))
                s_ref[place, rows, :] = e
                total += fold(e, jnp.sum)
        shrink = jnp.exp2((early[0:1, :] - peak) * C)
        share = 1.0 / (jnp.sum(total, axis=0, keepdims=True) + total_ref[w, 0:1, :] * shrink)
        share_ref[w] = jnp.broadcast_to(shrink * share, (8, 2 * TILE))
        dqt = jnp.zeros((DIM, 2 * TILE), F32)
        for place, col, first, last in steps:
            prob = s_ref[place] * share
            dqt += step_grads(far_ref, kt_ref, dk_ref, dv_ref, part_ref, 0, prob, q, g, delta, col, first, last)
        dqt_ref[w] = dqt

    sweep(body)


def rest_kernel(
    first_ref, gd_ref, near_ref, e_ref, share_ref, dqt_ref, part_ref, mine_ref,
    ktc_ref, kto_ref, dkc_ref, dvc_ref, dko_ref, dvo_ref,
):
    def body(w, steps):
        q = both(first_ref, w, 2)
        g, delta = grad_side(gd_ref, w)
        share = share_ref[w, 0:1, :]
        dqt = dqt_ref[w]
        for place, col, first, last in steps:
            prob = e_ref[w, 0, place].astype(F32) * share
            dqt += step_grads(near_ref, ktc_ref, dkc_ref, dvc_ref, part_ref, 0, prob, q, g, delta, col, first, last)
            prob = e_ref[w, 1, place].astype(F32) * share
            dqt += step_grads(first_ref, kto_ref, dko_ref, dvo_ref, mine_ref, 1, prob, q, g, delta, col, first, last)
        dq = (dqt.T * SCALE).astype(BF16)
        mine_ref[w, :TILE, :] = dq[:TILE]
        mine_ref[COLS + w, :TILE, :] = dq[TILE:]

    sweep(body)


def acc():
    return pltpu.VMEM((GROUP, TILE, DIM), F32)


def turned():
    return pltpu.VMEM((COLS, DIM, 2 * TILE), BF16)


ROWS_OF = jax.ShapeDtypeStruct((COLS, 8, 2 * TILE), F32)
PART = jax.ShapeDtypeStruct((GROUP, 2 * TILE, DIM), BF16)


def early(rows, live, first, near):
    return pl.pallas_call(
        early_kernel,
        in_specs=[SMEM, SMEM, VM, VM],
        out_specs=[VM, VM, VM],
        out_shape=[jax.ShapeDtypeStruct((COLS, 2, 3, 2 * TILE, 2 * TILE), BF16), ROWS_OF, ROWS_OF],
        scratch_shapes=[pltpu.VMEM((2, 3, 2 * TILE, 2 * TILE), F32)],
        compiler_params=params(),
        cost_estimate=pl.CostEstimate(flops=2 * 10**9, bytes_accessed=3 * 2**20, transcendentals=3 * 10**6),
        name="near_and_own_scores",
    )(rows, live, first, near)


def far_row(rows, live, first, gd, far, peak, total):
    return pl.pallas_call(
        far_kernel,
        in_specs=[SMEM, SMEM, VM, VM, VM, VM, VM],
        out_specs=[VM, VM, VM],
        out_shape=[PART, ROWS_OF, jax.ShapeDtypeStruct((COLS, DIM, 2 * TILE), F32)],
        scratch_shapes=[pltpu.VMEM((3, 2 * TILE, 2 * TILE), F32), turned(), acc(), acc()],
        compiler_params=params(),
        cost_estimate=pl.CostEstimate(flops=2 * 10**9, bytes_accessed=2**22, transcendentals=2 * 10**6),
        name="far_row",
    )(rows, live, first, gd, far, peak, total)


def rest(first, gd, near, e, share, dqt):
    return pl.pallas_call(
        rest_kernel,
        in_specs=[VM] * 6,
        out_specs=[VM, VM],
        out_shape=[PART, jax.ShapeDtypeStruct((GROUP, 3 * TILE, DIM), BF16)],
        scratch_shapes=[turned(), turned(), acc(), acc(), acc(), acc()],
        compiler_params=params(),
        cost_estimate=pl.CostEstimate(flops=4 * 10**9, bytes_accessed=2**23, transcendentals=0),
        name="near_and_own_rows",
    )(first, gd, near, e, share, dqt)


def per_device(queries, keys, values, d_out, saved_out, mask):
    group = ("frame", "head")
    row = lax.axis_index("row")
    is_even = lax.rem(row, 2) == 0
    chip_swap = [(i, i ^ 1) for i in range(ROWS)]
    link_swap = [(i, i + 1) for i in range(1, ROWS - 1, 2)] + [(i + 1, i) for i in range(1, ROWS - 1, 2)]

    def exchange(x):
        return lax.all_to_all(x, group, split_axis=0, concat_axis=0, tiled=True)

    w = lax.axis_index("head").astype(jnp.int32).reshape(1)
    first = exchange(pack_first(w, keys, values, queries, mask))
    second = pack_second(d_out, saved_out)
    first, second = lax.optimization_barrier((first, second))
    own = first[:, : 2 * TILE, :]
    far = lax.ppermute(own, "row", link_swap)
    near = lax.ppermute(own, "row", chip_swap)
    gd = exchange(second)

    far_index = jnp.where(is_even, row - 1, row + 1)
    near_index = jnp.where(is_even, row + 1, row - 1)
    rows = jnp.stack([near_index, row, far_index]).astype(jnp.int32)
    inside = ((rows >= 0) & (rows < ROWS)).astype(jnp.int32)
    rows = jnp.concatenate([jnp.clip(rows, 0, ROWS - 1), inside])
    live = first[:, 3 * TILE : 3 * TILE + 2, :].astype(jnp.int32).reshape(GROUP, 2 * TILE)

    e, peak, total = early(rows, live, first, near)
    far_part, share, dqt = far_row(rows, live, first, gd, far, peak, total)
    far_back = lax.ppermute(far_part, "row", link_swap)
    near_part, mine = rest(first, gd, near, e, share, dqt)
    far_back, mine = lax.optimization_barrier((far_back, mine))
    near_back = lax.ppermute(near_part, "row", chip_swap)
    return tuple(unpack(exchange(add_parts(mine, near_back, far_back))))


def solution(mesh):
    devices = mesh.devices
    if mesh.axis_names != ("head", "blk"):
        raise ValueError("mesh axes")
    heads = devices.shape[0]
    grid = Mesh(devices.reshape(heads, FRAMES, devices.shape[1] // FRAMES), ("head", "frame", "row"))
    tokens = P(("frame", "row", "head"), None)
    return jax.shard_map(
        per_device,
        mesh=grid,
        in_specs=(tokens,) * 5 + (P(("frame", "row"), None),),
        out_specs=(tokens,) * 3,
        check_vma=False,
    )
```

time: 156 us -> 113 us (0.72)
  Pallas kernels: 64.1 us -> 32.7 us
  blocking collectives: 0 us -> 26.8 us
  waiting for transfers between devices: 46.1 us -> 25.9 us
  starting transfers between devices: 36.7 us -> 22.4 us
  other arithmetic: 3.64 us -> 0.17 us
    pallas_call x5 -> x7, Pallas kernels: 64.1 us -> 32.7 us  [the longest x1 9.74 us: rest(): pl.pallas_call(rest_kernel, in_specs=[VM] * 6, out_specs=[VM, VM], out_sh...]
    all_to_all x0 -> x1, blocking collectives: none -> 26.8 us  [exchange(): return lax.all_to_all(x, group, split_axis=0, concat_axis=0, tiled=True)]
    all_to_all x4 -> x2, starting transfers between devices: 25.3 us -> 11.3 us  [exchange(): return lax.all_to_all(x, group, split_axis=0, concat_axis=0, tiled=True)]
    all_to_all x4 -> x2, waiting for transfers between devices: 36.3 us -> 23 us  [exchange(): return lax.all_to_all(x, group, split_axis=0, concat_axis=0, tiled=True)]
    ppermute x1, waiting for transfers between devices: 3.81 us -> 0.01 us  [per_device(): far = lax.ppermute(own, 'row', link_swap)]
    ppermute x1, waiting for transfers between devices: 6 us -> 2.89 us  [per_device(): far_back = lax.ppermute(far_part, 'row', link_swap)]
    convert_element_type x1 -> x0, other arithmetic: 2.93 us -> none  [per_device(): both = exchange(total.astype(BF16))]
    ppermute x1, starting transfers between devices: 6.52 us -> 4.63 us  [per_device(): far = lax.ppermute(own, 'row', link_swap)]
  transfers between devices with their start and end apart: 8 -> 6, of which waited for: 6 -> 3; matrix products, arithmetic and copies ran while one was open for 4% -> 0% of each run, Pallas kernels for 2% -> 15%
where the time goes in v1:
time: 113 us
  Pallas kernels  32.7 us (29%)
  blocking collectives  26.8 us (24%)
  waiting for transfers between devices  25.9 us (23%)
  starting transfers between devices  22.4 us (20%)
  local copies, waits for them, and re-layouts  3.78 us (3%)
    all_to_all x1, blocking collectives, exchange(): return lax.all_to_all(x, group, split_axis=0, concat_axis=0, tiled=True)  26.8 us
    all_to_all x2, waiting for transfers between devices, exchange(): return lax.all_to_all(x, group, split_axis=0, concat_axis=0, tiled=True)  23 us
    all_to_all x2, starting transfers between devices, exchange(): return lax.all_to_all(x, group, split_axis=0, concat_axis=0, tiled=True)  11.3 us
    pallas_call x1, Pallas kernels, rest(): pl.pallas_call(rest_kernel, in_specs=[VM] * 6, out_specs=[VM, VM], out_sh...  9.74 us
    pallas_call x1, Pallas kernels, far_row(): pl.pallas_call(far_kernel, in_specs=[SMEM, SMEM, VM, VM, VM, VM, VM], out...  9.68 us
    pallas_call x1, Pallas kernels, early(): pl.pallas_call(early_kernel, in_specs=[SMEM, SMEM, VM, VM], out_specs=[VM...  5.81 us
    ppermute x1, starting transfers between devices, per_device(): far = lax.ppermute(own, 'row', link_swap)  4.63 us
    ppermute x1, starting transfers between devices, per_device(): far_back = lax.ppermute(far_part, 'row', link_swap)  4.57 us
  transfers between devices with their start and end apart: 6, of which 3 were waited for; matrix products, arithmetic and copies ran while one was open for 0% of the time, Pallas kernels for 15%

profile of v1, /device:TPU:97, one launch (start us, length us, event | category | flops | bytes accessed | tf_op | source)
XLA Modules:
  0.0 112.6 jit_solution(4983633690128902042)
XLA Ops:
  0.6 3.6 %pack_first.1 = bf16[16,400,128]{2,1,0:T(8,128)(2,1)} custom-call(s32[1]{0:T(128)} %bitcast.3.w_ref, bf16[128,2048]{1,0:T(8,128)(2,1)} %k_ref.1, bf16[128,2048]{1,0:T(8,128)(2,1)} %v_ref.1, bf16[128,2048]{1,0:T(8,128)(2,1)} %q_ref.1, s32[8,256]{1,0:T(8,128)} %m_ref.1), custom_call_target="tpu_custom_call" | custom-call | bytes 3145728 | tf_op jit(solution)/shard_map/pack_first/pallas_call | solution.py:82
  4.3 0.0 copy-start
  4.3 0.0 copy-start.1
  4.3 6.9 %all-to-all-start = ((bf16[16,400,128]{2,1,0:T(8,128)(2,1)}), bf16[16,400,128]{2,1,0:T(8,128)(2,1)S(1)}, u32[]{:S(2)}, u32[]{:S(2)}) async-start(bf16[16,400,128]{2,1,0:T(8,128)(2,1)} %pack_first.1), calls=%async_computation | async-start | bytes 3276800 | tf_op jit(solution)/shard_map/all_to_all | solution.py:407
  11.2 0.0 copy-done
  11.2 0.0 copy-done.1
  11.2 1.9 %pack_second.1 = bf16[16,144,128]{2,1,0:T(8,128)(2,1)} custom-call(bf16[128,2048]{1,0:T(8,128)(2,1)S(1)} %copy-done, bf16[128,2048]{1,0:T(8,128)(2,1)S(1)} %copy-done.1), custom_call_target="tpu_custom_call" | custom-call | flops 1048576 | bytes 1572864 | tf_op jit(solution)/shard_map/pack_second/pallas_call | solution.py:116
  13.1 21.4 %all-to-all-done.first_ref = bf16[16,400,128]{2,1,0:T(8,128)(2,1)S(1)} async-done(((bf16[16,400,128]{2,1,0:T(8,128)(2,1)}), bf16[16,400,128]{2,1,0:T(8,128)(2,1)S(1)}, u32[]{:S(2)}, u32[]{:S(2)}) %all-to-all-start) | async-done | bytes 1638432 | tf_op jit(solution)/shard_map/all_to_all | solution.py:407
  34.5 1.1 slice.7
  35.6 1.9 %collective-permute-start.1 = (bf16[16,256,128]{2,1,0:T(8,128)(2,1)}, bf16[16,256,128]{2,1,0:T(8,128)(2,1)S(1)}, u32[]{:S(2)}, u32[]{:S(2)}) collective-permute-start(bf16[16,256,128]{2,1,0:T(8,128)(2,1)} %slice.7), channel_id=1, source_target_pairs={{0,1},{1,0},{2,3},{3,2},{4,5},{5,4},{6,7},{7,6},{8,9},{9,8},{10,11... | collective-permute-start | bytes 3145736 | tf_op jit(solution)/shard_map/ppermute | solution.py:415
  37.5 4.6 %collective-permute-start = (bf16[16,256,128]{2,1,0:T(8,128)(2,1)}, bf16[16,256,128]{2,1,0:T(8,128)(2,1)}, u32[]{:S(2)}, u32[]{:S(2)}) collective-permute-start(bf16[16,256,128]{2,1,0:T(8,128)(2,1)} %slice.7), channel_id=1, source_target_pairs={{1,2},{3,4},{5,6},{7,8},{9,10},{11,12},{13,14},{2,1},{4,3},{6,5},{... | collective-permute-start | bytes 3145736 | tf_op jit(solution)/shard_map/ppermute | solution.py:414
  42.2 0.1 broadcast_clamp_fusion
  42.2 4.4 %all-to-all-start.1 = ((bf16[16,144,128]{2,1,0:T(8,128)(2,1)}), bf16[16,144,128]{2,1,0:T(8,128)(2,1)S(1)}, u32[]{:S(2)}, u32[]{:S(2)}) async-start(bf16[16,144,128]{2,1,0:T(8,128)(2,1)} %pack_second.1), calls=%async_computation.1 | async-start | bytes 1179648 | tf_op jit(solution)/shard_map/all_to_all | solution.py:407
  46.6 0.1 pad_add_fusion.1.rows_ref
  46.7 0.0 collective-permute-done.1.near_ref
  46.8 5.8 %near_and_own_scores.1 = (bf16[8,2,3,256,256]{4,3,2,1,0:T(8,128)(2,1)S(1)}, f32[8,8,256]{2,1,0:T(8,128)S(1)}, f32[8,8,256]{2,1,0:T(8,128)S(1)}) custom-call(s32[6]{0:T(128)S(1)} %pad_add_fusion.1.rows_ref, s32[16,256]{1,0:T(8,128)S(1)} %bitcast.8, bf16[16,400,128]{2,1,0:T(8,128)(2,1)S(1)} %all-to-all-done.first_ref, ...), custom_call_target="tpu_custom_call" | custom-call | flops 2000000000 | bytes 3145728 | tf_op jit(solution)/shard_map/near_and_own_scores/pallas_call | solution.py:361
  52.6 0.0 copy-start.2
  52.6 2.6 %copy-done.2 = bf16[8,2,3,256,256]{4,3,2,1,0:T(8,128)(2,1)} copy-done((bf16[8,2,3,256,256]{4,3,2,1,0:T(8,128)(2,1)}, bf16[8,2,3,256,256]{4,3,2,1,0:T(8,128)(2,1)S(1)}, u32[]{:S(2)}) %copy-start.2) | copy-done | bytes 6291480
  55.2 1.6 %all-to-all-done.1.gd_ref = bf16[16,144,128]{2,1,0:T(8,128)(2,1)S(1)} async-done(((bf16[16,144,128]{2,1,0:T(8,128)(2,1)}), bf16[16,144,128]{2,1,0:T(8,128)(2,1)S(1)}, u32[]{:S(2)}, u32[]{:S(2)}) %all-to-all-start.1) | async-done | bytes 589856 | tf_op jit(solution)/shard_map/all_to_all | solution.py:407
  56.8 0.0 collective-permute-done.far_ref
  56.8 0.0 copy-start.3
  56.8 9.7 %far_row.1 = (bf16[16,256,128]{2,1,0:T(8,128)(2,1)S(1)}, f32[8,8,256]{2,1,0:T(8,128)S(1)}, f32[8,128,256]{2,1,0:T(8,128)S(1)}) custom-call(s32[6]{0:T(128)S(1)} %pad_add_fusion.1.rows_ref, s32[16,256]{1,0:T(8,128)S(1)} %bitcast.9, bf16[16,400,128]{2,1,0:T(8,128)(2,1)S(1)} %all-to-all-done.first_ref, bf16[16,144,128]{2,1,0:T(8,128)(2,1)S(1)} %all-to-all-done.1.gd_ref, ...), custom_call_target="tpu_custom_call" | custom-call | flops 2000000000 | bytes 4194304 | tf_op jit(solution)/shard_map/far_row/pallas_call | solution.py:374
  66.5 4.6 %collective-permute-start.2 = (bf16[16,256,128]{2,1,0:T(8,128)(2,1)S(1)}, bf16[16,256,128]{2,1,0:T(8,128)(2,1)S(1)}, u32[]{:S(2)}, u32[]{:S(2)}) collective-permute-start(bf16[16,256,128]{2,1,0:T(8,128)(2,1)S(1)} %get-tuple-element.19), channel_id=1, source_target_pairs={{1,2},{3,4},{5,6},{7,8},{9,10},{11,12},{13,14},{2,1},{4,3},{6,5},{... | collective-permute-start | bytes 3145736 | tf_op jit(solution)/shard_map/ppermute | solution.py:427
  71.1 0.0 copy-done.3
  71.1 9.7 %near_and_own_rows.1 = (bf16[16,256,128]{2,1,0:T(8,128)(2,1)S(1)}, bf16[16,384,128]{2,1,0:T(8,128)(2,1)S(1)}) custom-call(bf16[16,400,128]{2,1,0:T(8,128)(2,1)S(1)} %all-to-all-done.first_ref, bf16[16,144,128]{2,1,0:T(8,128)(2,1)S(1)} %all-to-all-done.1.gd_ref, bf16[16,256,128]{2,1,0:T(8,128)(2,1)S(1)} %collective-permute-done.1.near_ref, ...), custom_call_target="tpu_custom_call" | custom-call | flops 4000000000 | bytes 8388608 | tf_op jit(solution)/shard_map/near_and_own_rows/pallas_call | solution.py:387
  80.8 0.1 collective-permute-start.3
  80.9 2.9 %collective-permute-done.2.far_ref = bf16[16,256,128]{2,1,0:T(8,128)(2,1)S(1)} collective-permute-done((bf16[16,256,128]{2,1,0:T(8,128)(2,1)S(1)}, bf16[16,256,128]{2,1,0:T(8,128)(2,1)S(1)}, u32[]{:S(2)}, u32[]{:S(2)}) %collective-permute-start.2) | collective-permute-done | bytes 1048608 | tf_op jit(solution)/shard_map/ppermute | solution.py:427
  83.8 0.0 collective-permute-done.3.near_ref
  83.8 0.5 add_parts.1
  84.3 26.8 %all_to_all.15.in_ref = bf16[16,384,128]{2,1,0:T(8,128)(2,1)S(1)} all-to-all(bf16[16,384,128]{2,1,0:T(8,128)(2,1)S(1)} %add_parts.1), channel_id=1, replica_groups=mesh['head'=8,'frame'=2,'row'=16] {'frame','head'}, dimensions={0} | all-to-all | bytes 3145728 | tf_op jit(solution)/shard_map/all_to_all | solution.py:407
  111.1 1.5 %unpack_grads.1 = (bf16[128,2048]{1,0:T(8,128)(2,1)}, bf16[128,2048]{1,0:T(8,128)(2,1)}, bf16[128,2048]{1,0:T(8,128)(2,1)}) custom-call(bf16[16,384,128]{2,1,0:T(8,128)(2,1)S(1)} %all_to_all.15.in_ref), custom_call_target="tpu_custom_call" | custom-call | bytes 3145728 | tf_op jit(solution)/shard_map/unpack_grads/pallas_call | solution.py:146
  (3 shorter events, 0.0 us)
Async XLA Ops:
  4.3 6.9 %copy-start = (bf16[128,2048]{1,0:T(8,128)(2,1)S(1)}, bf16[128,2048]{1,0:T(8,128)(2,1)}, u32[]{:S(2)}) copy-start(bf16[128,2048]{1,0:T(8,128)(2,1)} %g_ref.1) | copy-start | bytes 1572868
  4.3 6.9 %copy-start.1 = (bf16[128,2048]{1,0:T(8,128)(2,1)S(1)}, bf16[128,2048]{1,0:T(8,128)(2,1)}, u32[]{:S(2)}) copy-start(bf16[128,2048]{1,0:T(8,128)(2,1)} %o_ref.1) | copy-start | bytes 1572868
  4.3 30.3 %all-to-all-start = ((bf16[16,400,128]{2,1,0:T(8,128)(2,1)}), bf16[16,400,128]{2,1,0:T(8,128)(2,1)S(1)}, u32[]{:S(2)}, u32[]{:S(2)}) async-start(bf16[16,400,128]{2,1,0:T(8,128)(2,1)} %pack_first.1), calls=%async_computation | async-start | bytes 3276800 | tf_op jit(solution)/shard_map/all_to_all | solution.py:407
  35.6 11.1 %collective-permute-start.1 = (bf16[16,256,128]{2,1,0:T(8,128)(2,1)}, bf16[16,256,128]{2,1,0:T(8,128)(2,1)S(1)}, u32[]{:S(2)}, u32[]{:S(2)}) collective-permute-start(bf16[16,256,128]{2,1,0:T(8,128)(2,1)} %slice.7), channel_id=1, source_target_pairs={{0,1},{1,0},{2,3},{3,2},{4,5},{5,4},{6,7},{7,6},{8,9},{9,8},{10,11... | collective-permute-start | bytes 3145736 | tf_op jit(solution)/shard_map/ppermute | solution.py:415
  37.5 19.3 %collective-permute-start = (bf16[16,256,128]{2,1,0:T(8,128)(2,1)}, bf16[16,256,128]{2,1,0:T(8,128)(2,1)}, u32[]{:S(2)}, u32[]{:S(2)}) collective-permute-start(bf16[16,256,128]{2,1,0:T(8,128)(2,1)} %slice.7), channel_id=1, source_target_pairs={{1,2},{3,4},{5,6},{7,8},{9,10},{11,12},{13,14},{2,1},{4,3},{6,5},{... | collective-permute-start | bytes 3145736 | tf_op jit(solution)/shard_map/ppermute | solution.py:414
  42.2 14.6 %all-to-all-start.1 = ((bf16[16,144,128]{2,1,0:T(8,128)(2,1)}), bf16[16,144,128]{2,1,0:T(8,128)(2,1)S(1)}, u32[]{:S(2)}, u32[]{:S(2)}) async-start(bf16[16,144,128]{2,1,0:T(8,128)(2,1)} %pack_second.1), calls=%async_computation.1 | async-start | bytes 1179648 | tf_op jit(solution)/shard_map/all_to_all | solution.py:407
  52.6 2.7 %copy-start.2 = (bf16[8,2,3,256,256]{4,3,2,1,0:T(8,128)(2,1)}, bf16[8,2,3,256,256]{4,3,2,1,0:T(8,128)(2,1)S(1)}, u32[]{:S(2)}) copy-start(bf16[8,2,3,256,256]{4,3,2,1,0:T(8,128)(2,1)S(1)} %get-tuple-element.20.e_ref) | copy-start | bytes 18874372
  56.8 14.3 %copy-start.3 = (bf16[8,2,3,256,256]{4,3,2,1,0:T(8,128)(2,1)S(1)}, bf16[8,2,3,256,256]{4,3,2,1,0:T(8,128)(2,1)}, u32[]{:S(2)}) copy-start(bf16[8,2,3,256,256]{4,3,2,1,0:T(8,128)(2,1)} %copy-done.2) | copy-start | bytes 18874372
  66.5 17.3 %collective-permute-start.2 = (bf16[16,256,128]{2,1,0:T(8,128)(2,1)S(1)}, bf16[16,256,128]{2,1,0:T(8,128)(2,1)S(1)}, u32[]{:S(2)}, u32[]{:S(2)}) collective-permute-start(bf16[16,256,128]{2,1,0:T(8,128)(2,1)S(1)} %get-tuple-element.19), channel_id=1, source_target_pairs={{1,2},{3,4},{5,6},{7,8},{9,10},{11,12},{13,14},{2,1},{4,3},{6,5},{... | collective-permute-start | bytes 3145736 | tf_op jit(solution)/shard_map/ppermute | solution.py:427
  80.8 3.0 %collective-permute-start.3 = (bf16[16,256,128]{2,1,0:T(8,128)(2,1)S(1)}, bf16[16,256,128]{2,1,0:T(8,128)(2,1)S(1)}, u32[]{:S(2)}, u32[]{:S(2)}) collective-permute-start(bf16[16,256,128]{2,1,0:T(8,128)(2,1)S(1)} %get-tuple-element.25), channel_id=1, source_target_pairs={{0,1},{1,0},{2,3},{3,2},{4,5},{5,4},{6,7},{7,6},{8,9},{9,8},{10,11... | collective-permute-start | bytes 3145736 | tf_op jit(solution)/shard_map/ppermute | solution.py:430

commit v2 on v1

--- a/solution.py
+++ b/solution.py
@@ -15,8 +15,7 @@
 FRAMES = 2
 GROUP = FRAMES * COLS
 EXTRA = 16
-FIRST = 3 * TILE + EXTRA
-SECOND = TILE + EXTRA
+SECOND = 2 * TILE + EXTRA
 BIG = 1e30
 SCALE = DIM**-0.5
 C = SCALE * 1.4426950408889634
@@ -42,9 +41,9 @@
 CHUNKS = 4
 
 
-def pack_first_kernel(w_ref, k_ref, v_ref, q_ref, m_ref, out_ref, buf_ref, mine_ref, in_sem, out_sem, mine_sem):
+def pack_first_kernel(k_ref, v_ref, out_ref, buf_ref, in_sem, out_sem):
     wide = HEADS // CHUNKS * DIM
-    refs = (k_ref, v_ref, q_ref)
+    refs = (k_ref, v_ref)
 
     def fetch(part, i):
         cols = pl.ds(i * wide, wide)
@@ -55,74 +54,66 @@
             buf_ref.at[part, :, pl.ds(h * DIM, DIM)], out_ref.at[h, pl.ds(part * TILE, TILE), :], out_sem.at[part, h]
         )
 
-    def send_mask(h):
-        return pltpu.make_async_copy(mine_ref, out_ref.at[h, pl.ds(3 * TILE, EXTRA), :], mine_sem.at[h])
-
     for i in range(CHUNKS):
-        for part in range(3):
+        for part in range(2):
             fetch(part, i).start()
-    mine = m_ref[pl.ds(w_ref[0], 1), :].astype(F32)
-    rows = lax.broadcasted_iota(jnp.int32, (EXTRA, TILE), 0)
-    extra = jnp.where(rows == 0, mine[:, :TILE], 0.0)
-    mine_ref[...] = jnp.where(rows == 1, mine[:, TILE:], extra).astype(BF16)
     for i in range(CHUNKS):
-        for part in range(3):
+        for part in range(2):
             fetch(part, i).wait()
             for h in range(i * HEADS // CHUNKS, (i + 1) * HEADS // CHUNKS):
                 send(part, h).start()
     for h in range(HEADS):
-        send_mask(h).start()
-    for h in range(HEADS):
-        for part in range(3):
+        for part in range(2):
             send(part, h).wait()
-        send_mask(h).wait()
-
-
-def pack_first(w, keys, values, queries, mask):
+
+
+def pack_first(keys, values):
     return pl.pallas_call(
         pack_first_kernel,
-        in_specs=[SMEM, ANY, ANY, ANY, VM],
+        in_specs=[ANY, ANY],
         out_specs=ANY,
-        out_shape=jax.ShapeDtypeStruct((HEADS, FIRST, DIM), BF16),
+        out_shape=jax.ShapeDtypeStruct((HEADS, 2 * TILE, DIM), BF16),
         scratch_shapes=[
-            pltpu.VMEM((3, TILE, HEADS * DIM), BF16),
-            pltpu.VMEM((EXTRA, TILE), BF16),
-            pltpu.SemaphoreType.DMA((3, CHUNKS)),
-            pltpu.SemaphoreType.DMA((3, HEADS)),
-            pltpu.SemaphoreType.DMA((HEADS,)),
+            pltpu.VMEM((2, TILE, HEADS * DIM), BF16),
+            pltpu.SemaphoreType.DMA((2, CHUNKS)),
+            pltpu.SemaphoreType.DMA((2, HEADS)),
         ],
         compiler_params=pltpu.CompilerParams(vmem_limit_bytes=58 * 1024 * 1024),
-        cost_estimate=pl.CostEstimate(flops=0, bytes_accessed=3 * 2**20, transcendentals=0),
-        name="pack_first",
-    )(w, keys, values, queries, mask)
-
-
-def pack_second_kernel(g_ref, o_ref, out_ref):
+        cost_estimate=pl.CostEstimate(flops=0, bytes_accessed=2**21, transcendentals=0),
+        name="pack_keys_values",
+    )(keys, values)
+
+
+def pack_second_kernel(w_ref, q_ref, g_ref, o_ref, m_ref, out_ref):
+    mine = m_ref[pl.ds(w_ref[0], 1), :].astype(F32)
     rows = lax.broadcasted_iota(jnp.int32, (EXTRA, TILE), 0)
     for h in range(out_ref.shape[0]):
         cols = slice(h * DIM, (h + 1) * DIM)
         g = g_ref[:, cols]
-        out_ref[h, :TILE, :] = g
+        out_ref[h, :TILE, :] = q_ref[:, cols]
+        out_ref[h, TILE : 2 * TILE, :] = g
         prod = g.astype(F32) * o_ref[:, cols].astype(F32)
         delta = jnp.sum(prod.T, axis=0, keepdims=True)
         high = delta.astype(BF16).astype(F32)
         extra = jnp.where(rows == 0, high, 0.0)
-        out_ref[h, TILE:, :] = jnp.where(rows == 1, delta - high, extra).astype(BF16)
-
-
-def pack_second(g, o):
+        extra = jnp.where(rows == 1, delta - high, extra)
+        extra = jnp.where(rows == 2, mine[:, :TILE], extra)
+        out_ref[h, 2 * TILE :, :] = jnp.where(rows == 3, mine[:, TILE:], extra).astype(BF16)
+
+
+def pack_second(w, q, g, o, mask):
     step = 4
     block = pl.BlockSpec((TILE, step * DIM), lambda i: (0, i))
     return pl.pallas_call(
         pack_second_kernel,
         grid=(HEADS // step,),
-        in_specs=[block, block],
+        in_specs=[SMEM, block, block, block, pl.BlockSpec((COLS, 2 * TILE), lambda i: (0, 0))],
         out_specs=pl.BlockSpec((step, SECOND, DIM), lambda i: (i, 0, 0)),
         out_shape=jax.ShapeDtypeStruct((HEADS, SECOND, DIM), BF16),
         compiler_params=small(),
-        cost_estimate=pl.CostEstimate(flops=2**20, bytes_accessed=3 * 2**19, transcendentals=0),
-        name="pack_second",
-    )(g, o)
+        cost_estimate=pl.CostEstimate(flops=2**20, bytes_accessed=5 * 2**19, transcendentals=0),
+        name="pack_queries",
+    )(w, q, g, o, mask)
 
 
 def unpack_kernel(in_ref, q_ref, k_ref, v_ref, sem):
@@ -185,16 +176,23 @@
     return lax.dot_general(a, b, (((1,), (0,)), ((), ())), preferred_element_type=F32)
 
 
+EDGE_LEFT = ((1, 0, True, False), (2, 1, True, False))
+EDGE_RIGHT = ((0, COLS - 2, False, True), (1, COLS - 1, False, True))
+
+
+def inner_steps(w):
+    return ((0, w - 1, False, True), (1, w, False, False), (2, w + 1, True, False))
+
+
 def sweep(body):
-    edge = COLS - 1
-    body(0, ((1, 0, True, False), (2, 1, True, False)))
+    body(0, EDGE_LEFT)
 
     def inner(w, carry):
-        body(w, ((0, w - 1, False, True), (1, w, False, False), (2, w + 1, True, False)))
+        body(w, inner_steps(w))
         return carry
 
-    lax.fori_loop(1, edge, inner, 0)
-    body(edge, ((0, edge - 1, False, True), (1, edge, False, True)))
+    lax.fori_loop(1, COLS - 1, inner, 0)
+    body(COLS - 1, EDGE_RIGHT)
 
 
 def both(ref, col, part):
@@ -219,13 +217,14 @@
     return op(x.reshape(TILE // 8, 8, 2 * TILE), axis=0)
 
 
-def grad_side(gd_ref, w):
-    g = both(gd_ref, w, 0)
+def query_side(qd_ref, w):
+    q = both(qd_ref, w, 0)
+    g = both(qd_ref, w, 1)
     delta = []
     for frame in range(FRAMES):
-        extra = gd_ref[frame * COLS + w, TILE:, :].astype(F32)
+        extra = qd_ref[frame * COLS + w, 2 * TILE :, :].astype(F32)
         delta.append(extra[0:1, :] + extra[1:2, :])
-    return g, jnp.concatenate(delta, axis=1)
+    return q, g, jnp.concatenate(delta, axis=1)
 
 
 def step_grads(kv_ref, kt_ref, dk_ref, dv_ref, out_ref, at, prob, q, g, delta, col, first, last):
@@ -259,11 +258,11 @@
     return [x[:TILE], x[TILE:]]
 
 
-def early_kernel(rows_ref, m_ref, first_ref, near_ref, e_ref, peak_ref, total_ref, s_ref):
-    units = ((0, near_ref), (1, first_ref))
+def early_kernel(rows_ref, m_ref, qd_ref, own_ref, near_ref, e_ref, peak_ref, total_ref, s_ref):
+    units = ((0, near_ref), (1, own_ref))
 
     def body(w, steps):
-        q = both(first_ref, w, 2)
+        q = both(qd_ref, w, 0)
         top = jnp.full((8, 2 * TILE), -BIG, F32)
         pens = {}
         for unit, kv_ref in units:
@@ -289,24 +288,26 @@
 
 
 def far_kernel(
-    rows_ref, m_ref, first_ref, gd_ref, far_ref, peak_ref, total_ref, part_ref, share_ref, dqt_ref,
-    s_ref, kt_ref, dk_ref, dv_ref,
+    rows_ref, m_ref, qd_ref, far_ref, peak_ref, total_ref, part_ref, share_ref, dqt_ref,
+    even_ref, odd_ref, kt_ref, dk_ref, dv_ref,
 ):
-    def body(w, steps):
-        q = both(first_ref, w, 2)
-        g, delta = grad_side(gd_ref, w)
+    def weigh(w, s_ref):
+        q = both(qd_ref, w, 0)
         early = peak_ref[w]
         top = early
-        pens = {}
-        for place, col, _, _ in steps:
+        pens = []
+        for place in range(3):
+            wanted = w + place - 1
+            col = jnp.clip(wanted, 0, COLS - 1)
             s = dot_nt(both(far_ref, col, 0), q)
             s_ref[place] = s
-            pens[place] = penalties(rows_ref, m_ref, 2, w, col)
+            outside = jnp.where(wanted == col, 0.0, BIG).astype(F32)
+            pens.append([pen + outside for pen in penalties(rows_ref, m_ref, 2, w, col)])
             for piece, pen in zip(halves(s), pens[place]):
                 top = jnp.maximum(top, fold(piece, jnp.max) - pen)
         peak = jnp.max(top, axis=0, keepdims=True)
         total = jnp.zeros((8, 2 * TILE), F32)
-        for place, _, _, _ in steps:
+        for place in range(3):
             for frame in range(FRAMES):
                 rows = slice(frame * TILE, (frame + 1) * TILE)
                 e = jnp.exp2(s_ref[place, rows, :] * C - (peak * C + pens[place][frame]))
@@ -315,29 +316,46 @@
         shrink = jnp.exp2((early[0:1, :] - peak) * C)
         share = 1.0 / (jnp.sum(total, axis=0, keepdims=True) + total_ref[w, 0:1, :] * shrink)
         share_ref[w] = jnp.broadcast_to(shrink * share, (8, 2 * TILE))
+        return share
+
+    def grads(w, share, s_ref, steps):
+        q, g, delta = query_side(qd_ref, w)
         dqt = jnp.zeros((DIM, 2 * TILE), F32)
         for place, col, first, last in steps:
             prob = s_ref[place] * share
             dqt += step_grads(far_ref, kt_ref, dk_ref, dv_ref, part_ref, 0, prob, q, g, delta, col, first, last)
         dqt_ref[w] = dqt
 
-    sweep(body)
+    edge = COLS - 1
+    share = weigh(0, even_ref)
+    later = weigh(1, odd_ref)
+    grads(0, share, even_ref, EDGE_LEFT)
+
+    def two(i, share):
+        w = 2 * i + 1
+        later = weigh(w + 1, even_ref)
+        grads(w, share, odd_ref, inner_steps(w))
+        share = weigh(w + 2, odd_ref)
+        grads(w + 1, later, even_ref, inner_steps(w + 1))
+        return share
+
+    share = lax.fori_loop(0, (COLS - 2) // 2, two, later)
+    grads(edge, share, odd_ref, EDGE_RIGHT)
 
 
 def rest_kernel(
-    first_ref, gd_ref, near_ref, e_ref, share_ref, dqt_ref, part_ref, mine_ref,
+    qd_ref, own_ref, near_ref, e_ref, share_ref, dqt_ref, part_ref, mine_ref,
     ktc_ref, kto_ref, dkc_ref, dvc_ref, dko_ref, dvo_ref,
 ):
     def body(w, steps):
-        q = both(first_ref, w, 2)
-        g, delta = grad_side(gd_ref, w)
+        q, g, delta = query_side(qd_ref, w)
         share = share_ref[w, 0:1, :]
         dqt = dqt_ref[w]
         for place, col, first, last in steps:
             prob = e_ref[w, 0, place].astype(F32) * share
             dqt += step_grads(near_ref, ktc_ref, dkc_ref, dvc_ref, part_ref, 0, prob, q, g, delta, col, first, last)
             prob = e_ref[w, 1, place].astype(F32) * share
-            dqt += step_grads(first_ref, kto_ref, dko_ref, dvo_ref, mine_ref, 1, prob, q, g, delta, col, first, last)
+            dqt += step_grads(own_ref, kto_ref, dko_ref, dvo_ref, mine_ref, 1, prob, q, g, delta, col, first, last)
         dq = (dqt.T * SCALE).astype(BF16)
         mine_ref[w, :TILE, :] = dq[:TILE]
         mine_ref[COLS + w, :TILE, :] = dq[TILE:]
@@ -357,33 +375,33 @@
 PART = jax.ShapeDtypeStruct((GROUP, 2 * TILE, DIM), BF16)
 
 
-def early(rows, live, first, near):
+def early(rows, live, qd, own, near):
     return pl.pallas_call(
         early_kernel,
-        in_specs=[SMEM, SMEM, VM, VM],
+        in_specs=[SMEM, SMEM, VM, VM, VM],
         out_specs=[VM, VM, VM],
         out_shape=[jax.ShapeDtypeStruct((COLS, 2, 3, 2 * TILE, 2 * TILE), BF16), ROWS_OF, ROWS_OF],
         scratch_shapes=[pltpu.VMEM((2, 3, 2 * TILE, 2 * TILE), F32)],
         compiler_params=params(),
         cost_estimate=pl.CostEstimate(flops=2 * 10**9, bytes_accessed=3 * 2**20, transcendentals=3 * 10**6),
         name="near_and_own_scores",
-    )(rows, live, first, near)
-
-
-def far_row(rows, live, first, gd, far, peak, total):
+    )(rows, live, qd, own, near)
+
+
+def far_row(rows, live, qd, far, peak, total):
     return pl.pallas_call(
         far_kernel,
-        in_specs=[SMEM, SMEM, VM, VM, VM, VM, VM],
+        in_specs=[SMEM, SMEM, VM, VM, VM, VM],
         out_specs=[VM, VM, VM],
         out_shape=[PART, ROWS_OF, jax.ShapeDtypeStruct((COLS, DIM, 2 * TILE), F32)],
-        scratch_shapes=[pltpu.VMEM((3, 2 * TILE, 2 * TILE), F32), turned(), acc(), acc()],
+        scratch_shapes=[pltpu.VMEM((3, 2 * TILE, 2 * TILE), F32)] * 2 + [turned(), acc(), acc()],
         compiler_params=params(),
         cost_estimate=pl.CostEstimate(flops=2 * 10**9, bytes_accessed=2**22, transcendentals=2 * 10**6),
         name="far_row",
-    )(rows, live, first, gd, far, peak, total)
-
-
-def rest(first, gd, near, e, share, dqt):
+    )(rows, live, qd, far, peak, total)
+
+
+def rest(qd, own, near, e, share, dqt):
     return pl.pallas_call(
         rest_kernel,
         in_specs=[VM] * 6,
@@ -393,7 +411,7 @@
         compiler_params=params(),
         cost_estimate=pl.CostEstimate(flops=4 * 10**9, bytes_accessed=2**23, transcendentals=0),
         name="near_and_own_rows",
-    )(first, gd, near, e, share, dqt)
+    )(qd, own, near, e, share, dqt)
 
 
 def per_device(queries, keys, values, d_out, saved_out, mask):
@@ -407,25 +425,24 @@
         return lax.all_to_all(x, group, split_axis=0, concat_axis=0, tiled=True)
 
     w = lax.axis_index("head").astype(jnp.int32).reshape(1)
-    first = exchange(pack_first(w, keys, values, queries, mask))
-    second = pack_second(d_out, saved_out)
-    first, second = lax.optimization_barrier((first, second))
-    own = first[:, : 2 * TILE, :]
+    own = exchange(pack_first(keys, values))
+    second = pack_second(w, queries, d_out, saved_out, mask)
+    own, second = lax.optimization_barrier((own, second))
+    qd = exchange(second)
     far = lax.ppermute(own, "row", link_swap)
     near = lax.ppermute(own, "row", chip_swap)
-    gd = exchange(second)
 
     far_index = jnp.where(is_even, row - 1, row + 1)
     near_index = jnp.where(is_even, row + 1, row - 1)
     rows = jnp.stack([near_index, row, far_index]).astype(jnp.int32)
     inside = ((rows >= 0) & (rows < ROWS)).astype(jnp.int32)
     rows = jnp.concatenate([jnp.clip(rows, 0, ROWS - 1), inside])
-    live = first[:, 3 * TILE : 3 * TILE + 2, :].astype(jnp.int32).reshape(GROUP, 2 * TILE)
-
-    e, peak, total = early(rows, live, first, near)
-    far_part, share, dqt = far_row(rows, live, first, gd, far, peak, total)
+    live = qd[:, 2 * TILE + 2 : 2 * TILE + 4, :].astype(jnp.int32).reshape(GROUP, 2 * TILE)
+
+    e, peak, total = early(rows, live, qd, own, near)
+    far_part, share, dqt = far_row(rows, live, qd, far, peak, total)
     far_back = lax.ppermute(far_part, "row", link_swap)
-    near_part, mine = rest(first, gd, near, e, share, dqt)
+    near_part, mine = rest(qd, own, near, e, share, dqt)
     far_back, mine = lax.optimization_barrier((far_back, mine))
     near_back = lax.ppermute(near_part, "row", chip_swap)
     return tuple(unpack(exchange(add_parts(mine, near_back, far_back))))

time: 113 us -> 108 us (0.956); the launches traced: 113 us -> 106 us
  starting transfers between devices: 22.4 us -> 27.3 us
  local copies, waits for them, and re-layouts: 3.78 us -> 0.03 us
  Pallas kernels: 32.7 us -> 29.4 us
  waiting for transfers between devices: 25.9 us -> 23.1 us
  blocking collectives: 26.8 us -> 25.5 us
    ppermute x1, starting transfers between devices: 4.57 us -> 8.09 us  [per_device(): far_back = lax.ppermute(far_part, 'row', link_swap)]
    pallas_call x4, Pallas kernels: 21 us -> 17.7 us  [the longest x1 7.58 us: far_row(): pl.pallas_call(far_kernel, in_specs=[SMEM, SMEM, VM, VM, VM, VM], out_spe...]
    unnamed x9, local copies, waits for them, and re-layouts: 2.67 us -> 0.03 us
    all_to_all x2, waiting for transfers between devices: 23 us -> 20.4 us  [exchange(): return lax.all_to_all(x, group, split_axis=0, concat_axis=0, tiled=True)]
    all_to_all x1, blocking collectives: 26.8 us -> 25.5 us  [exchange(): return lax.all_to_all(x, group, split_axis=0, concat_axis=0, tiled=True)]
    all_to_all x2, starting transfers between devices: 11.3 us -> 12.5 us  [exchange(): return lax.all_to_all(x, group, split_axis=0, concat_axis=0, tiled=True)]
  transfers between devices with their start and end apart: 6 -> 6, of which waited for: 3 -> 3; matrix products, arithmetic and copies ran while one was open for 0% -> 0% of each run, Pallas kernels for 15% -> 16%
where the time goes in v2:
time: 108 us; the launch traced here: 106 us
  Pallas kernels  29.4 us (27%)
  starting transfers between devices  27.3 us (25%)
  blocking collectives  25.5 us (24%)
  waiting for transfers between devices  23.1 us (21%)
    all_to_all x1, blocking collectives, exchange(): return lax.all_to_all(x, group, split_axis=0, concat_axis=0, tiled=True)  25.5 us
    all_to_all x2, waiting for transfers between devices, exchange(): return lax.all_to_all(x, group, split_axis=0, concat_axis=0, tiled=True)  20.4 us
    all_to_all x2, starting transfers between devices, exchange(): return lax.all_to_all(x, group, split_axis=0, concat_axis=0, tiled=True)  12.5 us
    pallas_call x1, Pallas kernels, rest(): pl.pallas_call(rest_kernel, in_specs=[VM] * 6, out_specs=[VM, VM], out_sh...  9.7 us
    ppermute x1, starting transfers between devices, per_device(): far_back = lax.ppermute(far_part, 'row', link_swap)  8.09 us
    pallas_call x1, Pallas kernels, far_row(): pl.pallas_call(far_kernel, in_specs=[SMEM, SMEM, VM, VM, VM, VM], out_spe...  7.58 us
    pallas_call x1, Pallas kernels, early(): pl.pallas_call(early_kernel, in_specs=[SMEM, SMEM, VM, VM, VM], out_specs...  5.8 us
    ppermute x1, starting transfers between devices, per_device(): far = lax.ppermute(own, 'row', link_swap)  4.66 us
  transfers between devices with their start and end apart: 6, of which 3 were waited for; matrix products, arithmetic and copies ran while one was open for 0% of the time, Pallas kernels for 16%

profile of v2, /device:TPU:97, one launch (start us, length us, event | category | flops | bytes accessed | tf_op | source)
XLA Modules:
  0.0 106.4 jit_solution(15230382468814973930)
XLA Ops:
  0.6 2.4 %pack_keys_values.1 = bf16[16,256,128]{2,1,0:T(8,128)(2,1)} custom-call(bf16[128,2048]{1,0:T(8,128)(2,1)} %k_ref.1, bf16[128,2048]{1,0:T(8,128)(2,1)} %v_ref.1), custom_call_target="tpu_custom_call" | custom-call | bytes 2097152 | tf_op jit(solution)/shard_map/pack_keys_values/pallas_call | solution.py:71
  3.0 0.0 copy-start
  3.0 0.0 copy-start.1
  3.0 0.0 copy-start.2
  3.0 0.0 copy-start.3
  3.0 6.9 %all-to-all-start = ((bf16[16,256,128]{2,1,0:T(8,128)(2,1)}), bf16[16,256,128]{2,1,0:T(8,128)(2,1)S(1)}, u32[]{:S(2)}, u32[]{:S(2)}) async-start(bf16[16,256,128]{2,1,0:T(8,128)(2,1)} %pack_keys_values.1), calls=%async_computation | async-start | bytes 2097152 | tf_op jit(solution)/shard_map/all_to_all | solution.py:425
  9.9 0.0 copy-done
  10.0 0.0 copy-done.1
  10.0 0.0 copy-done.2
  10.0 0.0 copy-done.3
  10.0 2.0 %pack_queries.1 = bf16[16,272,128]{2,1,0:T(8,128)(2,1)} custom-call(s32[1]{0:T(128)} %bitcast.3.w_ref, bf16[128,2048]{1,0:T(8,128)(2,1)S(1)} %copy-done, bf16[128,2048]{1,0:T(8,128)(2,1)S(1)} %copy-done.1, bf16[128,2048]{1,0:T(8,128)(2,1)S(1)} %copy-done.2, s32[8,256]{1,0:T(8,128)S(1)} %copy-done.3), custom_call_target="tpu_custom_call" | custom-call | flops 1048576 | bytes 2621440 | tf_op jit(solution)/shard_map/pack_queries/pallas_call | solution.py:107
  12.0 12.6 %all-to-all-done.own_ref = bf16[16,256,128]{2,1,0:T(8,128)(2,1)S(1)} async-done(((bf16[16,256,128]{2,1,0:T(8,128)(2,1)}), bf16[16,256,128]{2,1,0:T(8,128)(2,1)S(1)}, u32[]{:S(2)}, u32[]{:S(2)}) %all-to-all-start) | async-done | bytes 1048608 | tf_op jit(solution)/shard_map/all_to_all | solution.py:425
  24.6 5.6 %all-to-all-start.1 = ((bf16[16,272,128]{2,1,0:T(8,128)(2,1)}), bf16[16,272,128]{2,1,0:T(8,128)(2,1)S(1)}, u32[]{:S(2)}, u32[]{:S(2)}) async-start(bf16[16,272,128]{2,1,0:T(8,128)(2,1)} %pack_queries.1), calls=%async_computation.1 | async-start | bytes 2228224 | tf_op jit(solution)/shard_map/all_to_all | solution.py:425
  30.2 2.0 %collective-permute-start.1 = (bf16[16,256,128]{2,1,0:T(8,128)(2,1)S(1)}, bf16[16,256,128]{2,1,0:T(8,128)(2,1)S(1)}, u32[]{:S(2)}, u32[]{:S(2)}) collective-permute-start(bf16[16,256,128]{2,1,0:T(8,128)(2,1)S(1)} %all-to-all-done.own_ref), channel_id=1, source_target_pairs={{0,1},{1,0},{2,3},{3,2},{4,5},{5,4},{6,7},{7,6},{8,9},{9,8},{10,11... | collective-permute-start | bytes 3145736 | tf_op jit(solution)/shard_map/ppermute | solution.py:433
  32.2 4.7 %collective-permute-start = (bf16[16,256,128]{2,1,0:T(8,128)(2,1)S(1)}, bf16[16,256,128]{2,1,0:T(8,128)(2,1)}, u32[]{:S(2)}, u32[]{:S(2)}) collective-permute-start(bf16[16,256,128]{2,1,0:T(8,128)(2,1)S(1)} %all-to-all-done.own_ref), channel_id=1, source_target_pairs={{1,2},{3,4},{5,6},{7,8},{9,10},{11,12},{13,14},{2,1},{4,3},{6,5},{... | collective-permute-start | bytes 3145736 | tf_op jit(solution)/shard_map/ppermute | solution.py:432
  36.9 0.1 broadcast_clamp_fusion
  37.0 0.1 pad_add_fusion.1.rows_ref
  37.0 7.8 %all-to-all-done.1.qd_ref = bf16[16,272,128]{2,1,0:T(8,128)(2,1)S(1)} async-done(((bf16[16,272,128]{2,1,0:T(8,128)(2,1)}), bf16[16,272,128]{2,1,0:T(8,128)(2,1)S(1)}, u32[]{:S(2)}, u32[]{:S(2)}) %all-to-all-start.1) | async-done | bytes 1114144 | tf_op jit(solution)/shard_map/all_to_all | solution.py:425
  44.9 0.0 collective-permute-done.1.near_ref
  44.9 5.8 %near_and_own_scores.1 = (bf16[8,2,3,256,256]{4,3,2,1,0:T(8,128)(2,1)S(1)}, f32[8,8,256]{2,1,0:T(8,128)S(1)}, f32[8,8,256]{2,1,0:T(8,128)S(1)}) custom-call(s32[6]{0:T(128)S(1)} %pad_add_fusion.1.rows_ref, s32[16,256]{1,0:T(8,128)S(1)} %bitcast.8, bf16[16,272,128]{2,1,0:T(8,128)(2,1)S(1)} %all-to-all-done.1.qd_ref, ...), custom_call_target="tpu_custom_call" | custom-call | flops 2000000000 | bytes 3145728 | tf_op jit(solution)/shard_map/near_and_own_scores/pallas_call | solution.py:379
  50.7 0.0 collective-permute-done.far_ref
  50.7 7.6 %far_row.1 = (bf16[16,256,128]{2,1,0:T(8,128)(2,1)S(1)}, f32[8,8,256]{2,1,0:T(8,128)S(1)}, f32[8,128,256]{2,1,0:T(8,128)S(1)}) custom-call(s32[6]{0:T(128)S(1)} %pad_add_fusion.1.rows_ref, s32[16,256]{1,0:T(8,128)S(1)} %bitcast.9, bf16[16,272,128]{2,1,0:T(8,128)(2,1)S(1)} %all-to-all-done.1.qd_ref, bf16[16,256,128]{2,1,0:T(8,128)(2,1)} %collective-permute-done.far_ref, ...), custom_call_target="tpu_custom_call" | custom-call | flops 2000000000 | bytes 4194304 | tf_op jit(solution)/shard_map/far_row/pallas_call | solution.py:392
  58.3 8.1 %collective-permute-start.2 = (bf16[16,256,128]{2,1,0:T(8,128)(2,1)S(1)}, bf16[16,256,128]{2,1,0:T(8,128)(2,1)S(1)}, u32[]{:S(2)}, u32[]{:S(2)}) collective-permute-start(bf16[16,256,128]{2,1,0:T(8,128)(2,1)S(1)} %get-tuple-element.19), channel_id=1, source_target_pairs={{1,2},{3,4},{5,6},{7,8},{9,10},{11,12},{13,14},{2,1},{4,3},{6,5},{... | collective-permute-start | bytes 3145736 | tf_op jit(solution)/shard_map/ppermute | solution.py:444
  66.4 9.7 %near_and_own_rows.1 = (bf16[16,256,128]{2,1,0:T(8,128)(2,1)S(1)}, bf16[16,384,128]{2,1,0:T(8,128)(2,1)S(1)}) custom-call(bf16[16,272,128]{2,1,0:T(8,128)(2,1)S(1)} %all-to-all-done.1.qd_ref, bf16[16,256,128]{2,1,0:T(8,128)(2,1)S(1)} %all-to-all-done.own_ref, bf16[16,256,128]{2,1,0:T(8,128)(2,1)S(1)} %collective-permute-done.1.near_ref, ...), custom_call_target="tpu_custom_call" | custom-call | flops 4000000000 | bytes 8388608 | tf_op jit(solution)/shard_map/near_and_own_rows/pallas_call | solution.py:405
  76.1 0.1 collective-permute-start.3
  76.2 2.7 %collective-permute-done.2.far_ref = bf16[16,256,128]{2,1,0:T(8,128)(2,1)S(1)} collective-permute-done((bf16[16,256,128]{2,1,0:T(8,128)(2,1)S(1)}, bf16[16,256,128]{2,1,0:T(8,128)(2,1)S(1)}, u32[]{:S(2)}, u32[]{:S(2)}) %collective-permute-start.2) | collective-permute-done | bytes 1048608 | tf_op jit(solution)/shard_map/ppermute | solution.py:444
  78.9 0.0 collective-permute-done.3.near_ref
  78.9 0.5 add_parts.1
  79.3 25.5 %all_to_all.15.in_ref = bf16[16,384,128]{2,1,0:T(8,128)(2,1)S(1)} all-to-all(bf16[16,384,128]{2,1,0:T(8,128)(2,1)S(1)} %add_parts.1), channel_id=1, replica_groups=mesh['head'=8,'frame'=2,'row'=16] {'frame','head'}, dimensions={0} | all-to-all | bytes 3145728 | tf_op jit(solution)/shard_map/all_to_all | solution.py:425
  104.8 1.5 %unpack_grads.1 = (bf16[128,2048]{1,0:T(8,128)(2,1)}, bf16[128,2048]{1,0:T(8,128)(2,1)}, bf16[128,2048]{1,0:T(8,128)(2,1)}) custom-call(bf16[16,384,128]{2,1,0:T(8,128)(2,1)S(1)} %all_to_all.15.in_ref), custom_call_target="tpu_custom_call" | custom-call | bytes 3145728 | tf_op jit(solution)/shard_map/unpack_grads/pallas_call | solution.py:137
  (3 shorter events, 0.0 us)
Async XLA Ops:
  3.0 7.0 %copy-start = (bf16[128,2048]{1,0:T(8,128)(2,1)S(1)}, bf16[128,2048]{1,0:T(8,128)(2,1)}, u32[]{:S(2)}) copy-start(bf16[128,2048]{1,0:T(8,128)(2,1)} %q_ref.1) | copy-start | bytes 1572868
  3.0 7.0 %copy-start.1 = (bf16[128,2048]{1,0:T(8,128)(2,1)S(1)}, bf16[128,2048]{1,0:T(8,128)(2,1)}, u32[]{:S(2)}) copy-start(bf16[128,2048]{1,0:T(8,128)(2,1)} %g_ref.1) | copy-start | bytes 1572868
  3.0 7.0 %copy-start.2 = (bf16[128,2048]{1,0:T(8,128)(2,1)S(1)}, bf16[128,2048]{1,0:T(8,128)(2,1)}, u32[]{:S(2)}) copy-start(bf16[128,2048]{1,0:T(8,128)(2,1)} %o_ref.1) | copy-start | bytes 1572868
  3.0 7.0 %copy-start.3 = (s32[8,256]{1,0:T(8,128)S(1)}, s32[8,256]{1,0:T(8,128)}, u32[]{:S(2)}) copy-start(s32[8,256]{1,0:T(8,128)} %m_ref.1) | copy-start | bytes 24580
  3.0 21.6 %all-to-all-start = ((bf16[16,256,128]{2,1,0:T(8,128)(2,1)}), bf16[16,256,128]{2,1,0:T(8,128)(2,1)S(1)}, u32[]{:S(2)}, u32[]{:S(2)}) async-start(bf16[16,256,128]{2,1,0:T(8,128)(2,1)} %pack_keys_values.1), calls=%async_computation | async-start | bytes 2097152 | tf_op jit(solution)/shard_map/all_to_all | solution.py:425
  24.6 20.2 %all-to-all-start.1 = ((bf16[16,272,128]{2,1,0:T(8,128)(2,1)}), bf16[16,272,128]{2,1,0:T(8,128)(2,1)S(1)}, u32[]{:S(2)}, u32[]{:S(2)}) async-start(bf16[16,272,128]{2,1,0:T(8,128)(2,1)} %pack_queries.1), calls=%async_computation.1 | async-start | bytes 2228224 | tf_op jit(solution)/shard_map/all_to_all | solution.py:425
  30.2 14.6 %collective-permute-start.1 = (bf16[16,256,128]{2,1,0:T(8,128)(2,1)S(1)}, bf16[16,256,128]{2,1,0:T(8,128)(2,1)S(1)}, u32[]{:S(2)}, u32[]{:S(2)}) collective-permute-start(bf16[16,256,128]{2,1,0:T(8,128)(2,1)S(1)} %all-to-all-done.own_ref), channel_id=1, source_target_pairs={{0,1},{1,0},{2,3},{3,2},{4,5},{5,4},{6,7},{7,6},{8,9},{9,8},{10,11... | collective-permute-start | bytes 3145736 | tf_op jit(solution)/shard_map/ppermute | solution.py:433
  32.2 18.5 %collective-permute-start = (bf16[16,256,128]{2,1,0:T(8,128)(2,1)S(1)}, bf16[16,256,128]{2,1,0:T(8,128)(2,1)}, u32[]{:S(2)}, u32[]{:S(2)}) collective-permute-start(bf16[16,256,128]{2,1,0:T(8,128)(2,1)S(1)} %all-to-all-done.own_ref), channel_id=1, source_target_pairs={{1,2},{3,4},{5,6},{7,8},{9,10},{11,12},{13,14},{2,1},{4,3},{6,5},{... | collective-permute-start | bytes 3145736 | tf_op jit(solution)/shard_map/ppermute | solution.py:432
  58.3 20.6 %collective-permute-start.2 = (bf16[16,256,128]{2,1,0:T(8,128)(2,1)S(1)}, bf16[16,256,128]{2,1,0:T(8,128)(2,1)S(1)}, u32[]{:S(2)}, u32[]{:S(2)}) collective-permute-start(bf16[16,256,128]{2,1,0:T(8,128)(2,1)S(1)} %get-tuple-element.19), channel_id=1, source_target_pairs={{1,2},{3,4},{5,6},{7,8},{9,10},{11,12},{13,14},{2,1},{4,3},{6,5},{... | collective-permute-start | bytes 3145736 | tf_op jit(solution)/shard_map/ppermute | solution.py:444
  76.1 2.8 %collective-permute-start.3 = (bf16[16,256,128]{2,1,0:T(8,128)(2,1)S(1)}, bf16[16,256,128]{2,1,0:T(8,128)(2,1)S(1)}, u32[]{:S(2)}, u32[]{:S(2)}) collective-permute-start(bf16[16,256,128]{2,1,0:T(8,128)(2,1)S(1)} %get-tuple-element.25), channel_id=1, source_target_pairs={{0,1},{1,0},{2,3},{3,2},{4,5},{5,4},{6,7},{7,6},{8,9},{9,8},{10,11... | collective-permute-start | bytes 3145736 | tf_op jit(solution)/shard_map/ppermute | solution.py:447

commit v3 on v2

--- a/solution.py
+++ b/solution.py
@@ -15,6 +15,8 @@
 FRAMES = 2
 GROUP = FRAMES * COLS
 EXTRA = 16
+NEAR_FLOPS = 2 * 10**9
+OWN_FLOPS = 2 * 10**9
 SECOND = 2 * TILE + EXTRA
 BIG = 1e30
 SCALE = DIM**-0.5
@@ -148,8 +150,10 @@
 
 def add_kernel(mine_ref, near_ref, far_ref, out_ref):
     out_ref[:, :TILE, :] = mine_ref[:, :TILE, :]
-    total = mine_ref[:, TILE:, :].astype(F32) + near_ref[...].astype(F32) + far_ref[...].astype(F32)
-    out_ref[:, TILE:, :] = total.astype(BF16)
+    for i in range(out_ref.shape[0]):
+        far = far_ref[i * 2 * TILE : (i + 1) * 2 * TILE, :].astype(F32)
+        total = mine_ref[i, TILE:, :].astype(F32) + near_ref[i].astype(F32) + far
+        out_ref[i, TILE:, :] = total.astype(BF16)
 
 
 def add_parts(mine, near, far):
@@ -159,7 +163,7 @@
     return pl.pallas_call(
         add_kernel,
         grid=(GROUP // step,),
-        in_specs=[wide, block, block],
+        in_specs=[wide, block, pl.BlockSpec((step * 2 * TILE, DIM), lambda i: (i, 0))],
         out_specs=wide,
         out_shape=jax.ShapeDtypeStruct((GROUP, 3 * TILE, DIM), BF16),
         compiler_params=small(),
@@ -200,17 +204,45 @@
     return jnp.concatenate([ref[col, rows, :], ref[COLS + col, rows, :]], axis=0)
 
 
-def penalties(rows_ref, m_ref, unit, w, col):
+def penalties(rows_ref, m_ref, unit, w, place):
+    wanted = w + place - 1
+    col = jnp.clip(wanted, 0, COLS - 1)
+    inside = (rows_ref[unit + 3] != 0) & (wanted == col)
     found = []
-    inside = rows_ref[unit + 3] != 0
     for key_frame in range(FRAMES):
         at = key_frame * TILE + rows_ref[unit] * COLS + col
-        cells = []
+        found.append(
+            [
+                jnp.where((m_ref[frame * COLS + w, at] != 0) & inside, 0.0, BIG).astype(F32)
+                for frame in range(FRAMES)
+            ]
+        )
+    return found
+
+
+def shifted(x, pens, sign):
+    return jnp.concatenate([x[:, :TILE] + sign * pens[0], x[:, TILE:] + sign * pens[1]], axis=1)
+
+
+def exponentials(piece, level):
+    e = jnp.exp2(piece.reshape(TILE // 8, 8, 2 * TILE) * C - level[None])
+    return e.reshape(TILE, 2 * TILE), jnp.sum(e, axis=0)
+
+
+def score(rows_ref, m_ref, unit, kv_ref, q, w, s_ref, top):
+    cols = [jnp.clip(w + place - 1, 0, COLS - 1) for place in range(3)]
+    scores = dot_nt(jnp.concatenate([both(kv_ref, col, 0) for col in cols], axis=0), q)
+    for place in range(3):
+        pens = penalties(rows_ref, m_ref, unit, w, place)
         for frame in range(FRAMES):
-            live = (m_ref[frame * COLS + w, at] != 0) & inside
-            cells.append(jnp.broadcast_to(jnp.where(live, 0.0, BIG).astype(F32), (1, TILE)))
-        found.append(jnp.concatenate(cells, axis=1))
-    return found
+            piece = scores[(FRAMES * place + frame) * TILE : (FRAMES * place + frame + 1) * TILE]
+            s_ref[place, frame * TILE : (frame + 1) * TILE, :] = piece
+            top = jnp.maximum(top, shifted(fold(piece, jnp.max), pens[frame], -1.0))
+    return top
+
+
+def spread(x):
+    return jnp.broadcast_to(x, (8, 2 * TILE))
 
 
 def fold(x, op):
@@ -227,104 +259,95 @@
     return q, g, jnp.concatenate(delta, axis=1)
 
 
-def step_grads(kv_ref, kt_ref, dk_ref, dv_ref, out_ref, at, prob, q, g, delta, col, first, last):
-    dprob = dot_nt(both(kv_ref, col, 1), g)
+def column_grads(kv_ref, kt_ref, dk_ref, dv_ref, out_ref, at, prob, q, g, delta, steps):
+    dprob = dot_nt(jnp.concatenate([both(kv_ref, col, 1) for _, col, _, _ in steps], axis=0), g)
     dscore = (prob * (dprob - delta)).astype(BF16)
-    prob = prob.astype(BF16)
-    dv = dot_nn(prob, g)
+    dv = dot_nn(prob.astype(BF16), g)
     dk = dot_nn(dscore, q)
-    if first:
-        turned_keys = jnp.concatenate([kv_ref[col, :TILE, :].T, kv_ref[COLS + col, :TILE, :].T], axis=1)
-        kt_ref[col] = turned_keys
-    else:
-        turned_keys = kt_ref[col]
-    for frame in range(FRAMES):
-        rows = slice(frame * TILE, (frame + 1) * TILE)
-        tile = frame * COLS + col
-        dv_here, dk_here = dv[rows], dk[rows]
-        if not first:
-            dv_here += dv_ref[tile]
-            dk_here += dk_ref[tile]
-        if last:
-            out_ref[tile, at * TILE : (at + 1) * TILE, :] = (dk_here * SCALE).astype(BF16)
-            out_ref[tile, (at + 1) * TILE : (at + 2) * TILE, :] = dv_here.astype(BF16)
-        else:
-            dv_ref[tile] = dv_here
-            dk_ref[tile] = dk_here
-    return dot_nn(turned_keys, dscore)
-
-
-def halves(x):
-    return [x[:TILE], x[TILE:]]
-
-
-def early_kernel(rows_ref, m_ref, qd_ref, own_ref, near_ref, e_ref, peak_ref, total_ref, s_ref):
-    units = ((0, near_ref), (1, own_ref))
-
-    def body(w, steps):
+    turned_keys = []
+    for i, (_, col, first, last) in enumerate(steps):
+        if first:
+            kt_ref[col] = jnp.concatenate([kv_ref[col, :TILE, :].T, kv_ref[COLS + col, :TILE, :].T], axis=1)
+        turned_keys.append(kt_ref[col])
+        for frame in range(FRAMES):
+            rows = slice((FRAMES * i + frame) * TILE, (FRAMES * i + frame + 1) * TILE)
+            tile = frame * COLS + col
+            dv_here, dk_here = dv[rows], dk[rows]
+            if not first:
+                dv_here += dv_ref[tile]
+                dk_here += dk_ref[tile]
+            if last and at is None:
+                out_ref[pl.ds(tile * 2 * TILE, TILE), :] = (dk_here * SCALE).astype(BF16)
+                out_ref[pl.ds(tile * 2 * TILE + TILE, TILE), :] = dv_here.astype(BF16)
+            elif last:
+                out_ref[tile, at * TILE : (at + 1) * TILE, :] = (dk_here * SCALE).astype(BF16)
+                out_ref[tile, (at + 1) * TILE : (at + 2) * TILE, :] = dv_here.astype(BF16)
+            else:
+                dv_ref[tile] = dv_here
+                dk_ref[tile] = dk_here
+    return dot_nn(jnp.concatenate(turned_keys, axis=1), dscore)
+
+
+def early_kernel(rows_ref, m_ref, qd_ref, own_ref, near_ref, e_ref, peak_ref, total_ref, even_ref, odd_ref):
+    def scores(w, s_ref):
         q = both(qd_ref, w, 0)
         top = jnp.full((8, 2 * TILE), -BIG, F32)
-        pens = {}
-        for unit, kv_ref in units:
-            for place, col, _, _ in steps:
-                s = dot_nt(both(kv_ref, col, 0), q)
-                s_ref[unit, place] = s
-                pens[unit, place] = penalties(rows_ref, m_ref, unit, w, col)
-                for piece, pen in zip(halves(s), pens[unit, place]):
-                    top = jnp.maximum(top, fold(piece, jnp.max) - pen)
-        peak = jnp.max(top, axis=0, keepdims=True)
+        for unit, kv_ref in enumerate((near_ref, own_ref)):
+            top = score(rows_ref, m_ref, unit, kv_ref, q, w, s_ref.at[unit], top)
+        peak_ref[w] = spread(jnp.max(top, axis=0, keepdims=True))
+
+    def weigh(w, s_ref):
+        level = peak_ref[w] * C
         total = jnp.zeros((8, 2 * TILE), F32)
-        for unit, _ in units:
-            for place, _, _, _ in steps:
+        for unit in range(2):
+            for place in range(3):
+                pens = penalties(rows_ref, m_ref, unit, w, place)
                 for frame in range(FRAMES):
                     rows = slice(frame * TILE, (frame + 1) * TILE)
-                    e = jnp.exp2(s_ref[unit, place, rows, :] * C - (peak * C + pens[unit, place][frame]))
+                    e, part = exponentials(s_ref[unit, place, rows, :], shifted(level, pens[frame], 1.0))
                     e_ref[w, unit, place, rows, :] = e.astype(BF16)
-                    total += fold(e, jnp.sum)
-        peak_ref[w] = jnp.broadcast_to(peak, (8, 2 * TILE))
-        total_ref[w] = jnp.broadcast_to(jnp.sum(total, axis=0, keepdims=True), (8, 2 * TILE))
-
-    sweep(body)
+                    total += part
+        total_ref[w] = spread(jnp.sum(total, axis=0, keepdims=True))
+
+    def two(i, carry):
+        w = 2 * i
+        scores(w + 1, odd_ref)
+        weigh(w, even_ref)
+        scores(jnp.minimum(w + 2, COLS - 1), even_ref)
+        weigh(w + 1, odd_ref)
+        return carry
+
+    scores(0, even_ref)
+    lax.fori_loop(0, COLS // 2, two, 0)
 
 
 def far_kernel(
     rows_ref, m_ref, qd_ref, far_ref, peak_ref, total_ref, part_ref, share_ref, dqt_ref,
     even_ref, odd_ref, kt_ref, dk_ref, dv_ref,
 ):
+    part_ref[GROUP * 2 * TILE :, :] = jnp.zeros((EXTRA, DIM), BF16)
+
     def weigh(w, s_ref):
-        q = both(qd_ref, w, 0)
         early = peak_ref[w]
-        top = early
-        pens = []
-        for place in range(3):
-            wanted = w + place - 1
-            col = jnp.clip(wanted, 0, COLS - 1)
-            s = dot_nt(both(far_ref, col, 0), q)
-            s_ref[place] = s
-            outside = jnp.where(wanted == col, 0.0, BIG).astype(F32)
-            pens.append([pen + outside for pen in penalties(rows_ref, m_ref, 2, w, col)])
-            for piece, pen in zip(halves(s), pens[place]):
-                top = jnp.maximum(top, fold(piece, jnp.max) - pen)
-        peak = jnp.max(top, axis=0, keepdims=True)
+        top = score(rows_ref, m_ref, 2, far_ref, both(qd_ref, w, 0), w, s_ref, early)
+        peak = spread(jnp.max(top, axis=0, keepdims=True))
         total = jnp.zeros((8, 2 * TILE), F32)
         for place in range(3):
+            pens = penalties(rows_ref, m_ref, 2, w, place)
             for frame in range(FRAMES):
                 rows = slice(frame * TILE, (frame + 1) * TILE)
-                e = jnp.exp2(s_ref[place, rows, :] * C - (peak * C + pens[place][frame]))
+                e, part = exponentials(s_ref[place, rows, :], shifted(peak * C, pens[frame], 1.0))
                 s_ref[place, rows, :] = e
-                total += fold(e, jnp.sum)
-        shrink = jnp.exp2((early[0:1, :] - peak) * C)
-        share = 1.0 / (jnp.sum(total, axis=0, keepdims=True) + total_ref[w, 0:1, :] * shrink)
-        share_ref[w] = jnp.broadcast_to(shrink * share, (8, 2 * TILE))
-        return share
+                total += part
+        shrink = jnp.exp2((early - peak) * C)
+        share = 1.0 / (jnp.sum(total, axis=0, keepdims=True) + total_ref[w] * shrink)
+        share_ref[w] = shrink * share
+        return share[0:1, :]
 
     def grads(w, share, s_ref, steps):
         q, g, delta = query_side(qd_ref, w)
-        dqt = jnp.zeros((DIM, 2 * TILE), F32)
-        for place, col, first, last in steps:
-            prob = s_ref[place] * share
-            dqt += step_grads(far_ref, kt_ref, dk_ref, dv_ref, part_ref, 0, prob, q, g, delta, col, first, last)
-        dqt_ref[w] = dqt
+        prob = jnp.concatenate([s_ref[place] for place, _, _, _ in steps], axis=0) * share
+        dqt_ref[w] = column_grads(far_ref, kt_ref, dk_ref, dv_ref, part_ref, None, prob, q, g, delta, steps)
 
     edge = COLS - 1
     share = weigh(0, even_ref)
@@ -343,24 +366,28 @@
     grads(edge, share, odd_ref, EDGE_RIGHT)
 
 
-def rest_kernel(
-    qd_ref, own_ref, near_ref, e_ref, share_ref, dqt_ref, part_ref, mine_ref,
-    ktc_ref, kto_ref, dkc_ref, dvc_ref, dko_ref, dvo_ref,
-):
+def row_kernel(unit, qd_ref, kv_ref, e_ref, share_ref, dqt_ref, out_ref, sum_ref, kt_ref, dk_ref, dv_ref):
     def body(w, steps):
         q, g, delta = query_side(qd_ref, w)
         share = share_ref[w, 0:1, :]
-        dqt = dqt_ref[w]
-        for place, col, first, last in steps:
-            prob = e_ref[w, 0, place].astype(F32) * share
-            dqt += step_grads(near_ref, ktc_ref, dkc_ref, dvc_ref, part_ref, 0, prob, q, g, delta, col, first, last)
-            prob = e_ref[w, 1, place].astype(F32) * share
-            dqt += step_grads(own_ref, kto_ref, dko_ref, dvo_ref, mine_ref, 1, prob, q, g, delta, col, first, last)
-        dq = (dqt.T * SCALE).astype(BF16)
-        mine_ref[w, :TILE, :] = dq[:TILE]
-        mine_ref[COLS + w, :TILE, :] = dq[TILE:]
+        prob = jnp.concatenate([e_ref[w, unit, place] for place, _, _, _ in steps], axis=0).astype(F32) * share
+        dqt = dqt_ref[w] + column_grads(kv_ref, kt_ref, dk_ref, dv_ref, out_ref, unit, prob, q, g, delta, steps)
+        if unit == 1:
+            dq = (dqt.T * SCALE).astype(BF16)
+            out_ref[w, :TILE, :] = dq[:TILE]
+            out_ref[COLS + w, :TILE, :] = dq[TILE:]
+        else:
+            sum_ref[w] = dqt
 
     sweep(body)
+
+
+def near_kernel(qd_ref, kv_ref, e_ref, share_ref, dqt_ref, out_ref, sum_ref, kt_ref, dk_ref, dv_ref):
+    row_kernel(0, qd_ref, kv_ref, e_ref, share_ref, dqt_ref, out_ref, sum_ref, kt_ref, dk_ref, dv_ref)
+
+
+def own_kernel(qd_ref, kv_ref, e_ref, share_ref, dqt_ref, out_ref, kt_ref, dk_ref, dv_ref):
+    row_kernel(1, qd_ref, kv_ref, e_ref, share_ref, dqt_ref, out_ref, None, kt_ref, dk_ref, dv_ref)
 
 
 def acc():
@@ -373,6 +400,7 @@
 
 ROWS_OF = jax.ShapeDtypeStruct((COLS, 8, 2 * TILE), F32)
 PART = jax.ShapeDtypeStruct((GROUP, 2 * TILE, DIM), BF16)
+FAR_PART = jax.ShapeDtypeStruct((GROUP * 2 * TILE + EXTRA, DIM), BF16)
 
 
 def early(rows, live, qd, own, near):
@@ -381,7 +409,7 @@
         in_specs=[SMEM, SMEM, VM, VM, VM],
         out_specs=[VM, VM, VM],
         out_shape=[jax.ShapeDtypeStruct((COLS, 2, 3, 2 * TILE, 2 * TILE), BF16), ROWS_OF, ROWS_OF],
-        scratch_shapes=[pltpu.VMEM((2, 3, 2 * TILE, 2 * TILE), F32)],
+        scratch_shapes=[pltpu.VMEM((2, 3, 2 * TILE, 2 * TILE), F32)] * 2,
         compiler_params=params(),
         cost_estimate=pl.CostEstimate(flops=2 * 10**9, bytes_accessed=3 * 2**20, transcendentals=3 * 10**6),
         name="near_and_own_scores",
@@ -393,7 +421,7 @@
         far_kernel,
         in_specs=[SMEM, SMEM, VM, VM, VM, VM],
         out_specs=[VM, VM, VM],
-        out_shape=[PART, ROWS_OF, jax.ShapeDtypeStruct((COLS, DIM, 2 * TILE), F32)],
+        out_shape=[FAR_PART, ROWS_OF, jax.ShapeDtypeStruct((COLS, DIM, 2 * TILE), F32)],
         scratch_shapes=[pltpu.VMEM((3, 2 * TILE, 2 * TILE), F32)] * 2 + [turned(), acc(), acc()],
         compiler_params=params(),
         cost_estimate=pl.CostEstimate(flops=2 * 10**9, bytes_accessed=2**22, transcendentals=2 * 10**6),
@@ -401,17 +429,33 @@
     )(rows, live, qd, far, peak, total)
 
 
-def rest(qd, own, near, e, share, dqt):
-    return pl.pallas_call(
-        rest_kernel,
-        in_specs=[VM] * 6,
+SUMS = jax.ShapeDtypeStruct((COLS, DIM, 2 * TILE), F32)
+
+
+def near_row(qd, near, e, share, dqt):
+    return pl.pallas_call(
+        near_kernel,
+        in_specs=[VM] * 5,
         out_specs=[VM, VM],
-        out_shape=[PART, jax.ShapeDtypeStruct((GROUP, 3 * TILE, DIM), BF16)],
-        scratch_shapes=[turned(), turned(), acc(), acc(), acc(), acc()],
+        out_shape=[PART, SUMS],
+        scratch_shapes=[turned(), acc(), acc()],
         compiler_params=params(),
-        cost_estimate=pl.CostEstimate(flops=4 * 10**9, bytes_accessed=2**23, transcendentals=0),
-        name="near_and_own_rows",
-    )(qd, own, near, e, share, dqt)
+        cost_estimate=pl.CostEstimate(flops=NEAR_FLOPS, bytes_accessed=2**22, transcendentals=0),
+        name="near_row",
+    )(qd, near, e, share, dqt)
+
+
+def own_row(qd, own, e, share, dqt):
+    return pl.pallas_call(
+        own_kernel,
+        in_specs=[VM] * 5,
+        out_specs=VM,
+        out_shape=jax.ShapeDtypeStruct((GROUP, 3 * TILE, DIM), BF16),
+        scratch_shapes=[turned(), acc(), acc()],
+        compiler_params=params(),
+        cost_estimate=pl.CostEstimate(flops=OWN_FLOPS, bytes_accessed=2**22, transcendentals=0),
+        name="own_row",
+    )(qd, own, e, share, dqt)
 
 
 def per_device(queries, keys, values, d_out, saved_out, mask):
@@ -442,9 +486,9 @@
     e, peak, total = early(rows, live, qd, own, near)
     far_part, share, dqt = far_row(rows, live, qd, far, peak, total)
     far_back = lax.ppermute(far_part, "row", link_swap)
-    near_part, mine = rest(qd, own, near, e, share, dqt)
-    far_back, mine = lax.optimization_barrier((far_back, mine))
+    near_part, dqt = near_row(qd, near, e, share, dqt)
     near_back = lax.ppermute(near_part, "row", chip_swap)
+    mine = own_row(qd, own, e, share, dqt)
     return tuple(unpack(exchange(add_parts(mine, near_back, far_back))))
 
 

time: 108 us -> 106 us (0.981); the launches traced: 106 us -> 106 us
  Pallas kernels: 29.4 us -> 26.9 us
    pallas_call x1 -> x2, Pallas kernels: 9.7 us -> 8.76 us  [the longest x1 4.64 us: own_row(): pl.pallas_call(own_kernel, in_specs=[VM] * 5, out_specs=VM, out_shape=jax...]
  transfers between devices with their start and end apart: 6 -> 6, of which waited for: 3 -> 3; matrix products, arithmetic and copies ran while one was open for 0% -> 0% of each run, Pallas kernels for 16% -> 15%
where the time goes in v3:
time: 106 us
  starting transfers between devices  27.3 us (26%)
  Pallas kernels  26.9 us (25%)
  blocking collectives  26.3 us (25%)
  waiting for transfers between devices  24.1 us (23%)
    all_to_all x1, blocking collectives, exchange(): return lax.all_to_all(x, group, split_axis=0, concat_axis=0, tiled=True)  26.3 us
    all_to_all x2, waiting for transfers between devices, exchange(): return lax.all_to_all(x, group, split_axis=0, concat_axis=0, tiled=True)  20.4 us
    all_to_all x2, starting transfers between devices, exchange(): return lax.all_to_all(x, group, split_axis=0, concat_axis=0, tiled=True)  12.5 us
    ppermute x1, starting transfers between devices, per_device(): far_back = lax.ppermute(far_part, 'row', link_swap)  8.09 us
    pallas_call x1, Pallas kernels, far_row(): pl.pallas_call(far_kernel, in_specs=[SMEM, SMEM, VM, VM, VM, VM], out_spe...  6.67 us
    pallas_call x1, Pallas kernels, early(): pl.pallas_call(early_kernel, in_specs=[SMEM, SMEM, VM, VM, VM], out_specs...  5.07 us
    ppermute x1, starting transfers between devices, per_device(): far = lax.ppermute(own, 'row', link_swap)  4.66 us
    pallas_call x1, Pallas kernels, own_row(): pl.pallas_call(own_kernel, in_specs=[VM] * 5, out_specs=VM, out_shape=jax...  4.64 us
  transfers between devices with their start and end apart: 6, of which 3 were waited for; matrix products, arithmetic and copies ran while one was open for 0% of the time, Pallas kernels for 15%

profile of v3, /device:TPU:97, one launch (start us, length us, event | category | flops | bytes accessed | tf_op | source)
XLA Modules:
  0.0 105.6 jit_solution(14872106731213909130)
XLA Ops:
  0.6 2.4 %pack_keys_values.1 = bf16[16,256,128]{2,1,0:T(8,128)(2,1)} custom-call(bf16[128,2048]{1,0:T(8,128)(2,1)} %k_ref.1, bf16[128,2048]{1,0:T(8,128)(2,1)} %v_ref.1), custom_call_target="tpu_custom_call" | custom-call | bytes 2097152 | tf_op jit(solution)/shard_map/pack_keys_values/pallas_call | solution.py:73
  3.0 0.0 copy-start
  3.0 0.0 copy-start.1
  3.0 0.0 copy-start.2
  3.0 0.0 copy-start.3
  3.0 6.9 %all-to-all-start = ((bf16[16,256,128]{2,1,0:T(8,128)(2,1)}), bf16[16,256,128]{2,1,0:T(8,128)(2,1)S(1)}, u32[]{:S(2)}, u32[]{:S(2)}) async-start(bf16[16,256,128]{2,1,0:T(8,128)(2,1)} %pack_keys_values.1), calls=%async_computation | async-start | bytes 2097152 | tf_op jit(solution)/shard_map/all_to_all | solution.py:469
  9.9 0.0 copy-done
  10.0 0.0 copy-done.1
  10.0 0.0 copy-done.2
  10.0 0.0 copy-done.3
  10.0 2.0 %pack_queries.1 = bf16[16,272,128]{2,1,0:T(8,128)(2,1)} custom-call(s32[1]{0:T(128)} %bitcast.w_ref, bf16[128,2048]{1,0:T(8,128)(2,1)S(1)} %copy-done, bf16[128,2048]{1,0:T(8,128)(2,1)S(1)} %copy-done.1, bf16[128,2048]{1,0:T(8,128)(2,1)S(1)} %copy-done.2, s32[8,256]{1,0:T(8,128)S(1)} %copy-done.3), custom_call_target="tpu_custom_call" | custom-call | flops 1048576 | bytes 2621440 | tf_op jit(solution)/shard_map/pack_queries/pallas_call | solution.py:109
  12.0 12.6 %all-to-all-done.own_ref.kv_ref = bf16[16,256,128]{2,1,0:T(8,128)(2,1)S(1)} async-done(((bf16[16,256,128]{2,1,0:T(8,128)(2,1)}), bf16[16,256,128]{2,1,0:T(8,128)(2,1)S(1)}, u32[]{:S(2)}, u32[]{:S(2)}) %all-to-all-start) | async-done | bytes 1048608 | tf_op jit(solution)/shard_map/all_to_all | solution.py:469
  24.6 5.6 %all-to-all-start.1 = ((bf16[16,272,128]{2,1,0:T(8,128)(2,1)}), bf16[16,272,128]{2,1,0:T(8,128)(2,1)S(1)}, u32[]{:S(2)}, u32[]{:S(2)}) async-start(bf16[16,272,128]{2,1,0:T(8,128)(2,1)} %pack_queries.1), calls=%async_computation.1 | async-start | bytes 2228224 | tf_op jit(solution)/shard_map/all_to_all | solution.py:469
  30.2 2.0 %collective-permute-start = (bf16[16,256,128]{2,1,0:T(8,128)(2,1)S(1)}, bf16[16,256,128]{2,1,0:T(8,128)(2,1)S(1)}, u32[]{:S(2)}, u32[]{:S(2)}) collective-permute-start(bf16[16,256,128]{2,1,0:T(8,128)(2,1)S(1)} %all-to-all-done.own_ref.kv_ref), channel_id=1, source_target_pairs={{0,1},{1,0},{2,3},{3,2},{4,5},{5,4},{6,7},{7,6},{8,9},{9,8},{10,11... | collective-permute-start | bytes 3145736 | tf_op jit(solution)/shard_map/ppermute | solution.py:477
  32.2 4.7 %collective-permute-start.1 = (bf16[16,256,128]{2,1,0:T(8,128)(2,1)S(1)}, bf16[16,256,128]{2,1,0:T(8,128)(2,1)}, u32[]{:S(2)}, u32[]{:S(2)}) collective-permute-start(bf16[16,256,128]{2,1,0:T(8,128)(2,1)S(1)} %all-to-all-done.own_ref.kv_ref), channel_id=1, source_target_pairs={{1,2},{3,4},{5,6},{7,8},{9,10},{11,12},{13,14},{2,1},{4,3},{6,5},{... | collective-permute-start | bytes 3145736 | tf_op jit(solution)/shard_map/ppermute | solution.py:476
  36.9 0.1 broadcast_clamp_fusion
  37.0 0.1 pad_add_fusion.1.rows_ref
  37.0 7.8 %all-to-all-done.1.qd_ref = bf16[16,272,128]{2,1,0:T(8,128)(2,1)S(1)} async-done(((bf16[16,272,128]{2,1,0:T(8,128)(2,1)}), bf16[16,272,128]{2,1,0:T(8,128)(2,1)S(1)}, u32[]{:S(2)}, u32[]{:S(2)}) %all-to-all-start.1) | async-done | bytes 1114144 | tf_op jit(solution)/shard_map/all_to_all | solution.py:469
  44.9 0.0 collective-permute-done.near_ref.kv_ref
  44.9 5.1 %near_and_own_scores.1 = (bf16[8,2,3,256,256]{4,3,2,1,0:T(8,128)(2,1)S(1)}, f32[8,8,256]{2,1,0:T(8,128)S(1)}, f32[8,8,256]{2,1,0:T(8,128)S(1)}) custom-call(s32[6]{0:T(128)S(1)} %pad_add_fusion.1.rows_ref, s32[16,256]{1,0:T(8,128)S(1)} %bitcast.8, bf16[16,272,128]{2,1,0:T(8,128)(2,1)S(1)} %all-to-all-done.1.qd_ref, ...), custom_call_target="tpu_custom_call" | custom-call | flops 2000000000 | bytes 3145728 | tf_op jit(solution)/shard_map/near_and_own_scores/pallas_call | solution.py:407
  50.0 0.0 collective-permute-done.1.far_ref
  50.0 6.7 %far_row.1 = (bf16[4112,128]{1,0:T(8,128)(2,1)S(1)}, f32[8,8,256]{2,1,0:T(8,128)S(1)}, f32[8,128,256]{2,1,0:T(8,128)S(1)}) custom-call(s32[6]{0:T(128)S(1)} %pad_add_fusion.1.rows_ref, s32[16,256]{1,0:T(8,128)S(1)} %bitcast.9, bf16[16,272,128]{2,1,0:T(8,128)(2,1)S(1)} %all-to-all-done.1.qd_ref, bf16[16,256,128]{2,1,0:T(8,128)(2,1)} %collective-permute-done.1.far_ref, ...), custom_call_target="tpu_custom_call" | custom-call | flops 2000000000 | bytes 4194304 | tf_op jit(solution)/shard_map/far_row/pallas_call | solution.py:420
  56.7 8.1 %collective-permute-start.3 = (bf16[4112,128]{1,0:T(8,128)(2,1)S(1)}, bf16[4112,128]{1,0:T(8,128)(2,1)S(1)}, u32[]{:S(2)}, u32[]{:S(2)}) collective-permute-start(bf16[4112,128]{1,0:T(8,128)(2,1)S(1)} %get-tuple-element.22), channel_id=1, source_target_pairs={{1,2},{3,4},{5,6},{7,8},{9,10},{11,12},{13,14},{2,1},{4,3},{6,5},{... | collective-permute-start | bytes 3158024 | tf_op jit(solution)/shard_map/ppermute | solution.py:488
  64.8 4.1 %near_row.1 = (bf16[16,256,128]{2,1,0:T(8,128)(2,1)S(1)}, f32[8,128,256]{2,1,0:T(8,128)S(1)}) custom-call(bf16[16,272,128]{2,1,0:T(8,128)(2,1)S(1)} %all-to-all-done.1.qd_ref, bf16[16,256,128]{2,1,0:T(8,128)(2,1)S(1)} %collective-permute-done.near_ref.kv_ref, bf16[8,2,3,256,256]{4,3,2,1,0:T(8,128)(2,1)S(1)} %get-tuple-element.15.e_ref, ...), custom_call_target="tpu_custom_call" | custom-call | flops 2000000000 | bytes 4194304 | tf_op jit(solution)/shard_map/near_row/pallas_call | solution.py:436
  68.9 0.1 collective-permute-start.2
  69.0 4.6 %own_row.1.mine_ref = bf16[16,384,128]{2,1,0:T(8,128)(2,1)S(1)} custom-call(bf16[16,272,128]{2,1,0:T(8,128)(2,1)S(1)} %all-to-all-done.1.qd_ref, bf16[16,256,128]{2,1,0:T(8,128)(2,1)S(1)} %all-to-all-done.own_ref.kv_ref, bf16[8,2,3,256,256]{4,3,2,1,0:T(8,128)(2,1)S(1)} %get-tuple-element.15.e_ref, f32[8,8,256]{2,1,0:T(8,128)S(1)} %get-tuple-element.18.share_ref, ...), custom_call_target="tpu_custom_call" | custom-call | flops 2000000000 | bytes 4194304 | tf_op jit(solution)/shard_map/own_row/pallas_call | solution.py:449
  73.6 0.0 collective-permute-done.2.near_ref
  73.6 3.6 %collective-permute-done.3.far_ref = bf16[4112,128]{1,0:T(8,128)(2,1)S(1)} collective-permute-done((bf16[4112,128]{1,0:T(8,128)(2,1)S(1)}, bf16[4112,128]{1,0:T(8,128)(2,1)S(1)}, u32[]{:S(2)}, u32[]{:S(2)}) %collective-permute-start.3) | collective-permute-done | bytes 1052704 | tf_op jit(solution)/shard_map/ppermute | solution.py:488
  77.3 0.5 add_parts.1
  77.7 26.3 %all_to_all.15.in_ref = bf16[16,384,128]{2,1,0:T(8,128)(2,1)S(1)} all-to-all(bf16[16,384,128]{2,1,0:T(8,128)(2,1)S(1)} %add_parts.1), channel_id=1, replica_groups=mesh['head'=8,'frame'=2,'row'=16] {'frame','head'}, dimensions={0} | all-to-all | bytes 3145728 | tf_op jit(solution)/shard_map/all_to_all | solution.py:469
  104.0 1.5 %unpack_grads.1 = (bf16[128,2048]{1,0:T(8,128)(2,1)}, bf16[128,2048]{1,0:T(8,128)(2,1)}, bf16[128,2048]{1,0:T(8,128)(2,1)}) custom-call(bf16[16,384,128]{2,1,0:T(8,128)(2,1)S(1)} %all_to_all.15.in_ref), custom_call_target="tpu_custom_call" | custom-call | bytes 3145728 | tf_op jit(solution)/shard_map/unpack_grads/pallas_call | solution.py:139
  (3 shorter events, 0.0 us)
Async XLA Ops:
  3.0 7.0 %copy-start = (bf16[128,2048]{1,0:T(8,128)(2,1)S(1)}, bf16[128,2048]{1,0:T(8,128)(2,1)}, u32[]{:S(2)}) copy-start(bf16[128,2048]{1,0:T(8,128)(2,1)} %q_ref.1) | copy-start | bytes 1572868
  3.0 7.0 %copy-start.1 = (bf16[128,2048]{1,0:T(8,128)(2,1)S(1)}, bf16[128,2048]{1,0:T(8,128)(2,1)}, u32[]{:S(2)}) copy-start(bf16[128,2048]{1,0:T(8,128)(2,1)} %g_ref.1) | copy-start | bytes 1572868
  3.0 7.0 %copy-start.2 = (bf16[128,2048]{1,0:T(8,128)(2,1)S(1)}, bf16[128,2048]{1,0:T(8,128)(2,1)}, u32[]{:S(2)}) copy-start(bf16[128,2048]{1,0:T(8,128)(2,1)} %o_ref.1) | copy-start | bytes 1572868
  3.0 7.0 %copy-start.3 = (s32[8,256]{1,0:T(8,128)S(1)}, s32[8,256]{1,0:T(8,128)}, u32[]{:S(2)}) copy-start(s32[8,256]{1,0:T(8,128)} %m_ref.1) | copy-start | bytes 24580
  3.0 21.6 %all-to-all-start = ((bf16[16,256,128]{2,1,0:T(8,128)(2,1)}), bf16[16,256,128]{2,1,0:T(8,128)(2,1)S(1)}, u32[]{:S(2)}, u32[]{:S(2)}) async-start(bf16[16,256,128]{2,1,0:T(8,128)(2,1)} %pack_keys_values.1), calls=%async_computation | async-start | bytes 2097152 | tf_op jit(solution)/shard_map/all_to_all | solution.py:469
  24.6 20.2 %all-to-all-start.1 = ((bf16[16,272,128]{2,1,0:T(8,128)(2,1)}), bf16[16,272,128]{2,1,0:T(8,128)(2,1)S(1)}, u32[]{:S(2)}, u32[]{:S(2)}) async-start(bf16[16,272,128]{2,1,0:T(8,128)(2,1)} %pack_queries.1), calls=%async_computation.1 | async-start | bytes 2228224 | tf_op jit(solution)/shard_map/all_to_all | solution.py:469
  30.2 14.6 %collective-permute-start = (bf16[16,256,128]{2,1,0:T(8,128)(2,1)S(1)}, bf16[16,256,128]{2,1,0:T(8,128)(2,1)S(1)}, u32[]{:S(2)}, u32[]{:S(2)}) collective-permute-start(bf16[16,256,128]{2,1,0:T(8,128)(2,1)S(1)} %all-to-all-done.own_ref.kv_ref), channel_id=1, source_target_pairs={{0,1},{1,0},{2,3},{3,2},{4,5},{5,4},{6,7},{7,6},{8,9},{9,8},{10,11... | collective-permute-start | bytes 3145736 | tf_op jit(solution)/shard_map/ppermute | solution.py:477
  32.2 17.8 %collective-permute-start.1 = (bf16[16,256,128]{2,1,0:T(8,128)(2,1)S(1)}, bf16[16,256,128]{2,1,0:T(8,128)(2,1)}, u32[]{:S(2)}, u32[]{:S(2)}) collective-permute-start(bf16[16,256,128]{2,1,0:T(8,128)(2,1)S(1)} %all-to-all-done.own_ref.kv_ref), channel_id=1, source_target_pairs={{1,2},{3,4},{5,6},{7,8},{9,10},{11,12},{13,14},{2,1},{4,3},{6,5},{... | collective-permute-start | bytes 3145736 | tf_op jit(solution)/shard_map/ppermute | solution.py:476
  56.7 20.6 %collective-permute-start.3 = (bf16[4112,128]{1,0:T(8,128)(2,1)S(1)}, bf16[4112,128]{1,0:T(8,128)(2,1)S(1)}, u32[]{:S(2)}, u32[]{:S(2)}) collective-permute-start(bf16[4112,128]{1,0:T(8,128)(2,1)S(1)} %get-tuple-element.22), channel_id=1, source_target_pairs={{1,2},{3,4},{5,6},{7,8},{9,10},{11,12},{13,14},{2,1},{4,3},{6,5},{... | collective-permute-start | bytes 3158024 | tf_op jit(solution)/shard_map/ppermute | solution.py:488
  68.9 4.8 %collective-permute-start.2 = (bf16[16,256,128]{2,1,0:T(8,128)(2,1)S(1)}, bf16[16,256,128]{2,1,0:T(8,128)(2,1)S(1)}, u32[]{:S(2)}, u32[]{:S(2)}) collective-permute-start(bf16[16,256,128]{2,1,0:T(8,128)(2,1)S(1)} %get-tuple-element.21), channel_id=1, source_target_pairs={{0,1},{1,0},{2,3},{3,2},{4,5},{5,4},{6,7},{7,6},{8,9},{9,8},{10,11... | collective-permute-start | bytes 3145736 | tf_op jit(solution)/shard_map/ppermute | solution.py:490

commit v4 on v3

--- a/solution.py
+++ b/solution.py
@@ -14,7 +14,7 @@
 ROWS = 16
 FRAMES = 2
 GROUP = FRAMES * COLS
-EXTRA = 16
+EXTRA = 8
 NEAR_FLOPS = 2 * 10**9
 OWN_FLOPS = 2 * 10**9
 SECOND = 2 * TILE + EXTRA
@@ -43,18 +43,17 @@
 CHUNKS = 4
 
 
-def pack_first_kernel(k_ref, v_ref, out_ref, buf_ref, in_sem, out_sem):
-    wide = HEADS // CHUNKS * DIM
+def pack_first_kernel(k_ref, v_ref, out_ref, flat_ref, packed_ref, in_sem, out_sem):
+    rows_in = TILE // CHUNKS
     refs = (k_ref, v_ref)
 
     def fetch(part, i):
-        cols = pl.ds(i * wide, wide)
-        return pltpu.make_async_copy(refs[part].at[:, cols], buf_ref.at[part, :, cols], in_sem.at[part, i])
-
-    def send(part, h):
-        return pltpu.make_async_copy(
-            buf_ref.at[part, :, pl.ds(h * DIM, DIM)], out_ref.at[h, pl.ds(part * TILE, TILE), :], out_sem.at[part, h]
-        )
+        rows = pl.ds(i * rows_in, rows_in)
+        return pltpu.make_async_copy(refs[part].at[rows, :], flat_ref.at[part, rows, :], in_sem.at[part, i])
+
+    def send(part, i):
+        rows = pl.ds(part * TILE + i * rows_in, rows_in)
+        return pltpu.make_async_copy(packed_ref.at[:, rows, :], out_ref.at[:, rows, :], out_sem.at[part, i])
 
     for i in range(CHUNKS):
         for part in range(2):
@@ -62,11 +61,14 @@
     for i in range(CHUNKS):
         for part in range(2):
             fetch(part, i).wait()
-            for h in range(i * HEADS // CHUNKS, (i + 1) * HEADS // CHUNKS):
-                send(part, h).start()
-    for h in range(HEADS):
+            for h in range(HEADS):
+                packed_ref[h, part * TILE + i * rows_in : part * TILE + (i + 1) * rows_in, :] = flat_ref[
+                    part, i * rows_in : (i + 1) * rows_in, h * DIM : (h + 1) * DIM
+                ]
+            send(part, i).start()
+    for i in range(CHUNKS):
         for part in range(2):
-            send(part, h).wait()
+            send(part, i).wait()
 
 
 def pack_first(keys, values):
@@ -77,8 +79,9 @@
         out_shape=jax.ShapeDtypeStruct((HEADS, 2 * TILE, DIM), BF16),
         scratch_shapes=[
             pltpu.VMEM((2, TILE, HEADS * DIM), BF16),
+            pltpu.VMEM((HEADS, 2 * TILE, DIM), BF16),
             pltpu.SemaphoreType.DMA((2, CHUNKS)),
-            pltpu.SemaphoreType.DMA((2, HEADS)),
+            pltpu.SemaphoreType.DMA((2, CHUNKS)),
         ],
         compiler_params=pltpu.CompilerParams(vmem_limit_bytes=58 * 1024 * 1024),
         cost_estimate=pl.CostEstimate(flops=0, bytes_accessed=2**21, transcendentals=0),
@@ -118,20 +121,24 @@
     )(w, q, g, o, mask)
 
 
-def unpack_kernel(in_ref, q_ref, k_ref, v_ref, sem):
+def unpack_kernel(in_ref, q_ref, k_ref, v_ref, flat_ref, sem):
+    rows_out = TILE // CHUNKS
     refs = (q_ref, k_ref, v_ref)
 
-    def move(part, h):
-        return pltpu.make_async_copy(
-            in_ref.at[h, pl.ds(part * TILE, TILE), :], refs[part].at[:, pl.ds(h * DIM, DIM)], sem.at[part, h]
-        )
-
-    for h in range(HEADS):
-        for part in range(3):
-            move(part, h).start()
-    for h in range(HEADS):
-        for part in range(3):
-            move(part, h).wait()
+    def send(part, i):
+        rows = pl.ds(i * rows_out, rows_out)
+        return pltpu.make_async_copy(flat_ref.at[part, rows, :], refs[part].at[rows, :], sem.at[part, i])
+
+    for part in range(3):
+        for i in range(CHUNKS):
+            for h in range(HEADS):
+                flat_ref[part, i * rows_out : (i + 1) * rows_out, h * DIM : (h + 1) * DIM] = in_ref[
+                    h, part * TILE + i * rows_out : part * TILE + (i + 1) * rows_out, :
+                ]
+            send(part, i).start()
+    for part in range(3):
+        for i in range(CHUNKS):
+            send(part, i).wait()
 
 
 def unpack(x):
@@ -141,7 +148,7 @@
         in_specs=[VM],
         out_specs=[ANY] * 3,
         out_shape=[out] * 3,
-        scratch_shapes=[pltpu.SemaphoreType.DMA((3, HEADS))],
+        scratch_shapes=[pltpu.VMEM((3, TILE, HEADS * DIM), BF16), pltpu.SemaphoreType.DMA((3, CHUNKS))],
         compiler_params=small(),
         cost_estimate=pl.CostEstimate(flops=0, bytes_accessed=3 * 2**20, transcendentals=0),
         name="unpack_grads",

time: 106 us -> 105 us (level)
  no operation moved by 1% of the time
where the time goes in v4:
time: 105 us
  starting transfers between devices  27.3 us (26%)
  Pallas kernels  26.4 us (25%)
  blocking collectives  26.3 us (25%)
  waiting for transfers between devices  23.7 us (23%)
    all_to_all x1, blocking collectives, exchange(): return lax.all_to_all(x, group, split_axis=0, concat_axis=0, tiled=True)  26.3 us
    all_to_all x2, waiting for transfers between devices, exchange(): return lax.all_to_all(x, group, split_axis=0, concat_axis=0, tiled=True)  20.1 us
    all_to_all x2, starting transfers between devices, exchange(): return lax.all_to_all(x, group, split_axis=0, concat_axis=0, tiled=True)  12.5 us
    ppermute x1, starting transfers between devices, per_device(): far_back = lax.ppermute(far_part, 'row', link_swap)  8.08 us
    pallas_call x1, Pallas kernels, far_row(): pl.pallas_call(far_kernel, in_specs=[SMEM, SMEM, VM, VM, VM, VM], out_spe...  6.68 us
    pallas_call x1, Pallas kernels, early(): pl.pallas_call(early_kernel, in_specs=[SMEM, SMEM, VM, VM, VM], out_specs...  5.08 us
    ppermute x1, starting transfers between devices, per_device(): far = lax.ppermute(own, 'row', link_swap)  4.66 us
    pallas_call x1, Pallas kernels, own_row(): pl.pallas_call(own_kernel, in_specs=[VM] * 5, out_specs=VM, out_shape=jax...  4.64 us
  transfers between devices with their start and end apart: 6, of which 3 were waited for; matrix products, arithmetic and copies ran while one was open for 0% of the time, Pallas kernels for 15%

profile of v4, /device:TPU:97, one launch (start us, length us, event | category | flops | bytes accessed | tf_op | source)
XLA Modules:
  0.0 104.7 jit_solution(5726484482908692068)
XLA Ops:
  0.6 2.2 %pack_keys_values.1 = bf16[16,256,128]{2,1,0:T(8,128)(2,1)} custom-call(bf16[128,2048]{1,0:T(8,128)(2,1)} %k_ref.1, bf16[128,2048]{1,0:T(8,128)(2,1)} %v_ref.1), custom_call_target="tpu_custom_call" | custom-call | bytes 2097152 | tf_op jit(solution)/shard_map/pack_keys_values/pallas_call | solution.py:75
  2.8 0.0 copy-start
  2.8 0.0 copy-start.1
  2.8 0.0 copy-start.2
  2.8 0.0 copy-start.3
  2.9 6.9 %all-to-all-start = ((bf16[16,256,128]{2,1,0:T(8,128)(2,1)}), bf16[16,256,128]{2,1,0:T(8,128)(2,1)S(1)}, u32[]{:S(2)}, u32[]{:S(2)}) async-start(bf16[16,256,128]{2,1,0:T(8,128)(2,1)} %pack_keys_values.1), calls=%async_computation | async-start | bytes 2097152 | tf_op jit(solution)/shard_map/all_to_all | solution.py:476
  9.8 0.0 copy-done
  9.8 0.0 copy-done.1
  9.8 0.0 copy-done.2
  9.8 0.0 copy-done.3
  9.8 2.0 %pack_queries.1 = bf16[16,264,128]{2,1,0:T(8,128)(2,1)} custom-call(s32[1]{0:T(128)} %bitcast.w_ref, bf16[128,2048]{1,0:T(8,128)(2,1)S(1)} %copy-done, bf16[128,2048]{1,0:T(8,128)(2,1)S(1)} %copy-done.1, bf16[128,2048]{1,0:T(8,128)(2,1)S(1)} %copy-done.2, s32[8,256]{1,0:T(8,128)S(1)} %copy-done.3), custom_call_target="tpu_custom_call" | custom-call | flops 1048576 | bytes 2621440 | tf_op jit(solution)/shard_map/pack_queries/pallas_call | solution.py:112
  11.8 12.6 %all-to-all-done.own_ref.kv_ref = bf16[16,256,128]{2,1,0:T(8,128)(2,1)S(1)} async-done(((bf16[16,256,128]{2,1,0:T(8,128)(2,1)}), bf16[16,256,128]{2,1,0:T(8,128)(2,1)S(1)}, u32[]{:S(2)}, u32[]{:S(2)}) %all-to-all-start) | async-done | bytes 1048608 | tf_op jit(solution)/shard_map/all_to_all | solution.py:476
  24.5 5.6 %all-to-all-start.1 = ((bf16[16,264,128]{2,1,0:T(8,128)(2,1)}), bf16[16,264,128]{2,1,0:T(8,128)(2,1)S(1)}, u32[]{:S(2)}, u32[]{:S(2)}) async-start(bf16[16,264,128]{2,1,0:T(8,128)(2,1)} %pack_queries.1), calls=%async_computation.1 | async-start | bytes 2162688 | tf_op jit(solution)/shard_map/all_to_all | solution.py:476
  30.1 2.0 %collective-permute-start = (bf16[16,256,128]{2,1,0:T(8,128)(2,1)S(1)}, bf16[16,256,128]{2,1,0:T(8,128)(2,1)S(1)}, u32[]{:S(2)}, u32[]{:S(2)}) collective-permute-start(bf16[16,256,128]{2,1,0:T(8,128)(2,1)S(1)} %all-to-all-done.own_ref.kv_ref), channel_id=1, source_target_pairs={{0,1},{1,0},{2,3},{3,2},{4,5},{5,4},{6,7},{7,6},{8,9},{9,8},{10,11... | collective-permute-start | bytes 3145736 | tf_op jit(solution)/shard_map/ppermute | solution.py:484
  32.0 4.7 %collective-permute-start.1 = (bf16[16,256,128]{2,1,0:T(8,128)(2,1)S(1)}, bf16[16,256,128]{2,1,0:T(8,128)(2,1)}, u32[]{:S(2)}, u32[]{:S(2)}) collective-permute-start(bf16[16,256,128]{2,1,0:T(8,128)(2,1)S(1)} %all-to-all-done.own_ref.kv_ref), channel_id=1, source_target_pairs={{1,2},{3,4},{5,6},{7,8},{9,10},{11,12},{13,14},{2,1},{4,3},{6,5},{... | collective-permute-start | bytes 3145736 | tf_op jit(solution)/shard_map/ppermute | solution.py:483
  36.7 0.1 broadcast_clamp_fusion
  36.8 0.1 pad_add_fusion.1.rows_ref
  36.9 7.5 %all-to-all-done.1.qd_ref = bf16[16,264,128]{2,1,0:T(8,128)(2,1)S(1)} async-done(((bf16[16,264,128]{2,1,0:T(8,128)(2,1)}), bf16[16,264,128]{2,1,0:T(8,128)(2,1)S(1)}, u32[]{:S(2)}, u32[]{:S(2)}) %all-to-all-start.1) | async-done | bytes 1081376 | tf_op jit(solution)/shard_map/all_to_all | solution.py:476
  44.4 0.0 collective-permute-done.near_ref.kv_ref
  44.4 5.1 %near_and_own_scores.1 = (bf16[8,2,3,256,256]{4,3,2,1,0:T(8,128)(2,1)S(1)}, f32[8,8,256]{2,1,0:T(8,128)S(1)}, f32[8,8,256]{2,1,0:T(8,128)S(1)}) custom-call(s32[6]{0:T(128)S(1)} %pad_add_fusion.1.rows_ref, s32[16,256]{1,0:T(8,128)S(1)} %bitcast.8, bf16[16,264,128]{2,1,0:T(8,128)(2,1)S(1)} %all-to-all-done.1.qd_ref, ...), custom_call_target="tpu_custom_call" | custom-call | flops 2000000000 | bytes 3145728 | tf_op jit(solution)/shard_map/near_and_own_scores/pallas_call | solution.py:414
  49.5 0.0 collective-permute-done.1.far_ref
  49.5 6.7 %far_row.1 = (bf16[4104,128]{1,0:T(8,128)(2,1)S(1)}, f32[8,8,256]{2,1,0:T(8,128)S(1)}, f32[8,128,256]{2,1,0:T(8,128)S(1)}) custom-call(s32[6]{0:T(128)S(1)} %pad_add_fusion.1.rows_ref, s32[16,256]{1,0:T(8,128)S(1)} %bitcast.9, bf16[16,264,128]{2,1,0:T(8,128)(2,1)S(1)} %all-to-all-done.1.qd_ref, bf16[16,256,128]{2,1,0:T(8,128)(2,1)} %collective-permute-done.1.far_ref, ...), custom_call_target="tpu_custom_call" | custom-call | flops 2000000000 | bytes 4194304 | tf_op jit(solution)/shard_map/far_row/pallas_call | solution.py:427
  56.2 8.1 %collective-permute-start.3 = (bf16[4104,128]{1,0:T(8,128)(2,1)S(1)}, bf16[4104,128]{1,0:T(8,128)(2,1)S(1)}, u32[]{:S(2)}, u32[]{:S(2)}) collective-permute-start(bf16[4104,128]{1,0:T(8,128)(2,1)S(1)} %get-tuple-element.22), channel_id=1, source_target_pairs={{1,2},{3,4},{5,6},{7,8},{9,10},{11,12},{13,14},{2,1},{4,3},{6,5},{... | collective-permute-start | bytes 3151880 | tf_op jit(solution)/shard_map/ppermute | solution.py:495
  64.2 4.1 %near_row.1 = (bf16[16,256,128]{2,1,0:T(8,128)(2,1)S(1)}, f32[8,128,256]{2,1,0:T(8,128)S(1)}) custom-call(bf16[16,264,128]{2,1,0:T(8,128)(2,1)S(1)} %all-to-all-done.1.qd_ref, bf16[16,256,128]{2,1,0:T(8,128)(2,1)S(1)} %collective-permute-done.near_ref.kv_ref, bf16[8,2,3,256,256]{4,3,2,1,0:T(8,128)(2,1)S(1)} %get-tuple-element.15.e_ref, ...), custom_call_target="tpu_custom_call" | custom-call | flops 2000000000 | bytes 4194304 | tf_op jit(solution)/shard_map/near_row/pallas_call | solution.py:443
  68.4 0.1 collective-permute-start.2
  68.5 4.6 %own_row.1.mine_ref = bf16[16,384,128]{2,1,0:T(8,128)(2,1)S(1)} custom-call(bf16[16,264,128]{2,1,0:T(8,128)(2,1)S(1)} %all-to-all-done.1.qd_ref, bf16[16,256,128]{2,1,0:T(8,128)(2,1)S(1)} %all-to-all-done.own_ref.kv_ref, bf16[8,2,3,256,256]{4,3,2,1,0:T(8,128)(2,1)S(1)} %get-tuple-element.15.e_ref, f32[8,8,256]{2,1,0:T(8,128)S(1)} %get-tuple-element.18.share_ref, ...), custom_call_target="tpu_custom_call" | custom-call | flops 2000000000 | bytes 4194304 | tf_op jit(solution)/shard_map/own_row/pallas_call | solution.py:456
  73.1 0.0 collective-permute-done.2.near_ref
  73.1 3.6 %collective-permute-done.3.far_ref = bf16[4104,128]{1,0:T(8,128)(2,1)S(1)} collective-permute-done((bf16[4104,128]{1,0:T(8,128)(2,1)S(1)}, bf16[4104,128]{1,0:T(8,128)(2,1)S(1)}, u32[]{:S(2)}, u32[]{:S(2)}) %collective-permute-start.3) | collective-permute-done | bytes 1050656 | tf_op jit(solution)/shard_map/ppermute | solution.py:495
  76.7 0.5 add_parts.1
  77.2 26.3 %all_to_all.15.in_ref = bf16[16,384,128]{2,1,0:T(8,128)(2,1)S(1)} all-to-all(bf16[16,384,128]{2,1,0:T(8,128)(2,1)S(1)} %add_parts.1), channel_id=1, replica_groups=mesh['head'=8,'frame'=2,'row'=16] {'frame','head'}, dimensions={0} | all-to-all | bytes 3145728 | tf_op jit(solution)/shard_map/all_to_all | solution.py:476
  103.5 1.3 %unpack_grads.1 = (bf16[128,2048]{1,0:T(8,128)(2,1)}, bf16[128,2048]{1,0:T(8,128)(2,1)}, bf16[128,2048]{1,0:T(8,128)(2,1)}) custom-call(bf16[16,384,128]{2,1,0:T(8,128)(2,1)S(1)} %all_to_all.15.in_ref), custom_call_target="tpu_custom_call" | custom-call | bytes 3145728 | tf_op jit(solution)/shard_map/unpack_grads/pallas_call | solution.py:146
  (3 shorter events, 0.0 us)
Async XLA Ops:
  2.8 7.0 %copy-start = (bf16[128,2048]{1,0:T(8,128)(2,1)S(1)}, bf16[128,2048]{1,0:T(8,128)(2,1)}, u32[]{:S(2)}) copy-start(bf16[128,2048]{1,0:T(8,128)(2,1)} %q_ref.1) | copy-start | bytes 1572868
  2.8 7.0 %copy-start.1 = (bf16[128,2048]{1,0:T(8,128)(2,1)S(1)}, bf16[128,2048]{1,0:T(8,128)(2,1)}, u32[]{:S(2)}) copy-start(bf16[128,2048]{1,0:T(8,128)(2,1)} %g_ref.1) | copy-start | bytes 1572868
  2.8 7.0 %copy-start.2 = (bf16[128,2048]{1,0:T(8,128)(2,1)S(1)}, bf16[128,2048]{1,0:T(8,128)(2,1)}, u32[]{:S(2)}) copy-start(bf16[128,2048]{1,0:T(8,128)(2,1)} %o_ref.1) | copy-start | bytes 1572868
  2.8 7.0 %copy-start.3 = (s32[8,256]{1,0:T(8,128)S(1)}, s32[8,256]{1,0:T(8,128)}, u32[]{:S(2)}) copy-start(s32[8,256]{1,0:T(8,128)} %m_ref.1) | copy-start | bytes 24580
  2.9 21.6 %all-to-all-start = ((bf16[16,256,128]{2,1,0:T(8,128)(2,1)}), bf16[16,256,128]{2,1,0:T(8,128)(2,1)S(1)}, u32[]{:S(2)}, u32[]{:S(2)}) async-start(bf16[16,256,128]{2,1,0:T(8,128)(2,1)} %pack_keys_values.1), calls=%async_computation | async-start | bytes 2097152 | tf_op jit(solution)/shard_map/all_to_all | solution.py:476
  24.5 19.9 %all-to-all-start.1 = ((bf16[16,264,128]{2,1,0:T(8,128)(2,1)}), bf16[16,264,128]{2,1,0:T(8,128)(2,1)S(1)}, u32[]{:S(2)}, u32[]{:S(2)}) async-start(bf16[16,264,128]{2,1,0:T(8,128)(2,1)} %pack_queries.1), calls=%async_computation.1 | async-start | bytes 2162688 | tf_op jit(solution)/shard_map/all_to_all | solution.py:476
  30.1 14.3 %collective-permute-start = (bf16[16,256,128]{2,1,0:T(8,128)(2,1)S(1)}, bf16[16,256,128]{2,1,0:T(8,128)(2,1)S(1)}, u32[]{:S(2)}, u32[]{:S(2)}) collective-permute-start(bf16[16,256,128]{2,1,0:T(8,128)(2,1)S(1)} %all-to-all-done.own_ref.kv_ref), channel_id=1, source_target_pairs={{0,1},{1,0},{2,3},{3,2},{4,5},{5,4},{6,7},{7,6},{8,9},{9,8},{10,11... | collective-permute-start | bytes 3145736 | tf_op jit(solution)/shard_map/ppermute | solution.py:484
  32.0 17.4 %collective-permute-start.1 = (bf16[16,256,128]{2,1,0:T(8,128)(2,1)S(1)}, bf16[16,256,128]{2,1,0:T(8,128)(2,1)}, u32[]{:S(2)}, u32[]{:S(2)}) collective-permute-start(bf16[16,256,128]{2,1,0:T(8,128)(2,1)S(1)} %all-to-all-done.own_ref.kv_ref), channel_id=1, source_target_pairs={{1,2},{3,4},{5,6},{7,8},{9,10},{11,12},{13,14},{2,1},{4,3},{6,5},{... | collective-permute-start | bytes 3145736 | tf_op jit(solution)/shard_map/ppermute | solution.py:483
  56.2 20.6 %collective-permute-start.3 = (bf16[4104,128]{1,0:T(8,128)(2,1)S(1)}, bf16[4104,128]{1,0:T(8,128)(2,1)S(1)}, u32[]{:S(2)}, u32[]{:S(2)}) collective-permute-start(bf16[4104,128]{1,0:T(8,128)(2,1)S(1)} %get-tuple-element.22), channel_id=1, source_target_pairs={{1,2},{3,4},{5,6},{7,8},{9,10},{11,12},{13,14},{2,1},{4,3},{6,5},{... | collective-permute-start | bytes 3151880 | tf_op jit(solution)/shard_map/ppermute | solution.py:495
  68.4 4.8 %collective-permute-start.2 = (bf16[16,256,128]{2,1,0:T(8,128)(2,1)S(1)}, bf16[16,256,128]{2,1,0:T(8,128)(2,1)S(1)}, u32[]{:S(2)}, u32[]{:S(2)}) collective-permute-start(bf16[16,256,128]{2,1,0:T(8,128)(2,1)S(1)} %get-tuple-element.21), channel_id=1, source_target_pairs={{0,1},{1,0},{2,3},{3,2},{4,5},{5,4},{6,7},{7,6},{8,9},{9,8},{10,11... | collective-permute-start | bytes 3145736 | tf_op jit(solution)/shard_map/ppermute | solution.py:497

commit v5 on v4

--- a/solution.py
+++ b/solution.py
@@ -236,13 +236,18 @@
     return e.reshape(TILE, 2 * TILE), jnp.sum(e, axis=0)
 
 
-def score(rows_ref, m_ref, unit, kv_ref, q, w, s_ref, top):
+def score(rows_ref, m_ref, unit, kv_ref, q, w, s_ref, top, wide):
     cols = [jnp.clip(w + place - 1, 0, COLS - 1) for place in range(3)]
-    scores = dot_nt(jnp.concatenate([both(kv_ref, col, 0) for col in cols], axis=0), q)
+    keys = [both(kv_ref, col, 0) for col in cols]
+    if wide:
+        scores = dot_nt(jnp.concatenate(keys, axis=0), q)
+        scores = [scores[2 * TILE * place : 2 * TILE * (place + 1)] for place in range(3)]
+    else:
+        scores = [dot_nt(key, q) for key in keys]
     for place in range(3):
         pens = penalties(rows_ref, m_ref, unit, w, place)
         for frame in range(FRAMES):
-            piece = scores[(FRAMES * place + frame) * TILE : (FRAMES * place + frame + 1) * TILE]
+            piece = scores[place][frame * TILE : (frame + 1) * TILE]
             s_ref[place, frame * TILE : (frame + 1) * TILE, :] = piece
             top = jnp.maximum(top, shifted(fold(piece, jnp.max), pens[frame], -1.0))
     return top
@@ -300,7 +305,7 @@
         q = both(qd_ref, w, 0)
         top = jnp.full((8, 2 * TILE), -BIG, F32)
         for unit, kv_ref in enumerate((near_ref, own_ref)):
-            top = score(rows_ref, m_ref, unit, kv_ref, q, w, s_ref.at[unit], top)
+            top = score(rows_ref, m_ref, unit, kv_ref, q, w, s_ref.at[unit], top, True)
         peak_ref[w] = spread(jnp.max(top, axis=0, keepdims=True))
 
     def weigh(w, s_ref):
@@ -310,10 +315,13 @@
             for place in range(3):
                 pens = penalties(rows_ref, m_ref, unit, w, place)
                 for frame in range(FRAMES):
-                    rows = slice(frame * TILE, (frame + 1) * TILE)
-                    e, part = exponentials(s_ref[unit, place, rows, :], shifted(level, pens[frame], 1.0))
-                    e_ref[w, unit, place, rows, :] = e.astype(BF16)
-                    total += part
+                    below = shifted(level, pens[frame], 1.0)
+                    for part in range(4):
+                        rows = slice(frame * TILE + part * 32, frame * TILE + part * 32 + 32)
+                        x = s_ref[unit, place, rows, :].reshape(4, 8, 2 * TILE)
+                        e = jnp.exp2(x * C - below[None])
+                        e_ref[w, unit, place, rows, :] = e.reshape(32, 2 * TILE).astype(BF16)
+                        total += (e[0] + e[1]) + (e[2] + e[3])
         total_ref[w] = spread(jnp.sum(total, axis=0, keepdims=True))
 
     def two(i, carry):
@@ -336,16 +344,19 @@
 
     def weigh(w, s_ref):
         early = peak_ref[w]
-        top = score(rows_ref, m_ref, 2, far_ref, both(qd_ref, w, 0), w, s_ref, early)
+        top = score(rows_ref, m_ref, 2, far_ref, both(qd_ref, w, 0), w, s_ref, early, False)
         peak = spread(jnp.max(top, axis=0, keepdims=True))
         total = jnp.zeros((8, 2 * TILE), F32)
         for place in range(3):
             pens = penalties(rows_ref, m_ref, 2, w, place)
             for frame in range(FRAMES):
-                rows = slice(frame * TILE, (frame + 1) * TILE)
-                e, part = exponentials(s_ref[place, rows, :], shifted(peak * C, pens[frame], 1.0))
-                s_ref[place, rows, :] = e
-                total += part
+                below = shifted(peak * C, pens[frame], 1.0)
+                for part in range(4):
+                    rows = slice(frame * TILE + part * 32, frame * TILE + part * 32 + 32)
+                    x = s_ref[place, rows, :].reshape(4, 8, 2 * TILE)
+                    e = jnp.exp2(x * C - below[None])
+                    s_ref[place, rows, :] = e.reshape(32, 2 * TILE)
+                    total += (e[0] + e[1]) + (e[2] + e[3])
         shrink = jnp.exp2((early - peak) * C)
         share = 1.0 / (jnp.sum(total, axis=0, keepdims=True) + total_ref[w] * shrink)
         share_ref[w] = shrink * share

time: 105 us -> 105 us (level)
  transfers between devices with their start and end apart: 6 -> 6, of which waited for: 3 -> 4; matrix products, arithmetic and copies ran while one was open for 0% -> 0% of each run, Pallas kernels for 15% -> 15%
where the time goes in v5:
time: 105 us
  starting transfers between devices  27.2 us (26%)
  Pallas kernels  26.3 us (25%)
  blocking collectives  26.3 us (25%)
  waiting for transfers between devices  23.8 us (23%)
    all_to_all x1, blocking collectives, exchange(): return lax.all_to_all(x, group, split_axis=0, concat_axis=0, tiled=True)  26.3 us
    all_to_all x2, waiting for transfers between devices, exchange(): return lax.all_to_all(x, group, split_axis=0, concat_axis=0, tiled=True)  20.1 us
    all_to_all x2, starting transfers between devices, exchange(): return lax.all_to_all(x, group, split_axis=0, concat_axis=0, tiled=True)  12.5 us
    ppermute x1, starting transfers between devices, per_device(): far_back = lax.ppermute(far_part, 'row', link_swap)  8.03 us
    pallas_call x1, Pallas kernels, far_row(): pl.pallas_call(far_kernel, in_specs=[SMEM, SMEM, VM, VM, VM, VM], out_spe...  6.61 us
    pallas_call x1, Pallas kernels, early(): pl.pallas_call(early_kernel, in_specs=[SMEM, SMEM, VM, VM, VM], out_specs...  4.99 us
    ppermute x1, starting transfers between devices, per_device(): far = lax.ppermute(own, 'row', link_swap)  4.66 us
    pallas_call x1, Pallas kernels, own_row(): pl.pallas_call(own_kernel, in_specs=[VM] * 5, out_specs=VM, out_shape=jax...  4.64 us
  transfers between devices with their start and end apart: 6, of which 4 were waited for; matrix products, arithmetic and copies ran while one was open for 0% of the time, Pallas kernels for 15%

profile of v5, /device:TPU:97, one launch (start us, length us, event | category | flops | bytes accessed | tf_op | source)
XLA Modules:
  0.0 104.6 jit_solution(5445430450758607575)
XLA Ops:
  0.6 2.2 %pack_keys_values.1 = bf16[16,256,128]{2,1,0:T(8,128)(2,1)} custom-call(bf16[128,2048]{1,0:T(8,128)(2,1)} %k_ref.1, bf16[128,2048]{1,0:T(8,128)(2,1)} %v_ref.1), custom_call_target="tpu_custom_call" | custom-call | bytes 2097152 | tf_op jit(solution)/shard_map/pack_keys_values/pallas_call | solution.py:75
  2.8 0.0 copy-start
  2.8 0.0 copy-start.1
  2.8 0.0 copy-start.2
  2.8 0.0 copy-start.3
  2.9 6.9 %all-to-all-start = ((bf16[16,256,128]{2,1,0:T(8,128)(2,1)}), bf16[16,256,128]{2,1,0:T(8,128)(2,1)S(1)}, u32[]{:S(2)}, u32[]{:S(2)}) async-start(bf16[16,256,128]{2,1,0:T(8,128)(2,1)} %pack_keys_values.1), calls=%async_computation | async-start | bytes 2097152 | tf_op jit(solution)/shard_map/all_to_all | solution.py:487
  9.8 0.0 copy-done
  9.8 0.0 copy-done.1
  9.8 0.0 copy-done.2
  9.8 0.0 copy-done.3
  9.8 2.0 %pack_queries.1 = bf16[16,264,128]{2,1,0:T(8,128)(2,1)} custom-call(s32[1]{0:T(128)} %bitcast.w_ref, bf16[128,2048]{1,0:T(8,128)(2,1)S(1)} %copy-done, bf16[128,2048]{1,0:T(8,128)(2,1)S(1)} %copy-done.1, bf16[128,2048]{1,0:T(8,128)(2,1)S(1)} %copy-done.2, s32[8,256]{1,0:T(8,128)S(1)} %copy-done.3), custom_call_target="tpu_custom_call" | custom-call | flops 1048576 | bytes 2621440 | tf_op jit(solution)/shard_map/pack_queries/pallas_call | solution.py:112
  11.8 12.6 %all-to-all-done.own_ref.kv_ref = bf16[16,256,128]{2,1,0:T(8,128)(2,1)S(1)} async-done(((bf16[16,256,128]{2,1,0:T(8,128)(2,1)}), bf16[16,256,128]{2,1,0:T(8,128)(2,1)S(1)}, u32[]{:S(2)}, u32[]{:S(2)}) %all-to-all-start) | async-done | bytes 1048608 | tf_op jit(solution)/shard_map/all_to_all | solution.py:487
  24.5 5.6 %all-to-all-start.1 = ((bf16[16,264,128]{2,1,0:T(8,128)(2,1)}), bf16[16,264,128]{2,1,0:T(8,128)(2,1)S(1)}, u32[]{:S(2)}, u32[]{:S(2)}) async-start(bf16[16,264,128]{2,1,0:T(8,128)(2,1)} %pack_queries.1), calls=%async_computation.1 | async-start | bytes 2162688 | tf_op jit(solution)/shard_map/all_to_all | solution.py:487
  30.1 2.0 %collective-permute-start = (bf16[16,256,128]{2,1,0:T(8,128)(2,1)S(1)}, bf16[16,256,128]{2,1,0:T(8,128)(2,1)S(1)}, u32[]{:S(2)}, u32[]{:S(2)}) collective-permute-start(bf16[16,256,128]{2,1,0:T(8,128)(2,1)S(1)} %all-to-all-done.own_ref.kv_ref), channel_id=1, source_target_pairs={{0,1},{1,0},{2,3},{3,2},{4,5},{5,4},{6,7},{7,6},{8,9},{9,8},{10,11... | collective-permute-start | bytes 3145736 | tf_op jit(solution)/shard_map/ppermute | solution.py:495
  32.0 4.7 %collective-permute-start.1 = (bf16[16,256,128]{2,1,0:T(8,128)(2,1)S(1)}, bf16[16,256,128]{2,1,0:T(8,128)(2,1)}, u32[]{:S(2)}, u32[]{:S(2)}) collective-permute-start(bf16[16,256,128]{2,1,0:T(8,128)(2,1)S(1)} %all-to-all-done.own_ref.kv_ref), channel_id=1, source_target_pairs={{1,2},{3,4},{5,6},{7,8},{9,10},{11,12},{13,14},{2,1},{4,3},{6,5},{... | collective-permute-start | bytes 3145736 | tf_op jit(solution)/shard_map/ppermute | solution.py:494
  36.7 0.1 broadcast_clamp_fusion
  36.8 0.1 pad_add_fusion.1.rows_ref
  36.9 7.5 %all-to-all-done.1.qd_ref = bf16[16,264,128]{2,1,0:T(8,128)(2,1)S(1)} async-done(((bf16[16,264,128]{2,1,0:T(8,128)(2,1)}), bf16[16,264,128]{2,1,0:T(8,128)(2,1)S(1)}, u32[]{:S(2)}, u32[]{:S(2)}) %all-to-all-start.1) | async-done | bytes 1081376 | tf_op jit(solution)/shard_map/all_to_all | solution.py:487
  44.4 0.0 collective-permute-done.near_ref.kv_ref
  44.4 5.0 %near_and_own_scores.1 = (bf16[8,2,3,256,256]{4,3,2,1,0:T(8,128)(2,1)S(1)}, f32[8,8,256]{2,1,0:T(8,128)S(1)}, f32[8,8,256]{2,1,0:T(8,128)S(1)}) custom-call(s32[6]{0:T(128)S(1)} %pad_add_fusion.1.rows_ref, s32[16,256]{1,0:T(8,128)S(1)} %bitcast.8, bf16[16,264,128]{2,1,0:T(8,128)(2,1)S(1)} %all-to-all-done.1.qd_ref, ...), custom_call_target="tpu_custom_call" | custom-call | flops 2000000000 | bytes 3145728 | tf_op jit(solution)/shard_map/near_and_own_scores/pallas_call | solution.py:425
  49.4 0.1 collective-permute-done.1.far_ref
  49.4 6.6 %far_row.1 = (bf16[4104,128]{1,0:T(8,128)(2,1)S(1)}, f32[8,8,256]{2,1,0:T(8,128)S(1)}, f32[8,128,256]{2,1,0:T(8,128)S(1)}) custom-call(s32[6]{0:T(128)S(1)} %pad_add_fusion.1.rows_ref, s32[16,256]{1,0:T(8,128)S(1)} %bitcast.9, bf16[16,264,128]{2,1,0:T(8,128)(2,1)S(1)} %all-to-all-done.1.qd_ref, bf16[16,256,128]{2,1,0:T(8,128)(2,1)} %collective-permute-done.1.far_ref, ...), custom_call_target="tpu_custom_call" | custom-call | flops 2000000000 | bytes 4194304 | tf_op jit(solution)/shard_map/far_row/pallas_call | solution.py:438
  56.1 8.0 %collective-permute-start.3 = (bf16[4104,128]{1,0:T(8,128)(2,1)S(1)}, bf16[4104,128]{1,0:T(8,128)(2,1)S(1)}, u32[]{:S(2)}, u32[]{:S(2)}) collective-permute-start(bf16[4104,128]{1,0:T(8,128)(2,1)S(1)} %get-tuple-element.22), channel_id=1, source_target_pairs={{1,2},{3,4},{5,6},{7,8},{9,10},{11,12},{13,14},{2,1},{4,3},{6,5},{... | collective-permute-start | bytes 3151880 | tf_op jit(solution)/shard_map/ppermute | solution.py:506
  64.1 4.1 %near_row.1 = (bf16[16,256,128]{2,1,0:T(8,128)(2,1)S(1)}, f32[8,128,256]{2,1,0:T(8,128)S(1)}) custom-call(bf16[16,264,128]{2,1,0:T(8,128)(2,1)S(1)} %all-to-all-done.1.qd_ref, bf16[16,256,128]{2,1,0:T(8,128)(2,1)S(1)} %collective-permute-done.near_ref.kv_ref, bf16[8,2,3,256,256]{4,3,2,1,0:T(8,128)(2,1)S(1)} %get-tuple-element.15.e_ref, ...), custom_call_target="tpu_custom_call" | custom-call | flops 2000000000 | bytes 4194304 | tf_op jit(solution)/shard_map/near_row/pallas_call | solution.py:454
  68.2 0.1 collective-permute-start.2
  68.3 4.6 %own_row.1.mine_ref = bf16[16,384,128]{2,1,0:T(8,128)(2,1)S(1)} custom-call(bf16[16,264,128]{2,1,0:T(8,128)(2,1)S(1)} %all-to-all-done.1.qd_ref, bf16[16,256,128]{2,1,0:T(8,128)(2,1)S(1)} %all-to-all-done.own_ref.kv_ref, bf16[8,2,3,256,256]{4,3,2,1,0:T(8,128)(2,1)S(1)} %get-tuple-element.15.e_ref, f32[8,8,256]{2,1,0:T(8,128)S(1)} %get-tuple-element.18.share_ref, ...), custom_call_target="tpu_custom_call" | custom-call | flops 2000000000 | bytes 4194304 | tf_op jit(solution)/shard_map/own_row/pallas_call | solution.py:467
  73.0 0.0 collective-permute-done.2.near_ref
  73.0 3.6 %collective-permute-done.3.far_ref = bf16[4104,128]{1,0:T(8,128)(2,1)S(1)} collective-permute-done((bf16[4104,128]{1,0:T(8,128)(2,1)S(1)}, bf16[4104,128]{1,0:T(8,128)(2,1)S(1)}, u32[]{:S(2)}, u32[]{:S(2)}) %collective-permute-start.3) | collective-permute-done | bytes 1050656 | tf_op jit(solution)/shard_map/ppermute | solution.py:506
  76.6 0.5 add_parts.1
  77.1 26.3 %all_to_all.15.in_ref = bf16[16,384,128]{2,1,0:T(8,128)(2,1)S(1)} all-to-all(bf16[16,384,128]{2,1,0:T(8,128)(2,1)S(1)} %add_parts.1), channel_id=1, replica_groups=mesh['head'=8,'frame'=2,'row'=16] {'frame','head'}, dimensions={0} | all-to-all | bytes 3145728 | tf_op jit(solution)/shard_map/all_to_all | solution.py:487
  103.3 1.3 %unpack_grads.1 = (bf16[128,2048]{1,0:T(8,128)(2,1)}, bf16[128,2048]{1,0:T(8,128)(2,1)}, bf16[128,2048]{1,0:T(8,128)(2,1)}) custom-call(bf16[16,384,128]{2,1,0:T(8,128)(2,1)S(1)} %all_to_all.15.in_ref), custom_call_target="tpu_custom_call" | custom-call | bytes 3145728 | tf_op jit(solution)/shard_map/unpack_grads/pallas_call | solution.py:146
  (3 shorter events, 0.0 us)
Async XLA Ops:
  2.8 7.0 %copy-start = (bf16[128,2048]{1,0:T(8,128)(2,1)S(1)}, bf16[128,2048]{1,0:T(8,128)(2,1)}, u32[]{:S(2)}) copy-start(bf16[128,2048]{1,0:T(8,128)(2,1)} %q_ref.1) | copy-start | bytes 1572868
  2.8 7.0 %copy-start.1 = (bf16[128,2048]{1,0:T(8,128)(2,1)S(1)}, bf16[128,2048]{1,0:T(8,128)(2,1)}, u32[]{:S(2)}) copy-start(bf16[128,2048]{1,0:T(8,128)(2,1)} %g_ref.1) | copy-start | bytes 1572868
  2.8 7.0 %copy-start.2 = (bf16[128,2048]{1,0:T(8,128)(2,1)S(1)}, bf16[128,2048]{1,0:T(8,128)(2,1)}, u32[]{:S(2)}) copy-start(bf16[128,2048]{1,0:T(8,128)(2,1)} %o_ref.1) | copy-start | bytes 1572868
  2.8 7.0 %copy-start.3 = (s32[8,256]{1,0:T(8,128)S(1)}, s32[8,256]{1,0:T(8,128)}, u32[]{:S(2)}) copy-start(s32[8,256]{1,0:T(8,128)} %m_ref.1) | copy-start | bytes 24580
  2.9 21.6 %all-to-all-start = ((bf16[16,256,128]{2,1,0:T(8,128)(2,1)}), bf16[16,256,128]{2,1,0:T(8,128)(2,1)S(1)}, u32[]{:S(2)}, u32[]{:S(2)}) async-start(bf16[16,256,128]{2,1,0:T(8,128)(2,1)} %pack_keys_values.1), calls=%async_computation | async-start | bytes 2097152 | tf_op jit(solution)/shard_map/all_to_all | solution.py:487
  24.5 19.9 %all-to-all-start.1 = ((bf16[16,264,128]{2,1,0:T(8,128)(2,1)}), bf16[16,264,128]{2,1,0:T(8,128)(2,1)S(1)}, u32[]{:S(2)}, u32[]{:S(2)}) async-start(bf16[16,264,128]{2,1,0:T(8,128)(2,1)} %pack_queries.1), calls=%async_computation.1 | async-start | bytes 2162688 | tf_op jit(solution)/shard_map/all_to_all | solution.py:487
  30.1 14.3 %collective-permute-start = (bf16[16,256,128]{2,1,0:T(8,128)(2,1)S(1)}, bf16[16,256,128]{2,1,0:T(8,128)(2,1)S(1)}, u32[]{:S(2)}, u32[]{:S(2)}) collective-permute-start(bf16[16,256,128]{2,1,0:T(8,128)(2,1)S(1)} %all-to-all-done.own_ref.kv_ref), channel_id=1, source_target_pairs={{0,1},{1,0},{2,3},{3,2},{4,5},{5,4},{6,7},{7,6},{8,9},{9,8},{10,11... | collective-permute-start | bytes 3145736 | tf_op jit(solution)/shard_map/ppermute | solution.py:495
  32.0 17.4 %collective-permute-start.1 = (bf16[16,256,128]{2,1,0:T(8,128)(2,1)S(1)}, bf16[16,256,128]{2,1,0:T(8,128)(2,1)}, u32[]{:S(2)}, u32[]{:S(2)}) collective-permute-start(bf16[16,256,128]{2,1,0:T(8,128)(2,1)S(1)} %all-to-all-done.own_ref.kv_ref), channel_id=1, source_target_pairs={{1,2},{3,4},{5,6},{7,8},{9,10},{11,12},{13,14},{2,1},{4,3},{6,5},{... | collective-permute-start | bytes 3145736 | tf_op jit(solution)/shard_map/ppermute | solution.py:494
  56.1 20.5 %collective-permute-start.3 = (bf16[4104,128]{1,0:T(8,128)(2,1)S(1)}, bf16[4104,128]{1,0:T(8,128)(2,1)S(1)}, u32[]{:S(2)}, u32[]{:S(2)}) collective-permute-start(bf16[4104,128]{1,0:T(8,128)(2,1)S(1)} %get-tuple-element.22), channel_id=1, source_target_pairs={{1,2},{3,4},{5,6},{7,8},{9,10},{11,12},{13,14},{2,1},{4,3},{6,5},{... | collective-permute-start | bytes 3151880 | tf_op jit(solution)/shard_map/ppermute | solution.py:506
  68.2 4.8 %collective-permute-start.2 = (bf16[16,256,128]{2,1,0:T(8,128)(2,1)S(1)}, bf16[16,256,128]{2,1,0:T(8,128)(2,1)S(1)}, u32[]{:S(2)}, u32[]{:S(2)}) collective-permute-start(bf16[16,256,128]{2,1,0:T(8,128)(2,1)S(1)} %get-tuple-element.21), channel_id=1, source_target_pairs={{0,1},{1,0},{2,3},{3,2},{4,5},{5,4},{6,7},{7,6},{8,9},{9,8},{10,11... | collective-permute-start | bytes 3145736 | tf_op jit(solution)/shard_map/ppermute | solution.py:508

commit v6 on v5

--- a/solution.py
+++ b/solution.py
@@ -40,7 +40,7 @@
 ANY = pl.BlockSpec(memory_space=pl.ANY)
 
 
-CHUNKS = 4
+CHUNKS = 2
 
 
 def pack_first_kernel(k_ref, v_ref, out_ref, flat_ref, packed_ref, in_sem, out_sem):

time: 105 us -> 105 us (level)
  no operation moved by 1% of the time
where the time goes in v6:
time: 105 us; the launch traced here: 104 us
  starting transfers between devices  27.2 us (26%)
  Pallas kernels  26.2 us (25%)
  blocking collectives  26.2 us (25%)
  waiting for transfers between devices  23.8 us (23%)
    all_to_all x1, blocking collectives, exchange(): return lax.all_to_all(x, group, split_axis=0, concat_axis=0, tiled=True)  26.2 us
    all_to_all x2, waiting for transfers between devices, exchange(): return lax.all_to_all(x, group, split_axis=0, concat_axis=0, tiled=True)  20.1 us
    all_to_all x2, starting transfers between devices, exchange(): return lax.all_to_all(x, group, split_axis=0, concat_axis=0, tiled=True)  12.5 us
    ppermute x1, starting transfers between devices, per_device(): far_back = lax.ppermute(far_part, 'row', link_swap)  8.02 us
    pallas_call x1, Pallas kernels, far_row(): pl.pallas_call(far_kernel, in_specs=[SMEM, SMEM, VM, VM, VM, VM], out_spe...  6.62 us
    pallas_call x1, Pallas kernels, early(): pl.pallas_call(early_kernel, in_specs=[SMEM, SMEM, VM, VM, VM], out_specs...  4.99 us
    ppermute x1, starting transfers between devices, per_device(): far = lax.ppermute(own, 'row', link_swap)  4.66 us
    pallas_call x1, Pallas kernels, own_row(): pl.pallas_call(own_kernel, in_specs=[VM] * 5, out_specs=VM, out_shape=jax...  4.64 us
  transfers between devices with their start and end apart: 6, of which 4 were waited for; matrix products, arithmetic and copies ran while one was open for 0% of the time, Pallas kernels for 15%

profile of v6, /device:TPU:97, one launch (start us, length us, event | category | flops | bytes accessed | tf_op | source)
XLA Modules:
  0.0 104.4 jit_solution(485136331086039349)
XLA Ops:
  0.6 2.1 %pack_keys_values.1 = bf16[16,256,128]{2,1,0:T(8,128)(2,1)} custom-call(bf16[128,2048]{1,0:T(8,128)(2,1)} %k_ref.1, bf16[128,2048]{1,0:T(8,128)(2,1)} %v_ref.1), custom_call_target="tpu_custom_call" | custom-call | bytes 2097152 | tf_op jit(solution)/shard_map/pack_keys_values/pallas_call | solution.py:75
  2.7 0.0 copy-start
  2.7 0.0 copy-start.1
  2.7 0.0 copy-start.2
  2.8 0.0 copy-start.3
  2.8 6.9 %all-to-all-start = ((bf16[16,256,128]{2,1,0:T(8,128)(2,1)}), bf16[16,256,128]{2,1,0:T(8,128)(2,1)S(1)}, u32[]{:S(2)}, u32[]{:S(2)}) async-start(bf16[16,256,128]{2,1,0:T(8,128)(2,1)} %pack_keys_values.1), calls=%async_computation | async-start | bytes 2097152 | tf_op jit(solution)/shard_map/all_to_all | solution.py:487
  9.7 0.0 copy-done
  9.7 0.0 copy-done.1
  9.7 0.0 copy-done.2
  9.7 0.0 copy-done.3
  9.7 2.0 %pack_queries.1 = bf16[16,264,128]{2,1,0:T(8,128)(2,1)} custom-call(s32[1]{0:T(128)} %bitcast.w_ref, bf16[128,2048]{1,0:T(8,128)(2,1)S(1)} %copy-done, bf16[128,2048]{1,0:T(8,128)(2,1)S(1)} %copy-done.1, bf16[128,2048]{1,0:T(8,128)(2,1)S(1)} %copy-done.2, s32[8,256]{1,0:T(8,128)S(1)} %copy-done.3), custom_call_target="tpu_custom_call" | custom-call | flops 1048576 | bytes 2621440 | tf_op jit(solution)/shard_map/pack_queries/pallas_call | solution.py:112
  11.8 12.6 %all-to-all-done.own_ref.kv_ref = bf16[16,256,128]{2,1,0:T(8,128)(2,1)S(1)} async-done(((bf16[16,256,128]{2,1,0:T(8,128)(2,1)}), bf16[16,256,128]{2,1,0:T(8,128)(2,1)S(1)}, u32[]{:S(2)}, u32[]{:S(2)}) %all-to-all-start) | async-done | bytes 1048608 | tf_op jit(solution)/shard_map/all_to_all | solution.py:487
  24.4 5.6 %all-to-all-start.1 = ((bf16[16,264,128]{2,1,0:T(8,128)(2,1)}), bf16[16,264,128]{2,1,0:T(8,128)(2,1)S(1)}, u32[]{:S(2)}, u32[]{:S(2)}) async-start(bf16[16,264,128]{2,1,0:T(8,128)(2,1)} %pack_queries.1), calls=%async_computation.1 | async-start | bytes 2162688 | tf_op jit(solution)/shard_map/all_to_all | solution.py:487
  30.0 2.0 %collective-permute-start = (bf16[16,256,128]{2,1,0:T(8,128)(2,1)S(1)}, bf16[16,256,128]{2,1,0:T(8,128)(2,1)S(1)}, u32[]{:S(2)}, u32[]{:S(2)}) collective-permute-start(bf16[16,256,128]{2,1,0:T(8,128)(2,1)S(1)} %all-to-all-done.own_ref.kv_ref), channel_id=1, source_target_pairs={{0,1},{1,0},{2,3},{3,2},{4,5},{5,4},{6,7},{7,6},{8,9},{9,8},{10,11... | collective-permute-start | bytes 3145736 | tf_op jit(solution)/shard_map/ppermute | solution.py:495
  31.9 4.7 %collective-permute-start.1 = (bf16[16,256,128]{2,1,0:T(8,128)(2,1)S(1)}, bf16[16,256,128]{2,1,0:T(8,128)(2,1)}, u32[]{:S(2)}, u32[]{:S(2)}) collective-permute-start(bf16[16,256,128]{2,1,0:T(8,128)(2,1)S(1)} %all-to-all-done.own_ref.kv_ref), channel_id=1, source_target_pairs={{1,2},{3,4},{5,6},{7,8},{9,10},{11,12},{13,14},{2,1},{4,3},{6,5},{... | collective-permute-start | bytes 3145736 | tf_op jit(solution)/shard_map/ppermute | solution.py:494
  36.6 0.1 broadcast_clamp_fusion
  36.7 0.1 pad_add_fusion.1.rows_ref
  36.8 7.5 %all-to-all-done.1.qd_ref = bf16[16,264,128]{2,1,0:T(8,128)(2,1)S(1)} async-done(((bf16[16,264,128]{2,1,0:T(8,128)(2,1)}), bf16[16,264,128]{2,1,0:T(8,128)(2,1)S(1)}, u32[]{:S(2)}, u32[]{:S(2)}) %all-to-all-start.1) | async-done | bytes 1081376 | tf_op jit(solution)/shard_map/all_to_all | solution.py:487
  44.3 0.0 collective-permute-done.near_ref.kv_ref
  44.3 5.0 %near_and_own_scores.1 = (bf16[8,2,3,256,256]{4,3,2,1,0:T(8,128)(2,1)S(1)}, f32[8,8,256]{2,1,0:T(8,128)S(1)}, f32[8,8,256]{2,1,0:T(8,128)S(1)}) custom-call(s32[6]{0:T(128)S(1)} %pad_add_fusion.1.rows_ref, s32[16,256]{1,0:T(8,128)S(1)} %bitcast.8, bf16[16,264,128]{2,1,0:T(8,128)(2,1)S(1)} %all-to-all-done.1.qd_ref, ...), custom_call_target="tpu_custom_call" | custom-call | flops 2000000000 | bytes 3145728 | tf_op jit(solution)/shard_map/near_and_own_scores/pallas_call | solution.py:425
  49.3 0.1 collective-permute-done.1.far_ref
  49.4 6.6 %far_row.1 = (bf16[4104,128]{1,0:T(8,128)(2,1)S(1)}, f32[8,8,256]{2,1,0:T(8,128)S(1)}, f32[8,128,256]{2,1,0:T(8,128)S(1)}) custom-call(s32[6]{0:T(128)S(1)} %pad_add_fusion.1.rows_ref, s32[16,256]{1,0:T(8,128)S(1)} %bitcast.9, bf16[16,264,128]{2,1,0:T(8,128)(2,1)S(1)} %all-to-all-done.1.qd_ref, bf16[16,256,128]{2,1,0:T(8,128)(2,1)} %collective-permute-done.1.far_ref, ...), custom_call_target="tpu_custom_call" | custom-call | flops 2000000000 | bytes 4194304 | tf_op jit(solution)/shard_map/far_row/pallas_call | solution.py:438
  56.0 8.0 %collective-permute-start.3 = (bf16[4104,128]{1,0:T(8,128)(2,1)S(1)}, bf16[4104,128]{1,0:T(8,128)(2,1)S(1)}, u32[]{:S(2)}, u32[]{:S(2)}) collective-permute-start(bf16[4104,128]{1,0:T(8,128)(2,1)S(1)} %get-tuple-element.22), channel_id=1, source_target_pairs={{1,2},{3,4},{5,6},{7,8},{9,10},{11,12},{13,14},{2,1},{4,3},{6,5},{... | collective-permute-start | bytes 3151880 | tf_op jit(solution)/shard_map/ppermute | solution.py:506
  64.0 4.1 %near_row.1 = (bf16[16,256,128]{2,1,0:T(8,128)(2,1)S(1)}, f32[8,128,256]{2,1,0:T(8,128)S(1)}) custom-call(bf16[16,264,128]{2,1,0:T(8,128)(2,1)S(1)} %all-to-all-done.1.qd_ref, bf16[16,256,128]{2,1,0:T(8,128)(2,1)S(1)} %collective-permute-done.near_ref.kv_ref, bf16[8,2,3,256,256]{4,3,2,1,0:T(8,128)(2,1)S(1)} %get-tuple-element.15.e_ref, ...), custom_call_target="tpu_custom_call" | custom-call | flops 2000000000 | bytes 4194304 | tf_op jit(solution)/shard_map/near_row/pallas_call | solution.py:454
  68.1 0.1 collective-permute-start.2
  68.2 4.6 %own_row.1.mine_ref = bf16[16,384,128]{2,1,0:T(8,128)(2,1)S(1)} custom-call(bf16[16,264,128]{2,1,0:T(8,128)(2,1)S(1)} %all-to-all-done.1.qd_ref, bf16[16,256,128]{2,1,0:T(8,128)(2,1)S(1)} %all-to-all-done.own_ref.kv_ref, bf16[8,2,3,256,256]{4,3,2,1,0:T(8,128)(2,1)S(1)} %get-tuple-element.15.e_ref, f32[8,8,256]{2,1,0:T(8,128)S(1)} %get-tuple-element.18.share_ref, ...), custom_call_target="tpu_custom_call" | custom-call | flops 2000000000 | bytes 4194304 | tf_op jit(solution)/shard_map/own_row/pallas_call | solution.py:467
  72.9 0.0 collective-permute-done.2.near_ref
  72.9 3.6 %collective-permute-done.3.far_ref = bf16[4104,128]{1,0:T(8,128)(2,1)S(1)} collective-permute-done((bf16[4104,128]{1,0:T(8,128)(2,1)S(1)}, bf16[4104,128]{1,0:T(8,128)(2,1)S(1)}, u32[]{:S(2)}, u32[]{:S(2)}) %collective-permute-start.3) | collective-permute-done | bytes 1050656 | tf_op jit(solution)/shard_map/ppermute | solution.py:506
  76.5 0.5 add_parts.1
  77.0 26.2 %all_to_all.15.in_ref = bf16[16,384,128]{2,1,0:T(8,128)(2,1)S(1)} all-to-all(bf16[16,384,128]{2,1,0:T(8,128)(2,1)S(1)} %add_parts.1), channel_id=1, replica_groups=mesh['head'=8,'frame'=2,'row'=16] {'frame','head'}, dimensions={0} | all-to-all | bytes 3145728 | tf_op jit(solution)/shard_map/all_to_all | solution.py:487
  103.2 1.2 %unpack_grads.1 = (bf16[128,2048]{1,0:T(8,128)(2,1)}, bf16[128,2048]{1,0:T(8,128)(2,1)}, bf16[128,2048]{1,0:T(8,128)(2,1)}) custom-call(bf16[16,384,128]{2,1,0:T(8,128)(2,1)S(1)} %all_to_all.15.in_ref), custom_call_target="tpu_custom_call" | custom-call | bytes 3145728 | tf_op jit(solution)/shard_map/unpack_grads/pallas_call | solution.py:146
  (3 shorter events, 0.0 us)
Async XLA Ops:
  2.7 7.0 %copy-start = (bf16[128,2048]{1,0:T(8,128)(2,1)S(1)}, bf16[128,2048]{1,0:T(8,128)(2,1)}, u32[]{:S(2)}) copy-start(bf16[128,2048]{1,0:T(8,128)(2,1)} %q_ref.1) | copy-start | bytes 1572868
  2.7 7.0 %copy-start.1 = (bf16[128,2048]{1,0:T(8,128)(2,1)S(1)}, bf16[128,2048]{1,0:T(8,128)(2,1)}, u32[]{:S(2)}) copy-start(bf16[128,2048]{1,0:T(8,128)(2,1)} %g_ref.1) | copy-start | bytes 1572868
  2.7 7.0 %copy-start.2 = (bf16[128,2048]{1,0:T(8,128)(2,1)S(1)}, bf16[128,2048]{1,0:T(8,128)(2,1)}, u32[]{:S(2)}) copy-start(bf16[128,2048]{1,0:T(8,128)(2,1)} %o_ref.1) | copy-start | bytes 1572868
  2.8 7.0 %copy-start.3 = (s32[8,256]{1,0:T(8,128)S(1)}, s32[8,256]{1,0:T(8,128)}, u32[]{:S(2)}) copy-start(s32[8,256]{1,0:T(8,128)} %m_ref.1) | copy-start | bytes 24580
  2.8 21.6 %all-to-all-start = ((bf16[16,256,128]{2,1,0:T(8,128)(2,1)}), bf16[16,256,128]{2,1,0:T(8,128)(2,1)S(1)}, u32[]{:S(2)}, u32[]{:S(2)}) async-start(bf16[16,256,128]{2,1,0:T(8,128)(2,1)} %pack_keys_values.1), calls=%async_computation | async-start | bytes 2097152 | tf_op jit(solution)/shard_map/all_to_all | solution.py:487
  24.4 19.9 %all-to-all-start.1 = ((bf16[16,264,128]{2,1,0:T(8,128)(2,1)}), bf16[16,264,128]{2,1,0:T(8,128)(2,1)S(1)}, u32[]{:S(2)}, u32[]{:S(2)}) async-start(bf16[16,264,128]{2,1,0:T(8,128)(2,1)} %pack_queries.1), calls=%async_computation.1 | async-start | bytes 2162688 | tf_op jit(solution)/shard_map/all_to_all | solution.py:487
  30.0 14.3 %collective-permute-start = (bf16[16,256,128]{2,1,0:T(8,128)(2,1)S(1)}, bf16[16,256,128]{2,1,0:T(8,128)(2,1)S(1)}, u32[]{:S(2)}, u32[]{:S(2)}) collective-permute-start(bf16[16,256,128]{2,1,0:T(8,128)(2,1)S(1)} %all-to-all-done.own_ref.kv_ref), channel_id=1, source_target_pairs={{0,1},{1,0},{2,3},{3,2},{4,5},{5,4},{6,7},{7,6},{8,9},{9,8},{10,11... | collective-permute-start | bytes 3145736 | tf_op jit(solution)/shard_map/ppermute | solution.py:495
  31.9 17.4 %collective-permute-start.1 = (bf16[16,256,128]{2,1,0:T(8,128)(2,1)S(1)}, bf16[16,256,128]{2,1,0:T(8,128)(2,1)}, u32[]{:S(2)}, u32[]{:S(2)}) collective-permute-start(bf16[16,256,128]{2,1,0:T(8,128)(2,1)S(1)} %all-to-all-done.own_ref.kv_ref), channel_id=1, source_target_pairs={{1,2},{3,4},{5,6},{7,8},{9,10},{11,12},{13,14},{2,1},{4,3},{6,5},{... | collective-permute-start | bytes 3145736 | tf_op jit(solution)/shard_map/ppermute | solution.py:494
  56.0 20.5 %collective-permute-start.3 = (bf16[4104,128]{1,0:T(8,128)(2,1)S(1)}, bf16[4104,128]{1,0:T(8,128)(2,1)S(1)}, u32[]{:S(2)}, u32[]{:S(2)}) collective-permute-start(bf16[4104,128]{1,0:T(8,128)(2,1)S(1)} %get-tuple-element.22), channel_id=1, source_target_pairs={{1,2},{3,4},{5,6},{7,8},{9,10},{11,12},{13,14},{2,1},{4,3},{6,5},{... | collective-permute-start | bytes 3151880 | tf_op jit(solution)/shard_map/ppermute | solution.py:506
  68.1 4.8 %collective-permute-start.2 = (bf16[16,256,128]{2,1,0:T(8,128)(2,1)S(1)}, bf16[16,256,128]{2,1,0:T(8,128)(2,1)S(1)}, u32[]{:S(2)}, u32[]{:S(2)}) collective-permute-start(bf16[16,256,128]{2,1,0:T(8,128)(2,1)S(1)} %get-tuple-element.21), channel_id=1, source_target_pairs={{0,1},{1,0},{2,3},{3,2},{4,5},{5,4},{6,7},{7,6},{8,9},{9,8},{10,11... | collective-permute-start | bytes 3145736 | tf_op jit(solution)/shard_map/ppermute | solution.py:508

commit v7 on v6

--- a/solution.py
+++ b/solution.py
@@ -164,7 +164,7 @@
 
 
 def add_parts(mine, near, far):
-    step = 4
+    step = 8
     block = pl.BlockSpec((step, 2 * TILE, DIM), lambda i: (i, 0, 0))
     wide = pl.BlockSpec((step, 3 * TILE, DIM), lambda i: (i, 0, 0))
     return pl.pallas_call(

time: 105 us -> 105 us (level)
  no operation moved by 1% of the time
where the time goes in v7:
time: 105 us; the launch traced here: 104 us
  starting transfers between devices  27.2 us (26%)
  blocking collectives  26.2 us (25%)
  Pallas kernels  26.1 us (25%)
  waiting for transfers between devices  23.8 us (23%)
    all_to_all x1, blocking collectives, exchange(): return lax.all_to_all(x, group, split_axis=0, concat_axis=0, tiled=True)  26.2 us
    all_to_all x2, waiting for transfers between devices, exchange(): return lax.all_to_all(x, group, split_axis=0, concat_axis=0, tiled=True)  20.1 us
    all_to_all x2, starting transfers between devices, exchange(): return lax.all_to_all(x, group, split_axis=0, concat_axis=0, tiled=True)  12.5 us
    ppermute x1, starting transfers between devices, per_device(): far_back = lax.ppermute(far_part, 'row', link_swap)  8.02 us
    pallas_call x1, Pallas kernels, far_row(): pl.pallas_call(far_kernel, in_specs=[SMEM, SMEM, VM, VM, VM, VM], out_spe...  6.62 us
    pallas_call x1, Pallas kernels, early(): pl.pallas_call(early_kernel, in_specs=[SMEM, SMEM, VM, VM, VM], out_specs...  4.99 us
    ppermute x1, starting transfers between devices, per_device(): far = lax.ppermute(own, 'row', link_swap)  4.66 us
    pallas_call x1, Pallas kernels, own_row(): pl.pallas_call(own_kernel, in_specs=[VM] * 5, out_specs=VM, out_shape=jax...  4.64 us
  transfers between devices with their start and end apart: 6, of which 4 were waited for; matrix products, arithmetic and copies ran while one was open for 0% of the time, Pallas kernels for 15%

profile of v7, /device:TPU:97, one launch (start us, length us, event | category | flops | bytes accessed | tf_op | source)
XLA Modules:
  0.0 104.4 jit_solution(10354861191774665136)
XLA Ops:
  0.6 2.1 %pack_keys_values.1 = bf16[16,256,128]{2,1,0:T(8,128)(2,1)} custom-call(bf16[128,2048]{1,0:T(8,128)(2,1)} %k_ref.1, bf16[128,2048]{1,0:T(8,128)(2,1)} %v_ref.1), custom_call_target="tpu_custom_call" | custom-call | bytes 2097152 | tf_op jit(solution)/shard_map/pack_keys_values/pallas_call | solution.py:75
  2.7 0.0 copy-start
  2.7 0.0 copy-start.1
  2.7 0.0 copy-start.2
  2.8 0.0 copy-start.3
  2.8 6.9 %all-to-all-start = ((bf16[16,256,128]{2,1,0:T(8,128)(2,1)}), bf16[16,256,128]{2,1,0:T(8,128)(2,1)S(1)}, u32[]{:S(2)}, u32[]{:S(2)}) async-start(bf16[16,256,128]{2,1,0:T(8,128)(2,1)} %pack_keys_values.1), calls=%async_computation | async-start | bytes 2097152 | tf_op jit(solution)/shard_map/all_to_all | solution.py:487
  9.7 0.0 copy-done
  9.7 0.0 copy-done.1
  9.7 0.0 copy-done.2
  9.7 0.0 copy-done.3
  9.7 2.0 %pack_queries.1 = bf16[16,264,128]{2,1,0:T(8,128)(2,1)} custom-call(s32[1]{0:T(128)} %bitcast.w_ref, bf16[128,2048]{1,0:T(8,128)(2,1)S(1)} %copy-done, bf16[128,2048]{1,0:T(8,128)(2,1)S(1)} %copy-done.1, bf16[128,2048]{1,0:T(8,128)(2,1)S(1)} %copy-done.2, s32[8,256]{1,0:T(8,128)S(1)} %copy-done.3), custom_call_target="tpu_custom_call" | custom-call | flops 1048576 | bytes 2621440 | tf_op jit(solution)/shard_map/pack_queries/pallas_call | solution.py:112
  11.8 12.6 %all-to-all-done.own_ref.kv_ref = bf16[16,256,128]{2,1,0:T(8,128)(2,1)S(1)} async-done(((bf16[16,256,128]{2,1,0:T(8,128)(2,1)}), bf16[16,256,128]{2,1,0:T(8,128)(2,1)S(1)}, u32[]{:S(2)}, u32[]{:S(2)}) %all-to-all-start) | async-done | bytes 1048608 | tf_op jit(solution)/shard_map/all_to_all | solution.py:487
  24.4 5.6 %all-to-all-start.1 = ((bf16[16,264,128]{2,1,0:T(8,128)(2,1)}), bf16[16,264,128]{2,1,0:T(8,128)(2,1)S(1)}, u32[]{:S(2)}, u32[]{:S(2)}) async-start(bf16[16,264,128]{2,1,0:T(8,128)(2,1)} %pack_queries.1), calls=%async_computation.1 | async-start | bytes 2162688 | tf_op jit(solution)/shard_map/all_to_all | solution.py:487
  30.0 2.0 %collective-permute-start = (bf16[16,256,128]{2,1,0:T(8,128)(2,1)S(1)}, bf16[16,256,128]{2,1,0:T(8,128)(2,1)S(1)}, u32[]{:S(2)}, u32[]{:S(2)}) collective-permute-start(bf16[16,256,128]{2,1,0:T(8,128)(2,1)S(1)} %all-to-all-done.own_ref.kv_ref), channel_id=1, source_target_pairs={{0,1},{1,0},{2,3},{3,2},{4,5},{5,4},{6,7},{7,6},{8,9},{9,8},{10,11... | collective-permute-start | bytes 3145736 | tf_op jit(solution)/shard_map/ppermute | solution.py:495
  31.9 4.7 %collective-permute-start.1 = (bf16[16,256,128]{2,1,0:T(8,128)(2,1)S(1)}, bf16[16,256,128]{2,1,0:T(8,128)(2,1)}, u32[]{:S(2)}, u32[]{:S(2)}) collective-permute-start(bf16[16,256,128]{2,1,0:T(8,128)(2,1)S(1)} %all-to-all-done.own_ref.kv_ref), channel_id=1, source_target_pairs={{1,2},{3,4},{5,6},{7,8},{9,10},{11,12},{13,14},{2,1},{4,3},{6,5},{... | collective-permute-start | bytes 3145736 | tf_op jit(solution)/shard_map/ppermute | solution.py:494
  36.6 0.1 broadcast_clamp_fusion
  36.7 0.1 pad_add_fusion.1.rows_ref
  36.8 7.5 %all-to-all-done.1.qd_ref = bf16[16,264,128]{2,1,0:T(8,128)(2,1)S(1)} async-done(((bf16[16,264,128]{2,1,0:T(8,128)(2,1)}), bf16[16,264,128]{2,1,0:T(8,128)(2,1)S(1)}, u32[]{:S(2)}, u32[]{:S(2)}) %all-to-all-start.1) | async-done | bytes 1081376 | tf_op jit(solution)/shard_map/all_to_all | solution.py:487
  44.3 0.0 collective-permute-done.near_ref.kv_ref
  44.3 5.0 %near_and_own_scores.1 = (bf16[8,2,3,256,256]{4,3,2,1,0:T(8,128)(2,1)S(1)}, f32[8,8,256]{2,1,0:T(8,128)S(1)}, f32[8,8,256]{2,1,0:T(8,128)S(1)}) custom-call(s32[6]{0:T(128)S(1)} %pad_add_fusion.1.rows_ref, s32[16,256]{1,0:T(8,128)S(1)} %bitcast.8, bf16[16,264,128]{2,1,0:T(8,128)(2,1)S(1)} %all-to-all-done.1.qd_ref, ...), custom_call_target="tpu_custom_call" | custom-call | flops 2000000000 | bytes 3145728 | tf_op jit(solution)/shard_map/near_and_own_scores/pallas_call | solution.py:425
  49.3 0.1 collective-permute-done.1.far_ref
  49.4 6.6 %far_row.1 = (bf16[4104,128]{1,0:T(8,128)(2,1)S(1)}, f32[8,8,256]{2,1,0:T(8,128)S(1)}, f32[8,128,256]{2,1,0:T(8,128)S(1)}) custom-call(s32[6]{0:T(128)S(1)} %pad_add_fusion.1.rows_ref, s32[16,256]{1,0:T(8,128)S(1)} %bitcast.9, bf16[16,264,128]{2,1,0:T(8,128)(2,1)S(1)} %all-to-all-done.1.qd_ref, bf16[16,256,128]{2,1,0:T(8,128)(2,1)} %collective-permute-done.1.far_ref, ...), custom_call_target="tpu_custom_call" | custom-call | flops 2000000000 | bytes 4194304 | tf_op jit(solution)/shard_map/far_row/pallas_call | solution.py:438
  56.0 8.0 %collective-permute-start.3 = (bf16[4104,128]{1,0:T(8,128)(2,1)S(1)}, bf16[4104,128]{1,0:T(8,128)(2,1)S(1)}, u32[]{:S(2)}, u32[]{:S(2)}) collective-permute-start(bf16[4104,128]{1,0:T(8,128)(2,1)S(1)} %get-tuple-element.22), channel_id=1, source_target_pairs={{1,2},{3,4},{5,6},{7,8},{9,10},{11,12},{13,14},{2,1},{4,3},{6,5},{... | collective-permute-start | bytes 3151880 | tf_op jit(solution)/shard_map/ppermute | solution.py:506
  64.0 4.1 %near_row.1 = (bf16[16,256,128]{2,1,0:T(8,128)(2,1)S(1)}, f32[8,128,256]{2,1,0:T(8,128)S(1)}) custom-call(bf16[16,264,128]{2,1,0:T(8,128)(2,1)S(1)} %all-to-all-done.1.qd_ref, bf16[16,256,128]{2,1,0:T(8,128)(2,1)S(1)} %collective-permute-done.near_ref.kv_ref, bf16[8,2,3,256,256]{4,3,2,1,0:T(8,128)(2,1)S(1)} %get-tuple-element.15.e_ref, ...), custom_call_target="tpu_custom_call" | custom-call | flops 2000000000 | bytes 4194304 | tf_op jit(solution)/shard_map/near_row/pallas_call | solution.py:454
  68.1 0.1 collective-permute-start.2
  68.2 4.6 %own_row.1.mine_ref = bf16[16,384,128]{2,1,0:T(8,128)(2,1)S(1)} custom-call(bf16[16,264,128]{2,1,0:T(8,128)(2,1)S(1)} %all-to-all-done.1.qd_ref, bf16[16,256,128]{2,1,0:T(8,128)(2,1)S(1)} %all-to-all-done.own_ref.kv_ref, bf16[8,2,3,256,256]{4,3,2,1,0:T(8,128)(2,1)S(1)} %get-tuple-element.15.e_ref, f32[8,8,256]{2,1,0:T(8,128)S(1)} %get-tuple-element.18.share_ref, ...), custom_call_target="tpu_custom_call" | custom-call | flops 2000000000 | bytes 4194304 | tf_op jit(solution)/shard_map/own_row/pallas_call | solution.py:467
  72.9 0.0 collective-permute-done.2.near_ref
  72.9 3.6 %collective-permute-done.3.far_ref = bf16[4104,128]{1,0:T(8,128)(2,1)S(1)} collective-permute-done((bf16[4104,128]{1,0:T(8,128)(2,1)S(1)}, bf16[4104,128]{1,0:T(8,128)(2,1)S(1)}, u32[]{:S(2)}, u32[]{:S(2)}) %collective-permute-start.3) | collective-permute-done | bytes 1050656 | tf_op jit(solution)/shard_map/ppermute | solution.py:506
  76.5 0.4 add_parts.1
  77.0 26.2 %all_to_all.15.in_ref = bf16[16,384,128]{2,1,0:T(8,128)(2,1)S(1)} all-to-all(bf16[16,384,128]{2,1,0:T(8,128)(2,1)S(1)} %add_parts.1), channel_id=1, replica_groups=mesh['head'=8,'frame'=2,'row'=16] {'frame','head'}, dimensions={0} | all-to-all | bytes 3145728 | tf_op jit(solution)/shard_map/all_to_all | solution.py:487
  103.2 1.2 %unpack_grads.1 = (bf16[128,2048]{1,0:T(8,128)(2,1)}, bf16[128,2048]{1,0:T(8,128)(2,1)}, bf16[128,2048]{1,0:T(8,128)(2,1)}) custom-call(bf16[16,384,128]{2,1,0:T(8,128)(2,1)S(1)} %all_to_all.15.in_ref), custom_call_target="tpu_custom_call" | custom-call | bytes 3145728 | tf_op jit(solution)/shard_map/unpack_grads/pallas_call | solution.py:146
  (3 shorter events, 0.0 us)
Async XLA Ops:
  2.7 7.0 %copy-start = (bf16[128,2048]{1,0:T(8,128)(2,1)S(1)}, bf16[128,2048]{1,0:T(8,128)(2,1)}, u32[]{:S(2)}) copy-start(bf16[128,2048]{1,0:T(8,128)(2,1)} %q_ref.1) | copy-start | bytes 1572868
  2.7 7.0 %copy-start.1 = (bf16[128,2048]{1,0:T(8,128)(2,1)S(1)}, bf16[128,2048]{1,0:T(8,128)(2,1)}, u32[]{:S(2)}) copy-start(bf16[128,2048]{1,0:T(8,128)(2,1)} %g_ref.1) | copy-start | bytes 1572868
  2.7 7.0 %copy-start.2 = (bf16[128,2048]{1,0:T(8,128)(2,1)S(1)}, bf16[128,2048]{1,0:T(8,128)(2,1)}, u32[]{:S(2)}) copy-start(bf16[128,2048]{1,0:T(8,128)(2,1)} %o_ref.1) | copy-start | bytes 1572868
  2.8 7.0 %copy-start.3 = (s32[8,256]{1,0:T(8,128)S(1)}, s32[8,256]{1,0:T(8,128)}, u32[]{:S(2)}) copy-start(s32[8,256]{1,0:T(8,128)} %m_ref.1) | copy-start | bytes 24580
  2.8 21.6 %all-to-all-start = ((bf16[16,256,128]{2,1,0:T(8,128)(2,1)}), bf16[16,256,128]{2,1,0:T(8,128)(2,1)S(1)}, u32[]{:S(2)}, u32[]{:S(2)}) async-start(bf16[16,256,128]{2,1,0:T(8,128)(2,1)} %pack_keys_values.1), calls=%async_computation | async-start | bytes 2097152 | tf_op jit(solution)/shard_map/all_to_all | solution.py:487
  24.4 19.9 %all-to-all-start.1 = ((bf16[16,264,128]{2,1,0:T(8,128)(2,1)}), bf16[16,264,128]{2,1,0:T(8,128)(2,1)S(1)}, u32[]{:S(2)}, u32[]{:S(2)}) async-start(bf16[16,264,128]{2,1,0:T(8,128)(2,1)} %pack_queries.1), calls=%async_computation.1 | async-start | bytes 2162688 | tf_op jit(solution)/shard_map/all_to_all | solution.py:487
  30.0 14.3 %collective-permute-start = (bf16[16,256,128]{2,1,0:T(8,128)(2,1)S(1)}, bf16[16,256,128]{2,1,0:T(8,128)(2,1)S(1)}, u32[]{:S(2)}, u32[]{:S(2)}) collective-permute-start(bf16[16,256,128]{2,1,0:T(8,128)(2,1)S(1)} %all-to-all-done.own_ref.kv_ref), channel_id=1, source_target_pairs={{0,1},{1,0},{2,3},{3,2},{4,5},{5,4},{6,7},{7,6},{8,9},{9,8},{10,11... | collective-permute-start | bytes 3145736 | tf_op jit(solution)/shard_map/ppermute | solution.py:495
  31.9 17.4 %collective-permute-start.1 = (bf16[16,256,128]{2,1,0:T(8,128)(2,1)S(1)}, bf16[16,256,128]{2,1,0:T(8,128)(2,1)}, u32[]{:S(2)}, u32[]{:S(2)}) collective-permute-start(bf16[16,256,128]{2,1,0:T(8,128)(2,1)S(1)} %all-to-all-done.own_ref.kv_ref), channel_id=1, source_target_pairs={{1,2},{3,4},{5,6},{7,8},{9,10},{11,12},{13,14},{2,1},{4,3},{6,5},{... | collective-permute-start | bytes 3145736 | tf_op jit(solution)/shard_map/ppermute | solution.py:494
  56.0 20.5 %collective-permute-start.3 = (bf16[4104,128]{1,0:T(8,128)(2,1)S(1)}, bf16[4104,128]{1,0:T(8,128)(2,1)S(1)}, u32[]{:S(2)}, u32[]{:S(2)}) collective-permute-start(bf16[4104,128]{1,0:T(8,128)(2,1)S(1)} %get-tuple-element.22), channel_id=1, source_target_pairs={{1,2},{3,4},{5,6},{7,8},{9,10},{11,12},{13,14},{2,1},{4,3},{6,5},{... | collective-permute-start | bytes 3151880 | tf_op jit(solution)/shard_map/ppermute | solution.py:506
  68.1 4.8 %collective-permute-start.2 = (bf16[16,256,128]{2,1,0:T(8,128)(2,1)S(1)}, bf16[16,256,128]{2,1,0:T(8,128)(2,1)S(1)}, u32[]{:S(2)}, u32[]{:S(2)}) collective-permute-start(bf16[16,256,128]{2,1,0:T(8,128)(2,1)S(1)} %get-tuple-element.21), channel_id=1, source_target_pairs={{0,1},{1,0},{2,3},{3,2},{4,5},{5,4},{6,7},{7,6},{8,9},{9,8},{10,11... | collective-permute-start | bytes 3145736 | tf_op jit(solution)/shard_map/ppermute | solution.py:508
